TPU v7x, 32 devices: a whole 2x2x4 slice. The times are simulated.
32 devices in a mesh: dp: 16 (over z, y, core), tensor: 2 (over x).
Axes of the slice: x: 2, y: 2, z: 4, core: 2. Of those that a mesh axis runs over, the one named last changes fastest.
Arguments:
- residual: bfloat16 [16384, 1536], P(('dp', 'tensor')), may hold values from -6 to 6
- norm_gain: float32 [1536], replicated, may hold values from 0.25 to 1.75
- w_gate_inner: bfloat16 [2, 1536, 3072], P(None, 'dp', 'tensor'), may hold values from -0.15625 to 0.15625
- w_state_io: bfloat16 [1536, 256], P('dp'), may hold values from -0.15625 to 0.15625
- w_step: bfloat16 [1536, 48], P('dp', 'tensor'), may hold values from -0.15625 to 0.15625
- conv_inner: float32 [5, 3072], P(None, 'tensor'), may hold values from -0.5 to 0.5
- conv_state: float32 [5, 256], replicated, may hold values from -0.5 to 0.5
- step_bias: float32 [48], P('tensor'), may hold values from -6 to -2
- decay_log: float32 [48], P('tensor'), may hold values from 0 to 2.5
- skip_gain: float32 [48], P('tensor'), may hold values from 0.5 to 1.5
- gate_gain: float32 [3072], P('tensor'), may hold values from 0.25 to 1.75
- w_output: bfloat16 [3072, 1536], P('tensor', 'dp'), may hold values from -0.109375 to 0.109375
- cotangent: bfloat16 [16384, 1536], P(('dp', 'tensor')), may hold values from -6 to 6
Outputs:
- output: bfloat16 [16384, 1536], P(('dp', 'tensor'))
- grad_residual: float32 [16384, 1536], P(('dp', 'tensor'))
- grad_norm_gain: float32 [1536], P(('dp', 'tensor'))
- grad_gate_inner: float32 [2, 1536, 3072], P(None, 'dp', 'tensor')
- grad_state_io: float32 [1536, 256], P('dp', 'tensor')
- grad_w_step: float32 [1536, 48], P('dp', 'tensor')
- grad_conv_inner: float32 [5, 3072], P(None, 'tensor')
- grad_conv_state: float32 [5, 256], P(None, 'tensor')
- grad_step_bias: float32 [48], P('tensor')
- grad_decay_log: float32 [48], P('tensor')
- grad_skip_gain: float32 [48], P('tensor')
- grad_gate_gain: float32 [3072], P('tensor')
- grad_w_output: float32 [3072, 1536], P('tensor', 'dp')
All inputs are finite; a program needn't handle non-finite values.
Results may differ from a plain program's by a relative error of at most 0.0099.
Values may be sent and summed in bfloat16 or wider, within the bound.
A program may use at most 256 MiB of HBM per device.

v0:
```python
import jax
import jax.numpy as jnp
from jax import lax
from jax.sharding import PartitionSpec as P

Q = 256
LEN = 1024


norm_eps = 1e-05


def silu_slope(pre_act):
    logistic = jax.nn.sigmoid(pre_act)
    return logistic * (1.0 + pre_act * (1.0 - logistic))


def rows_product(left_mat, right_mat):
    return lax.dot_general(
        left_mat, right_mat, (((0,), (0,)), ((), ())), preferred_element_type=jnp.float32
    )


def back_product(left_mat, right_mat):
    return lax.dot_general(
        left_mat, right_mat, (((1,), (1,)), ((), ())), preferred_element_type=jnp.float32
    )


def causal_conv(signal, kernel):
    tap_count = kernel.shape[0] - 1
    length = signal.shape[1]
    padded = jnp.pad(signal, ((0, 0), (tap_count - 1, 0), (0, 0)))
    result = kernel[tap_count] + kernel[0] * padded[:, 0:length]
    for offset in range(1, tap_count):
        result = result + kernel[offset] * padded[:, offset : offset + length]
    return result


def conv_back(signal, kernel, grad_out):
    tap_count = kernel.shape[0] - 1
    length = signal.shape[1]
    padded = jnp.pad(signal, ((0, 0), (tap_count - 1, 0), (0, 0)))
    grad_pad = jnp.pad(grad_out, ((0, 0), (0, tap_count - 1), (0, 0)))
    kernel_rows = []
    grad_in = jnp.zeros(signal.shape, jnp.float32)
    for offset in range(tap_count):
        kernel_rows.append(jnp.sum(grad_out * padded[:, offset : offset + length], axis=(0, 1)))
        shift_at = tap_count - 1 - offset
        grad_in = grad_in + kernel[offset] * grad_pad[:, shift_at : shift_at + length]
    kernel_rows.append(jnp.sum(grad_out, axis=(0, 1)))
    return (jnp.stack(kernel_rows), grad_in)


def span_parts(xs_part, b_part, c_part, step_part, decay_rate):
    seq_count, span_len, expanded_width = xs_part.shape
    head_count = step_part.shape[1]
    xs_heads = xs_part.reshape(seq_count, span_len, head_count, expanded_width // head_count)
    cumulative = jnp.cumsum(step_part * decay_rate[None, :, None], axis=2)
    span_total = cumulative[:, :, -1]
    x_low = xs_heads.astype(jnp.bfloat16)
    b_low = b_part.astype(jnp.bfloat16)
    c_low = c_part.astype(jnp.bfloat16)
    gram_mat = jnp.einsum("sqn,srn->sqr", c_low, b_low, preferred_element_type=jnp.float32)
    causal = lax.broadcasted_iota(jnp.int32, (span_len, span_len), 0) >= lax.broadcasted_iota(
        jnp.int32, (span_len, span_len), 1
    )
    log_gaps = cumulative[:, :, :, None] - cumulative[:, :, None, :]
    decays = jnp.where(causal, jnp.exp(jnp.where(causal, log_gaps, 0.0)), 0.0)
    scaled_gram = gram_mat[:, None] * decays
    mixing = scaled_gram * step_part[:, :, None, :]
    write_rate = jnp.exp(span_total[:, :, None] - cumulative)
    write_weight = write_rate * step_part
    xw_low = (xs_heads * jnp.swapaxes(write_weight, 1, 2)[..., None]).astype(jnp.bfloat16)
    return (
        xs_heads,
        cumulative,
        span_total,
        x_low,
        b_low,
        c_low,
        decays,
        scaled_gram,
        mixing,
        write_rate,
        write_weight,
        xw_low,
    )


def on_device(
    residual,
    norm_gain,
    w_gate_inner,
    w_state_io,
    w_step,
    conv_inner,
    conv_state,
    step_bias,
    decay_log,
    skip_gain,
    gate_gain,
    w_output,
    cotangent,
):
    rows_in = residual.astype(jnp.float32)
    rstd_in = lax.rsqrt(jnp.mean(rows_in * rows_in, axis=1, keepdims=True) + norm_eps)
    scaled = rows_in * rstd_in
    normed_local = (scaled * norm_gain).astype(jnp.bfloat16)
    full_gate_inner, full_state_io, full_step, full_output = (
        lax.all_gather(w_gate_inner, "dp", axis=1, tiled=True),
        lax.all_gather(w_state_io, "dp", axis=0, tiled=True),
        lax.all_gather(w_step, "dp", axis=0, tiled=True),
        lax.all_gather(w_output, "dp", axis=1, tiled=True),
    )
    normed = lax.all_gather(normed_local, "tensor", axis=0, tiled=True)
    gate_proj = jnp.dot(normed, full_gate_inner[0], preferred_element_type=jnp.float32)
    inner_proj = jnp.dot(normed, full_gate_inner[1], preferred_element_type=jnp.float32)
    state_proj = jnp.dot(normed, full_state_io, preferred_element_type=jnp.float32)
    step_raw = jnp.dot(normed, full_step, preferred_element_type=jnp.float32)
    step_pre = step_raw + step_bias
    step_size = jax.nn.softplus(step_pre)
    decay_rate = -jnp.exp(decay_log)
    every_row_count = normed.shape[0]
    seq_count = every_row_count // LEN
    span_count = LEN // Q
    expanded_width = gate_proj.shape[1]
    head_count = step_raw.shape[1]
    head_width = expanded_width // head_count
    state_width = state_proj.shape[1] // 2
    conv_in = jnp.concatenate([inner_proj, state_proj], axis=1).reshape(
        seq_count, LEN, expanded_width + 2 * state_width
    )
    kernel = jnp.concatenate([conv_inner, conv_state], axis=1)
    conv_out = causal_conv(conv_in, kernel)
    active = jax.nn.silu(conv_out)

    def spanned(source_buffer):
        return jnp.swapaxes(
            source_buffer.reshape(seq_count, span_count, Q, source_buffer.shape[-1]), 0, 1
        )

    def whole_sequence(source_buffer):
        return jnp.swapaxes(source_buffer, 0, 1).reshape(seq_count, LEN, source_buffer.shape[-1])

    xs_spans = spanned(active[:, :, :expanded_width])
    b_spans = spanned(active[:, :, expanded_width : expanded_width + state_width])
    c_spans = spanned(active[:, :, expanded_width + state_width :])
    step_spans = jnp.transpose(
        step_size.reshape(seq_count, span_count, Q, head_count), (1, 0, 3, 2)
    )

    def forward_step(state_in, inputs):
        xs_part, b_part, c_part, step_part = inputs
        span_vals = span_parts(xs_part, b_part, c_part, step_part, decay_rate)
        xs_heads, cumulative, span_total, x_low, b_low, c_low = span_vals[:6]
        mixing = span_vals[8]
        xw_low = span_vals[11]
        mix_low = mixing.astype(jnp.bfloat16)
        intra_out = jnp.einsum(
            "shtr,srhp->sthp", mix_low, x_low, preferred_element_type=jnp.float32
        )
        span_state = jnp.einsum("sqhp,sqn->shpn", xw_low, b_low, preferred_element_type=jnp.float32)
        state_low = state_in.astype(jnp.bfloat16)
        readout = jnp.einsum("sqn,shpn->sqhp", c_low, state_low, preferred_element_type=jnp.float32)
        growth = jnp.swapaxes(jnp.exp(cumulative), 1, 2)[..., None]
        ssd_out = intra_out + growth * readout + skip_gain[None, None, :, None] * xs_heads
        state_next = jnp.exp(span_total)[:, :, None, None] * state_in + span_state
        return (state_next, (ssd_out.reshape(xs_part.shape), state_in))

    start_state = jnp.zeros((seq_count, head_count, head_width, state_width), jnp.float32)
    final_state, (duality_span_output, entering) = lax.scan(
        forward_step, start_state, (xs_spans, b_spans, c_spans, step_spans)
    )
    duality_full_output = whole_sequence(duality_span_output).reshape(
        every_row_count, expanded_width
    )
    gate_act = jax.nn.silu(gate_proj)
    gated_out = duality_full_output * gate_act
    unit_total = expanded_width * lax.axis_size("tensor")
    squares = lax.psum(jnp.sum(gated_out * gated_out, axis=1), "tensor")
    gate_rstd = lax.rsqrt(squares / unit_total + norm_eps)[:, None]
    normed_gate = (gated_out * gate_rstd * gate_gain).astype(jnp.bfloat16)
    mixed = lax.psum_scatter(
        jnp.dot(normed_gate, full_output, preferred_element_type=jnp.float32),
        "tensor",
        scatter_dimension=0,
        tiled=True,
    )
    output = (rows_in + mixed).astype(jnp.bfloat16)
    full_gate_inner, full_state_io, full_step, full_output = (
        lax.all_gather(w_gate_inner, "dp", axis=1, tiled=True),
        lax.all_gather(w_state_io, "dp", axis=0, tiled=True),
        lax.all_gather(w_step, "dp", axis=0, tiled=True),
        lax.all_gather(w_output, "dp", axis=1, tiled=True),
    )
    piece = lax.all_gather(cotangent, "tensor", axis=0, tiled=True)
    grad_wout = rows_product(normed_gate, piece)
    grad_gate_out = back_product(piece, full_output)
    grad_wout, grad_gate_out = (grad_wout, grad_gate_out)
    grad_gate_gain = jnp.sum(grad_gate_out * gated_out * gate_rstd, axis=0)
    weighted = grad_gate_out * gate_gain
    gate_inner = lax.psum(jnp.sum(weighted * gated_out, axis=1), "tensor")
    grad_gated = (
        gate_rstd * weighted - gated_out * gate_rstd**3 * (gate_inner / unit_total)[:, None]
    )
    dy_low = (grad_gated * gate_act).astype(jnp.bfloat16)
    dgate_low = (grad_gated * duality_full_output * silu_slope(gate_proj)).astype(jnp.bfloat16)

    def backward_step(state_grad, inputs):
        xs_part, b_part, c_part, step_part, state_in, dy_part = inputs
        (
            xs_heads,
            cumulative,
            span_total,
            x_low,
            b_low,
            c_low,
            decays,
            scaled_gram,
            mixing,
            write_rate,
            write_weight,
            xw_low,
        ) = span_parts(xs_part, b_part, c_part, step_part, decay_rate)
        mix_low = mixing.astype(jnp.bfloat16)
        dy_heads = dy_part.reshape(xs_heads.shape)
        grad_skip = jnp.sum(dy_heads * xs_heads, axis=(0, 1, 3))
        grad_mix = jnp.einsum(
            "sthp,srhp->shtr", dy_heads, x_low, preferred_element_type=jnp.float32
        )
        grad_size = jnp.sum(grad_mix * scaled_gram, axis=2)
        edge_terms = grad_mix * mixing
        grad_cum = jnp.sum(edge_terms, axis=3) - jnp.sum(edge_terms, axis=2)
        gram_grad = jnp.sum(grad_mix * decays * step_part[:, :, None, :], axis=1).astype(
            jnp.bfloat16
        )
        grad_xs = skip_gain[None, None, :, None] * dy_heads + jnp.einsum(
            "shtr,sthp->srhp", mix_low, dy_heads, preferred_element_type=jnp.float32
        )
        growth = jnp.exp(cumulative)
        state_low = state_in.astype(jnp.bfloat16)
        readout = jnp.einsum("sqn,shpn->sqhp", c_low, state_low, preferred_element_type=jnp.float32)
        grad_cum = grad_cum + jnp.swapaxes(jnp.sum(dy_heads * readout, axis=3), 1, 2) * growth
        read_low = (dy_heads * jnp.swapaxes(growth, 1, 2)[..., None]).astype(jnp.bfloat16)
        grad_c = jnp.einsum(
            "sqhp,shpn->sqn", read_low, state_low, preferred_element_type=jnp.float32
        ) + jnp.einsum("sqr,srn->sqn", gram_grad, b_low, preferred_element_type=jnp.float32)
        grad_state_low = jnp.einsum(
            "sqhp,sqn->shpn", read_low, c_low, preferred_element_type=jnp.float32
        )
        fade_rate = jnp.exp(span_total)
        grad_total = jnp.sum(state_grad * state_in, axis=(2, 3)) * fade_rate
        carry_low = state_grad.astype(jnp.bfloat16)
        grad_xw = jnp.einsum("sqn,shpn->sqhp", b_low, carry_low, preferred_element_type=jnp.float32)
        grad_b = jnp.einsum(
            "sqhp,shpn->sqn", xw_low, carry_low, preferred_element_type=jnp.float32
        ) + jnp.einsum("sqr,sqn->srn", gram_grad, c_low, preferred_element_type=jnp.float32)
        grad_xs = grad_xs + grad_xw * jnp.swapaxes(write_weight, 1, 2)[..., None]
        weight_grad = jnp.swapaxes(jnp.sum(grad_xw * xs_heads, axis=3), 1, 2)
        grad_total = grad_total + jnp.sum(weight_grad * write_weight, axis=2)
        grad_cum = grad_cum - weight_grad * write_weight
        grad_size = grad_size + weight_grad * write_rate
        grad_cum = grad_cum.at[:, :, -1].add(grad_total)
        grad_rate = lax.cumsum(grad_cum, axis=2, reverse=True)
        grad_size = grad_size + grad_rate * decay_rate[None, :, None]
        grad_decay = jnp.sum(grad_rate * step_part, axis=(0, 2))
        state_prev = grad_state_low + fade_rate[:, :, None, None] * state_grad
        return (
            state_prev,
            (grad_xs.reshape(xs_part.shape), grad_b, grad_c, grad_size, grad_decay, grad_skip),
        )

    dy_spans = spanned(dy_low.reshape(seq_count, LEN, expanded_width))
    first_grad, (
        grad_head_input_spans,
        grad_input_b_spans,
        grad_readout_c_spans,
        gsize_spans,
        gdecay_spans,
        gskip_spans,
    ) = lax.scan(
        backward_step,
        jnp.zeros_like(start_state),
        (xs_spans, b_spans, c_spans, step_spans, entering, dy_spans),
        reverse=True,
    )
    grad_skip_gain = jnp.sum(gskip_spans, axis=0)
    grad_decay_log = jnp.sum(gdecay_spans, axis=0) * decay_rate
    grad_size_all = jnp.transpose(gsize_spans, (1, 0, 3, 2)).reshape(every_row_count, head_count)
    grad_pre = grad_size_all * jax.nn.sigmoid(step_pre)
    grad_step_bias = jnp.sum(grad_pre, axis=0)
    ddt_low = grad_pre.astype(jnp.bfloat16)
    grad_active = jnp.concatenate(
        [
            whole_sequence(grad_head_input_spans),
            whole_sequence(grad_input_b_spans),
            whole_sequence(grad_readout_c_spans),
        ],
        axis=2,
    )
    grad_conv_out = grad_active * silu_slope(conv_out)
    grad_kernel, grad_conv_in = conv_back(conv_in, kernel, grad_conv_out)
    grad_conv_in = grad_conv_in.reshape(every_row_count, expanded_width + 2 * state_width)
    dinner_low = grad_conv_in[:, :expanded_width].astype(jnp.bfloat16)
    dstate_low = grad_conv_in[:, expanded_width:].astype(jnp.bfloat16)
    grad_zx = jnp.stack([rows_product(normed, dgate_low), rows_product(normed, dinner_low)])
    grad_bcw = rows_product(normed, dstate_low)
    grad_stepw = rows_product(normed, ddt_low)
    grad_normed = lax.psum_scatter(
        back_product(dgate_low, full_gate_inner[0])
        + back_product(dinner_low, full_gate_inner[1])
        + back_product(dstate_low, full_state_io)
        + back_product(ddt_low, full_step),
        "tensor",
        scatter_dimension=0,
        tiled=True,
    )
    grad_norm_gain = jnp.sum(grad_normed * scaled, axis=0)
    grad_v = grad_normed * norm_gain
    grad_residual = cotangent.astype(jnp.float32) + rstd_in * (
        grad_v - scaled * jnp.mean(grad_v * scaled, axis=1, keepdims=True)
    )
    zx_shard, bcw_shard, stepw_shard, wout_shard, gain_shard = (
        lax.psum_scatter(grad_zx, "dp", scatter_dimension=1, tiled=True),
        lax.psum_scatter(grad_bcw, "dp", scatter_dimension=0, tiled=True),
        lax.psum_scatter(grad_stepw, "dp", scatter_dimension=0, tiled=True),
        lax.psum_scatter(grad_wout, "dp", scatter_dimension=1, tiled=True),
        lax.psum_scatter(grad_norm_gain, "dp", scatter_dimension=0, tiled=True),
    )
    conv_inner_sum, conv_state_sum, bias_sum, decay_sum, skip_sum, gate_gain_sum = lax.psum(
        (
            grad_kernel[:, :expanded_width],
            grad_kernel[:, expanded_width:],
            grad_step_bias,
            grad_decay_log,
            grad_skip_gain,
            grad_gate_gain,
        ),
        "dp",
    )
    bcw_part, conv_state_part, gain_part = (
        lax.psum_scatter(bcw_shard, "tensor", scatter_dimension=1, tiled=True),
        lax.psum_scatter(conv_state_sum, "tensor", scatter_dimension=1, tiled=True),
        lax.psum_scatter(gain_shard, "tensor", scatter_dimension=0, tiled=True),
    )
    return (
        output,
        grad_residual,
        gain_part,
        zx_shard,
        bcw_part,
        stepw_shard,
        conv_inner_sum,
        conv_state_part,
        bias_sum,
        decay_sum,
        skip_sum,
        gate_gain_sum,
        wout_shard,
    )


def solution(mesh):
    return jax.shard_map(
        on_device,
        mesh=mesh,
        in_specs=(
            P(("dp", "tensor"), None),
            P(),
            P(None, "dp", "tensor"),
            P("dp", None),
            P("dp", "tensor"),
            P(None, "tensor"),
            P(),
            P("tensor"),
            P("tensor"),
            P("tensor"),
            P("tensor"),
            P("tensor", "dp"),
            P(("dp", "tensor"), None),
        ),
        out_specs=(
            P(("dp", "tensor"), None),
            P(("dp", "tensor"), None),
            P(("dp", "tensor")),
            P(None, "dp", "tensor"),
            P("dp", "tensor"),
            P("dp", "tensor"),
            P(None, "tensor"),
            P(None, "tensor"),
            P("tensor"),
            P("tensor"),
            P("tensor"),
            P("tensor"),
            P("tensor", "dp"),
        ),
        check_vma=False,
    )
```

profile of v0, /device:TPU:0, one launch (start us, length us, event | category | flops | bytes accessed | tf_op | source)
XLA Modules:
  0.0 1213.9 jit_solution(8501519928231591435)
XLA Ops:
  14.3 25.5 %all_gather.25 = bf16[1536,256]{1,0:T(8,128)(2,1)S(1)} all-gather(bf16[96,256]{1,0:T(8,128)(2,1)S(1)} %copy-done.36), channel_id=1, replica_groups=mesh['dp'=16,'tensor'=2] {'dp'}, dimensions={0}, use_global_device_ids=true | all-gather | bytes 835584 | tf_op jit(solution)/shard_map/all_gather | solution.py:112
  39.9 17.7 %all-gather = bf16[16,96,24]{1,2,0:T(8,128)(2,1)S(1)} all-gather(bf16[1,96,24]{1,2,0:T(8,128)(2,1)S(1)} %bitcast.524), channel_id=1, replica_groups=mesh['dp'=16,'tensor'=2] {'dp'}, dimensions={0}, use_global_device_ids=true | all-gather | bytes 78336 | tf_op jit(solution)/shard_map/all_gather | solution.py:113
  67.0 76.2 %all-gather.8.cloned.1.call-done = bf16[2,1536,1536]{2,1,0:T(8,128)(2,1)} async-done(((bf16[2,96,1536]{2,1,0:T(8,128)(2,1)}), bf16[2,1536,1536]{2,1,0:T(8,128)(2,1)}) %all-gather.8.cloned.1.call-update) | async-done | bytes 9437200 | tf_op jit(solution)/shard_map/all_gather | solution.py:111
  143.1 8.0 fusion.90
  156.1 16.6 %fusion.81 = (f32[1,1024,1792]{2,1,0:T(8,128)}, f32[1,1024,1792]{2,1,0:T(8,128)}) fusion(f32[1,1024,256]{2,1,0:T(8,128)S(1)} %bitcast.506, f32[1,1024,1536]{2,1,0:T(8,128)} %bitcast.495, f32[1792]{0:T(1024)S(1)} %get-tuple-element.688, f32[1792]{0:T(1024)S(1)} %get-tuple-element.689, f32[1792]{0:T(1024)S(1)} %get-tuple-element.690, ...), kind=kLoop, calls=%fused_computation.151 | loop fusion | flops 23855104 | bytes 29395968 | tf_op jit(solution)/shard_map/jit(silu)/mul | solution.py:136
  174.8 5.8 slice.196
  180.6 6.6 copy.203
  190.7 73.6 %while.43 = (s32[]{:T(128)}, f32[1,24,64,128]{3,2,1,0:T(8,128)S(1)}, f32[4,1,256,1536]{3,2,0,1:T(8,128)}, f32[4,1,24,64,128]{4,3,2,1,0:T(8,128)}, f32[4,1,24,256...) while((s32[]{:T(128)}, ...), condition=%wide.region_4.5_spmd.clone, body=%wide.region_1.4_spmd.clone.sunk | while | flops 433479744 | bytes 35600088 | solution.py:172
  197.4 4.1 fusion.204
  215.8 4.1 fusion.204
  234.2 4.1 fusion.204
  252.7 4.1 fusion.204
  264.4 12.4 %multiply_reduce_fusion.11 = (f32[1024]{0:T(1024)S(1)}, f32[1024,1536]{1,0:T(8,128)}, f32[1024,1536]{1,0:T(8,128)}) fusion(f32[4,1,256,1536]{3,2,0,1:T(8,128)} %get-tuple-element.397, bf16[1024,1536]{1,0:T(8,128)(2,1)} %all-gather.6.cloned.1.call-done, bf16[2,1536,1536]{2,1,0:T(8,128)(2,1)} %all-gather.8.cloned.1.call-done), kind=kOutput, calls=%fused_computation.162 | convolution fusion | flops 4842847232 | bytes 26742784 | tf_op jit(solution)/shard_map/dot_general | solution.py:117
  276.8 4.9 psum.56
  281.7 11.9 multiply_reduce_fusion.9
  293.7 4.9 psum.57
  298.6 13.2 %fusion.83 = (bf16[1024,1536]{1,0:T(8,128)(2,1)}, bf16[1024,1536]{1,0:T(8,128)(2,1)}) fusion(f32[4,1,256,1536]{3,2,0,1:T(8,128)} %get-tuple-element.397, f32[1024,1536]{1,0:T(8,128)} %get-tuple-element.786, f32[1024]{0:T(1024)S(1)} %broadcast_multiply_fusion.2, f32[1024,1536]{1,0:T(8,128)} %get-tuple-element.763, f32[1024,1536]{1,0:T(8,128)} %get-tuple-element.787, ...), kind=kLoop, calls=%fused_computation.155 | loop fusion | flops 28311552 | bytes 31475712 | tf_op jit(solution)/shard_map/convert_element_type | solution.py:208
  318.7 246.5 %while.44 = (s32[]{:T(128)}, f32[1,24,64,128]{3,2,1,0:T(8,128)S(1)}, f32[4,1,256,1536]{3,2,0,1:T(8,128)}, f32[4,1,256,128]{3,2,1,0:T(8,128)}, f32[4,1,256,128]{3...) while((s32[]{:T(128)}, ...), condition=%wide.region_26.27_spmd.clone, body=%wide.region_10.26_spmd.clone.sunk | while | flops 996548800 | bytes 53172596 | solution.py:282
  328.4 5.7 fusion.226
  348.8 3.8 reduce-window.70
  363.6 4.9 fusion.228
  390.1 5.7 fusion.226
  425.3 4.9 fusion.228
  451.7 5.7 fusion.226
  486.9 4.9 fusion.228
  513.3 5.7 fusion.226
  548.5 4.9 fusion.228
  565.2 17.8 %fusion.114 = (f32[1792]{0:T(1024)S(1)}, f32[1792]{0:T(1024)S(1)}, f32[1792]{0:T(1024)S(1)}, f32[1792]{0:T(1024)S(1)}, f32[1792]{0:T(1024)S(1)}, /*index=5*/f32[1,1024,1792]{2,1,0:T(8,128)S(1)}) fusion(f32[1024,256]{1,0:T(8,128)} %copy-done.12, f32[1024,1536]{1,0:T(8,128)} %copy-done.2, f32[1,1024,1792]{2,1,0:T(8,128)} %maximum_bitcast_fusion, ...), kind=kLoop, calls=%fused_computation.216 | loop fusion | flops 36691200 | bytes 36736000 | tf_op jit(solution)/shard_map/reduce_sum | solution.py:51
  590.9 3.8 fusion.108
  594.7 4.8 fusion.106
  599.5 8.2 fusion.89
  607.7 7.1 fusion.91
  619.5 10.6 fusion.113
  630.2 19.2 %reduce-scatter.17.cloned.1.call-done = f32[96,256]{1,0:T(8,128)} async-done(((f32[1536,256]{1,0:T(8,128)}), f32[96,256]{1,0:T(8,128)}) %reduce-scatter.17.cloned.1.call-update) | async-done | bytes 98320 | tf_op jit(solution)/shard_map/reduce_scatter | solution.py:326
  649.5 11.2 fusion.112
  661.0 8.2 convolution_bitcast_fusion.4
  669.2 5.1 convolution_bitcast_fusion.5
  674.3 6.9 pad_maximum_fusion
  684.4 24.8 %reduce-scatter.25.cloned.1.call-done = f32[96,24]{1,0:T(8,128)} async-done(((f32[1536,24]{1,0:T(8,128)}), f32[96,24]{1,0:T(8,128)}) %reduce-scatter.25.cloned.1.call-update) | async-done | bytes 9232
  710.6 77.1 %reduce-scatter.13.cloned.1.call-done = f32[512,1536]{1,0:T(8,128)} async-done(((f32[1024,1536]{1,0:T(8,128)}), f32[512,1536]{1,0:T(8,128)}) %reduce-scatter.13.cloned.1.call-update) | async-done | bytes 3145744 | tf_op jit(solution)/shard_map/reduce_scatter | solution.py:310
  790.5 10.0 reduce-scatter.23.cloned.1.call-done
  800.4 62.5 %all-reduce.4 = (f32[1536]{0:T(1024)S(1)}, f32[5,1536]{1,0:T(8,128)}, f32[5,128]{1,0:T(8,128)}, f32[24]{0:T(128)}, f32[24]{0:T(128)}, /*index=5*/f32[24]{0:T(128)}, f32[1536]{0:T(1024)}) all-reduce(f32[1536]{0:T(1024)S(1)} %get-tuple-element.685, f32[5,1536]{1,0:T(8,128)S(1)} %slice.202, ...), channel_id=4, replica_groups=mesh['dp'=16,'tensor'=2] {'dp'}, use_global_device_ids=true, to_apply=%region_30.31.clone | all-reduce | flops 11464 | bytes 91712
  863.0 5.1 all-reduce.3
  868.8 11.2 reduce-scatter.11.cloned.1.call-done
  880.0 6.6 fusion.98
  886.6 6.1 reduce-scatter.19.cloned.1.call-done
  892.8 115.9 %reduce-scatter.21.cloned.1.call-done = f32[1536,96]{0,1:T(8,128)} async-done(((f32[1536,1536]{0,1:T(8,128)}), f32[1536,96]{0,1:T(8,128)}) %reduce-scatter.21.cloned.1.call-update) | async-done | bytes 589840 | tf_op jit(solution)/shard_map/reduce_scatter | solution.py:328
  1008.7 198.1 %reduce-scatter.15.cloned.1.call-done = f32[2,96,1536]{2,1,0:T(8,128)} async-done(((f32[2,1536,1536]{2,1,0:T(8,128)}), f32[2,96,1536]{2,1,0:T(8,128)}) %reduce-scatter.15.cloned.1.call-update) | async-done | bytes 1179664 | tf_op jit(solution)/shard_map/reduce_scatter | solution.py:325
  (631 shorter events, 309.3 us)
Async XLA Ops:
  7.2 32.6 %copy-start.37 = (f32[5,1536]{1,0:T(8,128)S(1)}, f32[5,1536]{1,0:T(8,128)}, u32[]{:S(2)}) copy-start(f32[5,1536]{1,0:T(8,128)} %param.24) | copy-start | bytes 92164
  7.2 32.6 %copy-start.45 = (f32[5,256]{1,0:T(8,128)S(1)}, f32[5,256]{1,0:T(8,128)}, u32[]{:S(2)}) copy-start(f32[5,256]{1,0:T(8,128)} %param.25) | copy-start | bytes 15364
  7.2 32.7 %copy-start.48 = (bf16[96,24]{0,1:T(8,128)(2,1)S(1)}, bf16[96,24]{0,1:T(8,128)(2,1)}, u32[]{:S(2)}) copy-start(bf16[96,24]{0,1:T(8,128)(2,1)} %param.23) | copy-start | bytes 13828
  7.2 50.6 %copy-start.50 = (f32[24]{0:T(128)S(1)}, f32[24]{0:T(128)}, u32[]{:S(2)}) copy-start(f32[24]{0:T(128)} %param.27) | copy-start | bytes 292
  7.2 52.7 %copy-start.49 = (f32[24]{0:T(128)S(1)}, f32[24]{0:T(128)}, u32[]{:S(2)}) copy-start(f32[24]{0:T(128)} %param.26) | copy-start | bytes 292
  7.2 52.6 %all-gather.6.cloned.1.call-start = ((), (), s32[]{:S(2)}) async-start(), calls=%async_computation.8 | async-start | bytes 4718592 | tf_op jit(solution)/shard_map/all_gather | solution.py:116
  12.1 131.0 %all-gather.8.cloned.1.call-start = ((), (), s32[]{:S(2)}) async-start(), calls=%async_computation.9 | async-start | bytes 10027008 | tf_op jit(solution)/shard_map/all_gather | solution.py:111
  12.9 268.8 %all-gather.12.cloned.1.call-start = ((), (), s32[]{:S(2)}) async-start(), calls=%async_computation.12 | async-start | bytes 4718592 | tf_op jit(solution)/shard_map/all_gather | solution.py:197
  13.6 268.1 %all-gather.10.cloned.1.call-start = ((), (), s32[]{:S(2)}) async-start(), calls=%async_computation.10 | async-start | bytes 5013504 | tf_op jit(solution)/shard_map/all_gather | solution.py:114
  14.2 635.2 %reduce-scatter.17.cloned.1.call-start = ((), (), s32[]{:S(2)}) async-start(), calls=%async_computation.15 | async-start | bytes 1671168 | tf_op jit(solution)/shard_map/reduce_scatter | solution.py:326
  39.7 27.2 %copy-start.16 = (bf16[1536,256]{1,0:T(8,128)(2,1)}, bf16[1536,256]{1,0:T(8,128)(2,1)S(1)}, u32[]{:S(2)}) copy-start(bf16[1536,256]{1,0:T(8,128)(2,1)S(1)} %all_gather.25) | copy-start | bytes 2359300
  39.9 116.2 %copy-start.28 = (f32[1792]{0:T(1024)}, f32[1792]{0:T(1024)S(1)}, u32[]{:S(2)}) copy-start(f32[1792]{0:T(1024)S(1)} %get-tuple-element.688) | copy-start | bytes 21508
  39.9 116.2 %copy-start.30 = (f32[1792]{0:T(1024)}, f32[1792]{0:T(1024)S(1)}, u32[]{:S(2)}) copy-start(f32[1792]{0:T(1024)S(1)} %get-tuple-element.689) | copy-start | bytes 21508
  39.9 116.2 %copy-start.32 = (f32[1792]{0:T(1024)}, f32[1792]{0:T(1024)S(1)}, u32[]{:S(2)}) copy-start(f32[1792]{0:T(1024)S(1)} %get-tuple-element.690) | copy-start | bytes 21508
  39.9 116.2 %copy-start.34 = (f32[1792]{0:T(1024)}, f32[1792]{0:T(1024)S(1)}, u32[]{:S(2)}) copy-start(f32[1792]{0:T(1024)S(1)} %get-tuple-element.691) | copy-start | bytes 21508
  66.9 89.2 %copy-start.12 = (f32[1024,256]{1,0:T(8,128)}, f32[1024,256]{1,0:T(8,128)S(1)}, u32[]{:S(2)}) copy-start(f32[1024,256]{1,0:T(8,128)S(1)} %fusion.119) | copy-start | bytes 3145732
  264.4 17.4 %copy-start.46 = (f32[1536]{0:T(1024)S(1)}, f32[1536]{0:T(1024)}, u32[]{:S(2)}) copy-start(f32[1536]{0:T(1024)} %param.29) | copy-start | bytes 18436
  281.7 16.9 %copy-start.40 = (f32[1024]{0:T(1024)}, f32[1024]{0:T(1024)S(1)}, u32[]{:S(2)}) copy-start(f32[1024]{0:T(1024)S(1)} %get-tuple-element.783) | copy-start | bytes 12292
  326.5 7.6 copy-start.26
  327.4 8.2 copy-start.5
  327.4 11.1 copy-start.7
  388.1 7.6 copy-start.26
  389.0 8.2 copy-start.5
  389.0 11.1 copy-start.7
  450.6 8.2 copy-start.5
  450.6 11.1 copy-start.7
  511.4 7.6 copy-start.26
  512.3 8.2 copy-start.5
  512.3 11.1 copy-start.7
  565.2 17.9 %copy-start.29 = (f32[1792]{0:T(1024)S(1)}, f32[1792]{0:T(1024)}, u32[]{:S(2)}) copy-start(f32[1792]{0:T(1024)} %copy-done.28) | copy-start | bytes 21508
  565.2 17.9 %copy-start.31 = (f32[1792]{0:T(1024)S(1)}, f32[1792]{0:T(1024)}, u32[]{:S(2)}) copy-start(f32[1792]{0:T(1024)} %copy-done.30) | copy-start | bytes 21508
  565.2 17.9 %copy-start.33 = (f32[1792]{0:T(1024)S(1)}, f32[1792]{0:T(1024)}, u32[]{:S(2)}) copy-start(f32[1792]{0:T(1024)} %copy-done.32) | copy-start | bytes 21508
  565.2 17.9 %copy-start.35 = (f32[1792]{0:T(1024)S(1)}, f32[1792]{0:T(1024)}, u32[]{:S(2)}) copy-start(f32[1792]{0:T(1024)} %copy-done.34) | copy-start | bytes 21508
  590.5 118.7 %reduce-scatter.25.cloned.1.call-start = ((), (), s32[]{:S(2)}) async-start(), calls=%async_computation.19 | async-start | bytes 835584
  599.5 188.2 %reduce-scatter.13.cloned.1.call-start = ((), (), s32[]{:S(2)}) async-start(), calls=%async_computation.13 | async-start | bytes 9437184 | tf_op jit(solution)/shard_map/reduce_scatter | solution.py:310
  599.5 8.2 copy-start.18
  599.5 15.3 %slice-start = ((s8[6291456]{0:T(1024)(128)(4,1)}), s8[4194304]{0:T(1024)(128)(4,1)S(1)}, s32[]{:S(2)}) async-start(s8[6291456]{0:T(1024)(128)(4,1)} %bitcast.496), calls=%async_computation.20 | async-start | bytes 8388608
  618.6 181.8 %reduce-scatter.23.cloned.1.call-start = ((), (), s32[]{:S(2)}) async-start(), calls=%async_computation.18 | async-start | bytes 12288 | tf_op jit(solution)/shard_map/reduce_scatter | solution.py:344
  619.4 260.6 %reduce-scatter.11.cloned.1.call-start = ((), (), s32[]{:S(2)}) async-start(), calls=%async_computation.11 | async-start | bytes 9437184 | tf_op jit(solution)/shard_map/reduce_scatter | solution.py:184
  630.1 262.6 %reduce-scatter.19.cloned.1.call-start = ((), (), s32[]{:S(2)}) async-start(), calls=%async_computation.16 | async-start | bytes 147456 | tf_op jit(solution)/shard_map/reduce_scatter | solution.py:343
  649.4 359.3 %reduce-scatter.21.cloned.1.call-start = ((), (), s32[]{:S(2)}) async-start(), calls=%async_computation.17 | async-start | bytes 10027008 | tf_op jit(solution)/shard_map/reduce_scatter | solution.py:328
  660.7 546.2 %reduce-scatter.15.cloned.1.call-start = ((), (), s32[]{:S(2)}) async-start(), calls=%async_computation.14 | async-start | bytes 20054016 | tf_op jit(solution)/shard_map/reduce_scatter | solution.py:325
  660.9 8.2 copy-start.4
  661.0 8.2 copy-start.19
  681.2 106.5 %copy-start.9 = (bf16[512,1536]{1,0:T(8,128)(2,1)S(1)}, bf16[512,1536]{1,0:T(8,128)(2,1)}, u32[]{:S(2)}) copy-start(bf16[512,1536]{1,0:T(8,128)(2,1)} %param.19) | copy-start | bytes 4718596
  681.2 106.5 %copy-start.27 = (f32[1536]{0:T(1024)S(1)}, f32[1536]{0:T(1024)}, u32[]{:S(2)}) copy-start(f32[1536]{0:T(1024)} %param.20) | copy-start | bytes 18436
  681.2 106.5 %copy-start.39 = (f32[512]{0:T(512)S(1)}, f32[512]{0:T(512)}, u32[]{:S(2)}) copy-start(f32[512]{0:T(512)} %copy-done.38) | copy-start | bytes 6148
  681.2 119.2 %copy-start.42 = (f32[1536]{0:T(1024)S(1)}, f32[1536]{0:T(1024)}, u32[]{:S(2)}) copy-start(f32[1536]{0:T(1024)} %get-tuple-element.678) | copy-start | bytes 18436
  (59 other events, 284.8 us)
Sparse Core Ops, SparseCore 0:
  12.2 47.6 all-gather.5
  62.2 80.9 all-gather.7
  144.7 43.2 all-gather.11
  190.2 53.1 all-gather.9
  590.6 58.7 reduce-scatter.16
  653.4 55.7 reduce-scatter.24
  711.5 76.1 reduce-scatter.12
  790.4 9.9 reduce-scatter.22
  802.7 77.2 reduce-scatter.10
  882.6 10.1 reduce-scatter.18
  897.5 111.2 reduce-scatter.20
  1013.2 193.5 reduce-scatter.14
where the time goes:
time: 1220 us; the launch traced here: 1210 us
  waiting for transfers between devices  543 us (45%)
  matrix products  208 us (17%)
  local copies, waits for them, and re-layouts  166 us (14%)
  other arithmetic  158 us (13%)
  blocking collectives  121 us (10%)
  between operations  16.4 us (1%)
    reduce_scatter x1, waiting for transfers between devices, on_device(): lax.psum_scatter(grad_zx, 'dp', scatter_dimension=1, tiled=True)  198 us
    reduce_scatter x1, waiting for transfers between devices, on_device(): lax.psum_scatter(grad_wout, 'dp', scatter_dimension=1, tiled=True)  116 us
    reduce_scatter x1, waiting for transfers between devices, on_device(): lax.psum_scatter(back_product(dgate_low, full_gate_inner[0]) + back_produ...  77.1 us
    all_gather x1, waiting for transfers between devices, on_device(): lax.all_gather(w_gate_inner, 'dp', axis=1, tiled=True)  76.2 us
    unnamed x2, blocking collectives  67.7 us
    dynamic_update_slice x16, local copies, waits for them, and re-layouts, on_device(): lax.scan(forward_step, start_state, (xs_spans, b_spans, c_spans, step_spa...  36 us
    another operation x78, local copies, waits for them, and re-layouts  35.8 us
    dot_general x5, matrix products, back_product(): lax.dot_general(left_mat, right_mat, (((1,), (1,)), ((), ())), preferred_...  35.7 us
  transfers between devices with their start and end apart: 12, of which 10 were waited for; matrix products, arithmetic and copies ran while one was open for 18% of the time, Pallas kernels for 0%

commit v1 on v0

v1 whole, which is shorter than its diff:
```python
import functools

import jax
import jax.numpy as jnp
from jax import lax
from jax.experimental import pallas as pl
from jax.experimental.pallas import tpu as pltpu
from jax.sharding import PartitionSpec as P

Q = 256
LEN = 1024
HEAD = 64
BW = 256
HB = BW // HEAD
LOG2E = 1.4426950408889634
FAR = -1e30
norm_eps = 1e-05
f32 = jnp.float32
bf16 = jnp.bfloat16


def mm(a, b, ca=1, cb=0):
    return lax.dot_general(a, b, (((ca,), (cb,)), ((), ())), preferred_element_type=f32)


def sigmoid(v):
    return 1.0 / (1.0 + jnp.exp(-v))


def split3(a):
    hi = a.astype(bf16)
    rest = a - hi.astype(f32)
    mid = rest.astype(bf16)
    low = (rest - mid.astype(f32)).astype(bf16)
    return hi, mid, low


def split2(a):
    hi = a.astype(bf16)
    return hi, (a - hi.astype(f32)).astype(bf16)


def iota(shape, axis):
    return lax.broadcasted_iota(jnp.int32, shape, axis)


def expand(cols):
    rows = cols.shape[0]
    left = iota((rows, 128), 1) < HEAD
    return jnp.concatenate(
        [jnp.where(left, cols[:, 2 * q : 2 * q + 1], cols[:, 2 * q + 1 : 2 * q + 2]) for q in range(2)],
        axis=1,
    )


def conv_taps(window, kernel):
    out = kernel[4:5] + kernel[3:4] * window[8:]
    for k in range(3):
        out = out + kernel[k : k + 1] * pltpu.roll(window, 3 - k, 0)[8:]
    return out


def head_masks():
    lane = iota((1, BW), 1) // HEAD
    return [(lane == j).astype(f32).astype(bf16) for j in range(HB)]


def quads():
    for r in range(0, Q, 64):
        for half in range(2):
            if half * 128 <= r:
                yield r, half, r < half * 128 + 128


def decay_chunk(col, row, r, half, diag):
    gap = col[r : r + 64] - row[:, half * 128 : half * 128 + 128]
    if diag:
        keep = iota((64, 128), 0) + (r - half * 128) >= iota((64, 128), 1)
        gap = jnp.where(keep, gap, FAR)
    return jnp.exp2(gap)


def mixer_forward(
    normed, wi, wsx, kin, kst, hp,
    inner_out, ssd_out, states_out, cst_out, bc_out, step_out, cum_out, stepT_out, cumT_out, preT_out,
    buf, gram, colc, cols, rowp, mst, xst, state,
):
    i = pl.program_id(0)
    tokens = normed.shape[0]
    spans = tokens // Q

    @pl.when(i == 0)
    def _():
        proj = mm(normed[...], wsx[...])
        buf[0:8] = jnp.zeros((8, BW), f32)
        cst_out[...] = proj[:, :BW]
        buf[8 : 8 + tokens] = proj[:, :BW]
        tri = (iota((Q, Q), 0) >= iota((Q, Q), 1)).astype(f32).astype(bf16)
        pre = proj[:, BW:] + hp[0:1]
        step = jnp.maximum(pre, 0.0) + jnp.log1p(jnp.exp(-jnp.abs(pre)))
        step_out[...] = step
        scaled = step * (hp[1:2] * LOG2E)
        for s in range(spans):
            parts = split3(scaled[s * Q : s * Q + Q])
            cum_out[s * Q : s * Q + Q] = mm(tri, parts[0]) + mm(tri, parts[1]) + mm(tri, parts[2])
            conv = conv_taps(buf[s * Q : s * Q + Q + 8], kst[...])
            bc = (conv * sigmoid(conv)).astype(bf16)
            bc_out[s * Q : s * Q + Q] = bc
            gram[s] = mm(bc[:, 128:], bc[:, :128], 1, 1)
        preT_out[...] = jnp.transpose(pre)[:48]
        stepT_out[...] = jnp.transpose(step)[:48]
        cumT_out[...] = jnp.transpose(cum_out[...])[:48]
        mst[...] = jnp.zeros(mst.shape, bf16)

    inner = mm(normed[...], wi[...])
    inner_out[...] = inner
    buf[8 : 8 + tokens] = inner
    turn = lax.rem(128 - 8 * i, 128)
    colc[...] = pltpu.roll(cum_out[...], turn, 1)
    cols[...] = pltpu.roll(step_out[...], turn, 1)
    rows8 = pl.ds(pl.multiple_of(8 * i, 8), 8)
    rowp[...] = cumT_out[rows8] - jnp.log2(stepT_out[rows8])
    state[...] = jnp.zeros(state.shape, f32)
    masks = head_masks()

    def span(s, carry):
        at = pl.multiple_of(s * Q, Q)
        rows = pl.ds(at, Q)
        conv = conv_taps(buf[pl.ds(at, Q + 8)], kin[...])
        xs = conv * sigmoid(conv)
        x_low = xs.astype(bf16)
        col = colc[rows]
        total = col[Q - 1 : Q]
        growth = expand(jnp.exp2(col[:, :8]))
        weight = expand(jnp.exp2(total[:, :8] - col[:, :8]) * cols[rows][:, :8])
        xw_low = (xs * weight).astype(bf16)
        for j in range(HB):
            xst[j * Q : j * Q + Q] = x_low * masks[j]
            row = rowp[j : j + 1, rows]
            for r, half, diag in quads():
                part = gram[s, r : r + 64, half * 128 : half * 128 + 128]
                dec = decay_chunk(col[:, j : j + 1], row, r, half, diag)
                mst[r : r + 64, j * Q + half * 128 : j * Q + half * 128 + 128] = (part * dec).astype(bf16)
        intra = mm(mst[...], xst[...])
        state_in = state[...]
        states_out[s] = state_in
        bc = bc_out[rows]
        readout = mm(bc[:, 128:], state_in.astype(bf16), 1, 1)
        ssd_out[rows] = intra + growth * readout + kin[5:6] * xs
        local = mm(xw_low, bc[:, :128], 0, 0)
        fade = jnp.exp2(total)
        for j in range(HB):
            at_j = slice(j * HEAD, j * HEAD + HEAD)
            state[at_j] = fade[:, j : j + 1] * state_in[at_j] + local[at_j]
        return carry

    lax.fori_loop(0, spans, span, 0)


def gate_forward(normed, cot, wg, wo, ssd, gain, gate_out, ggo_out, stats_out, sq, gi):
    i = pl.program_id(0)

    @pl.when(i == 0)
    def _():
        sq[...] = jnp.zeros(sq.shape, f32)
        gi[...] = jnp.zeros(gi.shape, f32)

    gate = mm(normed[...], wg[...])
    gate_out[...] = gate
    ggo = mm(cot[...], wo[...])
    ggo_out[...] = ggo
    gated = ssd[...] * (gate * sigmoid(gate))
    squares = gated * gated
    sq[...] += squares[:, :128] + squares[:, 128:]
    inner = ggo * gain[0:1] * gated
    gi[...] += inner[:, :128] + inner[:, 128:]

    @pl.when(i == pl.num_programs(0) - 1)
    def _():
        lane = iota(sq.shape, 1)
        both = jnp.where(
            lane == 0,
            jnp.sum(sq[...], axis=1, keepdims=True),
            jnp.where(lane == 1, jnp.sum(gi[...], axis=1, keepdims=True), 0.0),
        )
        stats_out[...] = jnp.transpose(both)[:8]


def gate_backward(unit_total, stats, gate, ssd, ggo, gain, dy_out, dgate_out, ng_out, gg_out, cols):
    @pl.when(pl.program_id(0) == 0)
    def _():
        full = jnp.concatenate([stats[...], jnp.zeros((120, stats.shape[1]), f32)], axis=0)
        cols[...] = jnp.transpose(full)

    rstd = lax.rsqrt(cols[:, 0:1] / unit_total + norm_eps)
    pull = rstd * rstd * rstd * (cols[:, 1:2] / unit_total)
    v = gate[...]
    sig = sigmoid(v)
    act = v * sig
    y = ssd[...]
    gated = y * act
    scaled = gated * rstd
    ng_out[...] = (scaled * gain[0:1]).astype(bf16)
    gg = ggo[...]
    gg_out[...] = jnp.broadcast_to(jnp.sum(gg * scaled, axis=0, keepdims=True), gg_out.shape)
    grad = rstd * (gg * gain[0:1]) - gated * pull
    dy_out[...] = (grad * act).astype(bf16)
    dgate_out[...] = (grad * y * (sig * (1.0 + v * (1.0 - sig)))).astype(bf16)


def mixer_backward(
    inner, dy, states, kin, kst, hp, cst, bc_in, step_in, cum_in, stepT, cumT, preT, rateT,
    dinner_out, gk_out, dsd_out, gks_out, hs_out,
    buf, dbuf, gram, gg, gb, gc, colc, cols, rowp, mst, dyst, gmix, sgrad, rs_t, cs_t, dr_t, wg_t, gt_t, gtaps,
):
    i = pl.program_id(0)
    tokens = inner.shape[0]
    spans = tokens // Q
    masks = head_masks()

    @pl.when(i == 0)
    def _():
        buf[0:8] = jnp.zeros((8, BW), f32)
        dbuf[tokens : tokens + 8] = jnp.zeros((8, BW), f32)
        for s in range(spans):
            bc = bc_in[s * Q : s * Q + Q]
            gram[s] = mm(bc[:, 128:], bc[:, :128], 1, 1)
        for ref in (gg, gb, gc, rs_t, cs_t, dr_t, wg_t, gt_t):
            ref[...] = jnp.zeros(ref.shape, f32)
        mst[...] = jnp.zeros(mst.shape, bf16)

    buf[8 : 8 + tokens] = inner[...]
    turn = lax.rem(128 - 8 * i, 128)
    colc[...] = pltpu.roll(cum_in[...], turn, 1)
    cols[...] = pltpu.roll(step_in[...], turn, 1)
    rows8 = pl.ds(pl.multiple_of(8 * i, 8), 8)
    rowp[...] = cumT[rows8] - jnp.log2(stepT[rows8])
    sgrad[...] = jnp.zeros(sgrad.shape, f32)
    gtaps[...] = jnp.zeros(gtaps.shape, f32)
    pick = (iota((8, BW), 1) // HEAD == iota((8, BW), 0)).astype(f32).astype(bf16)

    def conv_rows(at, kernel, grad_act):
        window = buf[pl.ds(at, Q + 8)]
        conv = conv_taps(window, kernel)
        sig = sigmoid(conv)
        gco = grad_act * (sig * (1.0 + conv * (1.0 - sig)))
        dbuf[pl.ds(at, Q)] = gco
        for k in range(4):
            prod = gco * (window[8:] if k == 3 else pltpu.roll(window, 3 - k, 0)[8:])
            gtaps[k : k + 1] += jnp.sum(prod, axis=0, keepdims=True)
        gtaps[4:5] += jnp.sum(gco, axis=0, keepdims=True)
        after = dbuf[pl.ds(at, Q + 8)]
        grad_in = kernel[3:4] * gco
        for k in range(3):
            grad_in = grad_in + kernel[k : k + 1] * pltpu.roll(after, Q + 8 - (3 - k), 0)[:Q]
        return grad_in

    def span(back, carry):
        s = spans - 1 - back
        at = pl.multiple_of(s * Q, Q)
        rows = pl.ds(at, Q)
        conv = conv_taps(buf[pl.ds(at, Q + 8)], kin[...])
        xs = conv * sigmoid(conv)
        x_low = xs.astype(bf16)
        dy_s = dy[rows]
        dy_f = dy_s.astype(f32)
        bc = bc_in[rows]
        b_low, c_low = bc[:, :128], bc[:, 128:]
        col = colc[rows]
        total = col[Q - 1 : Q]
        for j in range(HB):
            dyst[j * Q : j * Q + Q] = dy_s * masks[j]
        gmix[...] = mm(dyst[...], x_low, 1, 1)
        lane = iota((Q, 128), 1)
        row_sums = jnp.zeros((Q, 128), f32)
        for j in range(HB):
            row = rowp[j : j + 1, rows]
            col_sum = [jnp.zeros((1, 128), f32), jnp.zeros((1, 128), f32)]
            row_parts = []
            for r, half, diag in quads():
                here = slice(half * 128, half * 128 + 128)
                dec = decay_chunk(col[:, j : j + 1], row, r, half, diag)
                part = gram[s, r : r + 64, here]
                p = gmix[j * Q + r : j * Q + r + 64, here] * dec
                gg[s, r : r + 64, here] += p
                q = p * part
                mst[j * Q + r : j * Q + r + 64, here] = (part * dec).astype(bf16)
                col_sum[half] = col_sum[half] + jnp.sum(q, axis=0, keepdims=True)
                if half == 0:
                    row_parts.append(q)
                else:
                    row_parts[-1] = row_parts[-1] + q
            sums = jnp.concatenate([jnp.sum(q, axis=1, keepdims=True) for q in row_parts], axis=0)
            row_sums = jnp.where(lane == j, sums, row_sums)
            cs_t[pl.ds(8 * i + j, 1), rows] = jnp.concatenate(col_sum, axis=1)
        rs_t[rows8, rows] = jnp.transpose(row_sums)[:8]
        grad_xs = mm(mst[...], dyst[...], 0, 0) + kin[5:6] * dy_f

        growth = expand(jnp.exp2(col[:, :8]))
        weight = expand(jnp.exp2(total[:, :8] - col[:, :8]) * cols[rows][:, :8])
        state_in = states[s]
        state_low = state_in.astype(bf16)
        state_grad = sgrad[...]
        carry_low = state_grad.astype(bf16)
        readout = mm(c_low, state_low, 1, 1)
        read_low = (dy_f * growth).astype(bf16)
        hi, low = split2(dy_f * readout)
        dr_t[rows8, rows] = mm(pick, hi, 1, 1) + mm(pick, low, 1, 1)
        gc[rows] += mm(read_low, state_low)
        grad_xw = mm(b_low, carry_low, 1, 1)
        xw_low = (xs * weight).astype(bf16)
        gb[rows] += mm(xw_low, carry_low)
        hi, low = split2(grad_xw * xs)
        wg_t[rows8, rows] = mm(pick, hi, 1, 1) + mm(pick, low, 1, 1)
        hi, low = split2(state_grad * state_in)
        sums = jnp.sum(mm(pick, hi) + mm(pick, low), axis=1, keepdims=True)
        gt_t[rows8] = jnp.where(iota((8, 128), 1) == s, sums, gt_t[rows8])
        grad_xs = grad_xs + grad_xw * weight
        local = mm(read_low, c_low, 0, 0)
        fade = jnp.exp2(total)
        for j in range(HB):
            at_j = slice(j * HEAD, j * HEAD + HEAD)
            sgrad[at_j] = fade[:, j : j + 1] * state_grad[at_j] + local[at_j]
        gtaps[5:6] += jnp.sum(dy_f * xs, axis=0, keepdims=True)
        dinner_out[rows] = conv_rows(at, kin[...], grad_xs).astype(bf16)
        return carry

    lax.fori_loop(0, spans, span, 0)
    gk_out[...] = gtaps[...]

    @pl.when(i == pl.num_programs(0) - 1)
    def _():
        buf[8 : 8 + tokens] = cst[...]
        gtaps[...] = jnp.zeros(gtaps.shape, f32)
        rate = rateT[:, 0:1]
        later = (iota((Q, Q), 0) >= iota((Q, Q), 1)).astype(f32).astype(bf16)
        last = iota((48, Q), 1) == Q - 1
        bias_sum = jnp.zeros((48, 1), f32)
        decay_sum = jnp.zeros((48, 1), f32)
        for back in range(spans):
            s = spans - 1 - back
            rows = slice(s * Q, s * Q + Q)
            bc = bc_in[rows]
            gl = gg[s].astype(bf16)
            grad_c = gc[rows] + mm(gl, bc[:, :128])
            grad_b = gb[rows] + mm(gl, bc[:, 128:], 0, 0)
            both = jnp.concatenate([grad_b, grad_c], axis=1)
            dsd_out[rows, :BW] = conv_rows(s * Q, kst[...], both).astype(bf16)

            cum, step, pre = cumT[:, rows], stepT[:, rows], preT[:, rows]
            total = cum[:, Q - 1 : Q]
            rate_w = jnp.exp2(total - cum)
            wg = wg_t[:, rows]
            cs = cs_t[:, rows]
            moved = wg * (rate_w * step)
            grad_cum = rs_t[:, rows] - cs + jnp.exp2(cum) * dr_t[:, rows] - moved
            grad_total = jnp.exp2(total) * gt_t[:, s : s + 1] + jnp.sum(moved, axis=1, keepdims=True)
            grad_cum = grad_cum + jnp.where(last, grad_total, 0.0)
            parts = split3(grad_cum)
            grad_rate = mm(parts[0], later) + mm(parts[1], later) + mm(parts[2], later)
            sig = sigmoid(pre)
            ratio = jnp.where(pre < -15.0, 1.0, sig / step)
            grad_pre = (wg * rate_w + grad_rate * rate) * sig + cs * ratio
            bias_sum = bias_sum + jnp.sum(grad_pre, axis=1, keepdims=True)
            decay_sum = decay_sum + jnp.sum(grad_rate * step, axis=1, keepdims=True)
            full = jnp.concatenate([grad_pre, jnp.zeros((80, Q), f32)], axis=0)
            dsd_out[rows, BW:] = jnp.transpose(full).astype(bf16)
        gks_out[...] = gtaps[...]
        lane = iota((48, 128), 1)
        hs_out[...] = jnp.where(lane == 0, bias_sum, jnp.where(lane == 1, decay_sum * rate, 0.0))


def const(shape):
    return pl.BlockSpec(shape, lambda i: (0,) * len(shape))


def once(shape, at=None):
    where = at or (0,) * len(shape)
    return pl.BlockSpec(shape, lambda i: where, pipeline_mode=pl.Buffered(1))


def by_cols(rows, offset=0):
    return pl.BlockSpec((rows, BW), lambda i: (0, i + offset))


def params():
    return pltpu.CompilerParams(dimension_semantics=("arbitrary",), vmem_limit_bytes=60 * 1024 * 1024)


def spread(v):
    lead = v.shape[:-1]
    v = v.reshape(lead + (v.shape[-1] // HB, HB))
    v = jnp.pad(v, [(0, 0)] * len(lead) + [(0, 0), (0, 8 - HB)]).reshape(lead + (-1,))
    return jnp.pad(v, [(0, 0)] * len(lead) + [(0, 128 - v.shape[-1])])


def gathered_heads(v, heads):
    return v[..., : heads * 2].reshape(v.shape[:-1] + (heads // HB, 8))[..., :HB].reshape(v.shape[:-1] + (heads,))


def sds(shape, dtype=f32):
    return jax.ShapeDtypeStruct(shape, dtype)


def on_device(
    residual, norm_gain, w_gate_inner, w_state_io, w_step, conv_inner, conv_state,
    step_bias, decay_log, skip_gain, gate_gain, w_output, cotangent,
):
    width = residual.shape[1]
    units = w_gate_inner.shape[2]
    heads = w_step.shape[1]
    blocks = units // BW
    unit_total = units * lax.axis_size("tensor")
    rows_in = residual.astype(f32)
    rstd_in = lax.rsqrt(jnp.mean(rows_in * rows_in, axis=1, keepdims=True) + norm_eps)
    scaled = rows_in * rstd_in
    normed_local = (scaled * norm_gain).astype(bf16)
    pack_a = jnp.concatenate([w_gate_inner[1], w_state_io, spread(w_step)], axis=1)
    pack_b = jnp.concatenate([w_gate_inner[0], w_output.T], axis=1)
    wa = lax.all_gather(pack_a, "dp", axis=0, tiled=True)
    normed = lax.all_gather(normed_local, "tensor", axis=0, tiled=True)
    wb = lax.all_gather(pack_b, "dp", axis=0, tiled=True)
    cot = lax.all_gather(cotangent, "tensor", axis=0, tiled=True)
    tokens = normed.shape[0]
    spans = tokens // Q
    rate = -jnp.exp(decay_log)
    kin = jnp.concatenate([conv_inner, jnp.repeat(skip_gain, HEAD)[None], jnp.zeros((2, units), f32)], axis=0)
    kst = jnp.concatenate([conv_state, jnp.zeros((3, BW), f32)], axis=0)
    hp = jnp.concatenate([spread(step_bias)[None], spread(rate)[None], jnp.zeros((6, 128), f32)], axis=0)
    rate_t = jnp.broadcast_to(spread(rate)[:48, None], (48, 128))
    gain8 = jnp.broadcast_to(gate_gain[None], (8, units))

    inner, ssd, states, cst, bc, step, cum, step_t, cum_t, pre_t = pl.pallas_call(
        mixer_forward,
        name="mixer_forward",
        grid=(blocks,),
        in_specs=[
            once((tokens, width)), by_cols(width), once((width, 384), (0, units // 384)),
            by_cols(8), once((8, BW)), once((8, 128)),
        ],
        out_specs=[
            by_cols(tokens), by_cols(tokens), pl.BlockSpec((spans, BW, 128), lambda i: (0, i, 0)),
            once((tokens, BW)), once((tokens, BW)), once((tokens, 128)), once((tokens, 128)),
            once((48, tokens)), once((48, tokens)), once((48, tokens)),
        ],
        out_shape=[
            sds((tokens, units)), sds((tokens, units)), sds((spans, units, 128)),
            sds((tokens, BW)), sds((tokens, BW), bf16), sds((tokens, 128)), sds((tokens, 128)),
            sds((48, tokens)), sds((48, tokens)), sds((48, tokens)),
        ],
        scratch_shapes=[
            pltpu.VMEM((tokens + 8, BW), f32), pltpu.VMEM((spans, Q, Q), f32),
            pltpu.VMEM((tokens, 128), f32), pltpu.VMEM((tokens, 128), f32), pltpu.VMEM((8, tokens), f32),
            pltpu.VMEM((Q, HB * Q), bf16), pltpu.VMEM((HB * Q, BW), bf16), pltpu.VMEM((BW, 128), f32),
        ],
        compiler_params=params(),
        cost_estimate=pl.CostEstimate(flops=2 * tokens * width * (units + 384) + 4 * tokens * 256 * units, bytes_accessed=30_000_000, transcendentals=heads * spans * Q * Q),
    )(normed, wa, wa, kin, kst, hp)

    gate, ggo, stats = pl.pallas_call(
        gate_forward,
        name="gate_forward",
        grid=(blocks,),
        in_specs=[
            once((tokens, width)), once((tokens, width)), by_cols(width), by_cols(width, blocks),
            by_cols(tokens), by_cols(8),
        ],
        out_specs=[by_cols(tokens), by_cols(tokens), once((8, tokens))],
        out_shape=[sds((tokens, units)), sds((tokens, units)), sds((8, tokens))],
        scratch_shapes=[pltpu.VMEM((tokens, 128), f32), pltpu.VMEM((tokens, 128), f32)],
        compiler_params=params(),
        cost_estimate=pl.CostEstimate(flops=4 * tokens * width * units, bytes_accessed=35_000_000, transcendentals=tokens * units),
    )(normed, cot, wb, wb, ssd, gain8)
    stats = lax.psum(stats, "tensor")

    dy, dgate, ng, ggg = pl.pallas_call(
        functools.partial(gate_backward, float(unit_total)),
        name="gate_backward",
        grid=(blocks,),
        in_specs=[once((8, tokens)), by_cols(tokens), by_cols(tokens), by_cols(tokens), by_cols(8)],
        out_specs=[by_cols(tokens), by_cols(tokens), by_cols(tokens), by_cols(8)],
        out_shape=[sds((tokens, units), bf16), sds((tokens, units), bf16), sds((tokens, units), bf16), sds((8, units))],
        scratch_shapes=[pltpu.VMEM((tokens, 128), f32)],
        compiler_params=params(),
        cost_estimate=pl.CostEstimate(flops=20 * tokens * units, bytes_accessed=30_000_000, transcendentals=tokens * units),
    )(stats, gate, ssd, ggo, gain8)

    grad_wo = mm(cot, ng, 0, 0).astype(bf16)
    grad_wg = mm(normed, dgate, 0, 0).astype(bf16)
    wo_shard = lax.psum_scatter(grad_wo, "dp", scatter_dimension=0, tiled=True)
    wg_shard = lax.psum_scatter(grad_wg, "dp", scatter_dimension=0, tiled=True)
    mixed = lax.psum_scatter(mm(ng, wb[:, units:], 1, 1).astype(bf16), "tensor", scatter_dimension=0, tiled=True)
    output = (rows_in + mixed.astype(f32)).astype(bf16)

    dinner, gk, dsd, gks, hs = pl.pallas_call(
        mixer_backward,
        name="mixer_backward",
        grid=(blocks,),
        in_specs=[
            by_cols(tokens), by_cols(tokens), pl.BlockSpec((spans, BW, 128), lambda i: (0, i, 0)),
            by_cols(8), once((8, BW)), once((8, 128)),
            once((tokens, BW)), once((tokens, BW)), once((tokens, 128)), once((tokens, 128)),
            once((48, tokens)), once((48, tokens)), once((48, tokens)), once((48, 128)),
        ],
        out_specs=[by_cols(tokens), by_cols(8), once((tokens, 384)), once((8, BW)), once((48, 128))],
        out_shape=[sds((tokens, units), bf16), sds((8, units)), sds((tokens, 384), bf16), sds((8, BW)), sds((48, 128))],
        scratch_shapes=[
            pltpu.VMEM((tokens + 8, BW), f32), pltpu.VMEM((tokens + 8, BW), f32),
            pltpu.VMEM((spans, Q, Q), f32), pltpu.VMEM((spans, Q, Q), f32),
            pltpu.VMEM((tokens, 128), f32), pltpu.VMEM((tokens, 128), f32),
            pltpu.VMEM((tokens, 128), f32), pltpu.VMEM((tokens, 128), f32), pltpu.VMEM((8, tokens), f32),
            pltpu.VMEM((HB * Q, Q), bf16), pltpu.VMEM((HB * Q, BW), bf16), pltpu.VMEM((HB * Q, Q), f32),
            pltpu.VMEM((BW, 128), f32),
            pltpu.VMEM((48, tokens), f32), pltpu.VMEM((48, tokens), f32), pltpu.VMEM((48, tokens), f32),
            pltpu.VMEM((48, tokens), f32), pltpu.VMEM((48, 128), f32), pltpu.VMEM((8, BW), f32),
        ],
        compiler_params=params(),
        cost_estimate=pl.CostEstimate(flops=40_000_000_000, bytes_accessed=30_000_000, transcendentals=heads * spans * Q * Q),
    )(inner, dy, states, kin, kst, hp, cst, bc, step, cum, step_t, cum_t, pre_t, rate_t)

    grad_wi = mm(normed, dinner, 0, 0).astype(bf16)
    grad_ws = mm(normed, dsd, 0, 0).astype(bf16)
    wa_shard = lax.psum_scatter(jnp.concatenate([grad_wi, grad_ws], axis=1), "dp", scatter_dimension=0, tiled=True)
    grad_normed = (
        mm(dgate, wb[:, :units], 1, 1) + mm(dinner, wa[:, :units], 1, 1) + mm(dsd, wa[:, units:], 1, 1)
    ).astype(bf16)
    grad_normed = lax.psum_scatter(grad_normed, "tensor", scatter_dimension=0, tiled=True).astype(f32)
    grad_v = grad_normed * norm_gain
    grad_residual = cotangent.astype(f32) + rstd_in * (
        grad_v - scaled * jnp.mean(grad_v * scaled, axis=1, keepdims=True)
    )

    small = jnp.concatenate([gk, ggg, jnp.pad(gks, ((0, 0), (0, units - BW)))], axis=0)
    small = jnp.concatenate([small.reshape(-1), hs[:, 0], hs[:, 1]])
    small = lax.psum(small, "dp")
    table = small[: 24 * units].reshape(24, units)
    bias_sum = gathered_heads(small[24 * units : 24 * units + 48], heads)
    decay_sum = gathered_heads(small[24 * units + 48 : 24 * units + 96], heads)
    skip_sum = jnp.sum(table[5].reshape(heads, HEAD), axis=1)

    wg_f, wa_f, wo_f = wg_shard.astype(f32), wa_shard.astype(f32), wo_shard.astype(f32)
    gain_rows = jnp.sum(wg_f * w_gate_inner[0].astype(f32), axis=1) + jnp.sum(wa_f * pack_a.astype(f32), axis=1)
    gain_own = gain_rows / lax.dynamic_slice_in_dim(
        norm_gain, lax.axis_index("dp") * gain_rows.shape[0], gain_rows.shape[0]
    )
    state_own = wa_f[:, units : units + BW]
    conv_state_part, state_part, gain_part = (
        lax.psum_scatter(table[16:21, :BW], "tensor", scatter_dimension=1, tiled=True),
        lax.psum_scatter(state_own, "tensor", scatter_dimension=1, tiled=True),
        lax.psum_scatter(gain_own, "tensor", scatter_dimension=0, tiled=True),
    )
    return (
        output,
        grad_residual,
        gain_part,
        jnp.stack([wg_f, wa_f[:, :units]]),
        state_part,
        gathered_heads(wa_f[:, units + BW :], heads),
        table[0:5],
        conv_state_part,
        bias_sum,
        decay_sum,
        skip_sum,
        table[8],
        wo_f.T,
    )


def solution(mesh):
    return jax.shard_map(
        on_device,
        mesh=mesh,
        in_specs=(
            P(("dp", "tensor"), None),
            P(),
            P(None, "dp", "tensor"),
            P("dp", None),
            P("dp", "tensor"),
            P(None, "tensor"),
            P(),
            P("tensor"),
            P("tensor"),
            P("tensor"),
            P("tensor"),
            P("tensor", "dp"),
            P(("dp", "tensor"), None),
        ),
        out_specs=(
            P(("dp", "tensor"), None),
            P(("dp", "tensor"), None),
            P(("dp", "tensor")),
            P(None, "dp", "tensor"),
            P("dp", "tensor"),
            P("dp", "tensor"),
            P(None, "tensor"),
            P(None, "tensor"),
            P("tensor"),
            P("tensor"),
            P("tensor"),
            P("tensor"),
            P("tensor", "dp"),
        ),
        check_vma=False,
    )
```

time: 1220 us -> 821 us (0.67)
  matrix products: 208 us -> 57.1 us
  local copies, waits for them, and re-layouts: 166 us -> 27.6 us
  Pallas kernels: 0 us -> 136 us
  other arithmetic: 158 us -> 25.3 us
  blocking collectives: 121 us -> 14.5 us
    reduce_scatter x7 -> x6, waiting for transfers between devices: 438 us -> 253 us  [the longest x1 83.2 us: on_device(): lax.psum_scatter(jnp.concatenate([grad_wi, grad_ws], axis=1), 'dp', scatt...]
    dot_general x70 -> x8, matrix products: 204 us -> 57.1 us  [mm(): lax.dot_general(a, b, (((ca,), (cb,)), ((), ())), preferred_element_type=...]
    pallas_call x0 -> x4, Pallas kernels: none -> 136 us  [the longest x1 68.1 us: on_device(): pl.pallas_call(mixer_backward, name='mixer_backward', grid=(blocks,), in_...]
    all_gather x3, waiting for transfers between devices: 76.2 us -> 156 us  [the longest x1 83.6 us: on_device(): wb = lax.all_gather(pack_b, 'dp', axis=0, tiled=True)]
    unnamed x2 -> x1, blocking collectives: 67.7 us -> 4.91 us
    unnamed x13, waiting for transfers between devices: 26.9 us -> 75 us
    reduce_sum x25 -> x4, other arithmetic: 52.4 us -> 5.1 us  [the longest x1 2.15 us: on_device(): jnp.mean(grad_v * scaled, axis=1, keepdims=True)]
    dynamic_update_slice x24 -> x0, local copies, waits for them, and re-layouts: 45.8 us -> none  [the longest x16 36 us: on_device(): lax.scan(forward_step, start_state, (xs_spans, b_spans, c_spans, step_spa...]
  transfers between devices with their start and end apart: 12 -> 12, of which waited for: 10 -> 11; matrix products, arithmetic and copies ran while one was open for 18% -> 12% of each run, Pallas kernels for 0% -> 4%
where the time goes in v1:
time: 821 us; the launch traced here: 820 us
  waiting for transfers between devices  543 us (66%)
  Pallas kernels  136 us (17%)
  matrix products  57.1 us (7%)
  local copies, waits for them, and re-layouts  27.6 us (3%)
  other arithmetic  25.3 us (3%)
  between operations  15.3 us (2%)
  blocking collectives  14.5 us (2%)
    all_gather x1, waiting for transfers between devices, on_device(): wb = lax.all_gather(pack_b, 'dp', axis=0, tiled=True)  83.6 us
    reduce_scatter x1, waiting for transfers between devices, on_device(): lax.psum_scatter(jnp.concatenate([grad_wi, grad_ws], axis=1), 'dp', scatt...  83.2 us
    reduce_scatter x1, waiting for transfers between devices, on_device(): wg_shard = lax.psum_scatter(grad_wg, 'dp', scatter_dimension=0, tiled=True)  76.4 us
    unnamed x13, waiting for transfers between devices  75 us
    pallas_call x1, Pallas kernels, on_device(): pl.pallas_call(mixer_backward, name='mixer_backward', grid=(blocks,), in_...  68.1 us
    all_gather x1, waiting for transfers between devices, on_device(): wa = lax.all_gather(pack_a, 'dp', axis=0, tiled=True)  62.2 us
    dot_general x8, matrix products, mm(): lax.dot_general(a, b, (((ca,), (cb,)), ((), ())), preferred_element_type=...  57.1 us
    reduce_scatter x1, waiting for transfers between devices, on_device(): lax.psum_scatter(mm(ng, wb[:, units:], 1, 1).astype(bf16), 'tensor', scat...  43.5 us
  transfers between devices with their start and end apart: 12, of which 11 were waited for; matrix products, arithmetic and copies ran while one was open for 12% of the time, Pallas kernels for 4%

profile of v1, /device:TPU:0, one launch (start us, length us, event | category | flops | bytes accessed | tf_op | source)
XLA Modules:
  0.0 819.7 jit_solution(4613800077232038085)
XLA Ops:
  7.2 1.8 fusion.18
  9.1 3.0 fusion.13
  12.4 0.8 fusion.23
  14.0 0.9 pad_maximum_fusion.2
  17.6 42.3 %all-gather.5.cloned.1.call-done.normed = bf16[1024,1536]{1,0:T(8,128)(2,1)} async-done(((bf16[512,1536]{1,0:T(8,128)(2,1)}), bf16[1024,1536]{1,0:T(8,128)(2,1)}) %all-gather.5.cloned.1.call-update) | async-done | bytes 3145744 | tf_op jit(solution)/shard_map/all_gather | solution.py:421
  59.9 62.2 %all-gather.11.cloned.1.call-done.wi.wsx = bf16[1536,1920]{1,0:T(8,128)(2,1)} async-done(((bf16[96,1920]{1,0:T(8,128)(2,1)}), bf16[1536,1920]{1,0:T(8,128)(2,1)}) %all-gather.11.cloned.1.call-update) | async-done | bytes 5898256 | tf_op jit(solution)/shard_map/all_gather | solution.py:420
  122.1 35.1 %mixer_forward.1 = (f32[1024,1536]{1,0:T(8,128)}, f32[1024,1536]{1,0:T(8,128)}, f32[4,1536,128]{2,1,0:T(8,128)}, f32[1024,256]{1,0:T(8,128)}, bf16[1024,256]{1,0...) custom-call(bf16[1024,1536]{1,0:T(8,128)(2,1)} %all-gather.5.cloned., ...), custom_call_target="tpu_custom_call" | custom-call | flops 7650410496 | bytes 30000000 | tf_op jit(solution)/shard_map/mixer_forward/pallas_call | solution.py:433
  157.2 10.1 %all-gather.7.cloned.1.call-done.cot = bf16[1024,1536]{1,0:T(8,128)(2,1)} async-done(((bf16[512,1536]{1,0:T(8,128)(2,1)}), bf16[1024,1536]{1,0:T(8,128)(2,1)}) %all-gather.7.cloned.1.call-update) | async-done | bytes 3145744 | tf_op jit(solution)/shard_map/all_gather | solution.py:423
  167.2 83.6 %all-gather.9.cloned.1.call-done.wg.wo = bf16[1536,3072]{1,0:T(8,128)(2,1)} async-done(((bf16[96,3072]{1,0:T(8,128)(2,1)}), bf16[1536,3072]{1,0:T(8,128)(2,1)}) %all-gather.9.cloned.1.call-update) | async-done | bytes 9437200 | tf_op jit(solution)/shard_map/all_gather | solution.py:422
  251.5 18.9 %gate_forward.1 = (f32[1024,1536]{1,0:T(8,128)}, f32[1024,1536]{1,0:T(8,128)}, f32[8,1024]{1,0:T(8,128)}) custom-call(bf16[1024,1536]{1,0:T(8,128)(2,1)} %all-gather.5.cloned.1.call-done.normed, bf16[1024,1536]{1,0:T(8,128)(2,1)} %all-gather.7.cloned.1.call-done.cot, bf16[1536,3072]{1,0:T(8,128)(2,1)} %all-gather.9.cloned.1.call-done.wg.wo, ...), custom_call_target="tpu_custom_call" | custom-call | flops 9663676416 | bytes 35000000 | tf_op jit(solution)/shard_map/gate_forward/pallas_call | solution.py:460
  270.4 9.5 %psum.14.stats = f32[8,1024]{1,0:T(8,128)} all-reduce(f32[8,1024]{1,0:T(8,128)} %get-tuple-element.36), channel_id=1, replica_groups=mesh['dp'=16,'tensor'=2] {'tensor'}, use_global_device_ids=true, to_apply=%region_1.2 | all-reduce | flops 8192 | bytes 65536 | tf_op jit(solution)/shard_map/psum | solution.py:474
  280.0 13.9 %gate_backward.1 = (bf16[1024,1536]{1,0:T(8,128)(2,1)}, bf16[1024,1536]{1,0:T(8,128)(2,1)}, bf16[1024,1536]{1,0:T(8,128)(2,1)}, f32[8,1536]{1,0:T(8,128)}) custom-call(f32[8,1024]{1,0:T(8,128)} %psum.14.stats, f32[1024,1536]{1,0:T(8,128)} %get-tuple-element.37.gate, f32[1024,1536]{1,0:T(8,128)} %get-tuple-element.35.ssd, ...), custom_call_target="tpu_custom_call" | custom-call | flops 31457280 | bytes 30000000 | tf_op jit(solution)/shard_map/gate_backward/pallas_call | solution.py:476
  294.6 68.1 %mixer_backward.1 = (bf16[1024,1536]{1,0:T(8,128)(2,1)}, f32[8,1536]{1,0:T(8,128)}, bf16[1024,384]{1,0:T(8,128)(2,1)}, f32[8,256]{1,0:T(8,128)}, f32[48,128]{1,0:T(8,128)}) custom-call(f32[1024,1536]{1,0:T(8,128)} %get-tuple-element.41.inner, bf16[1024,1536]{1,0:T(8,128)(2,1)} %get-tuple-element.42.dy, f32[4,1536,128]{2,1,0:T(8,128)} %get-tuple-element.43.states, ...), custom_call_target="tpu_custom_call" | custom-call | flops 40000000000 | bytes 30000000 | tf_op jit(solution)/shard_map/mixer_backward/pallas_call | solution.py:495
  362.7 0.8 select_maximum_fusion
  363.6 1.0 slice_reduce_fusion
  365.4 8.1 fusion.1
  373.5 7.0 fusion.3
  380.5 4.8 add_convert_fusion
  385.7 9.3 %fusion.10 = bf16[1024,1536]{1,0:T(8,128)(2,1)} fusion(bf16[1024,1536]{1,0:T(8,128)(2,1)} %get-tuple-element.39, bf16[1536,3072]{1,0:T(8,128)(2,1)} %all-gather.9.cloned.1.call-done.wg.wo), kind=kOutput, calls=%fused_computation.18 | convolution fusion | flops 4833411072 | bytes 11010048 | tf_op jit(solution)/shard_map/dot_general | solution.py:23
  395.0 9.3 %fusion = bf16[1536,1536]{0,1:T(8,128)(2,1)} fusion(bf16[1024,1536]{1,0:T(8,128)(2,1)} %get-tuple-element.39, bf16[1024,1536]{1,0:T(8,128)(2,1)} %all-gather.7.cloned.1.call-done.cot), kind=kOutput, calls=%fused_computation.3 | convolution fusion | flops 4834197504 | bytes 11010048 | tf_op jit(solution)/shard_map/dot_general | solution.py:23
  404.3 6.7 copy.48
  411.0 9.3 %convolution_convert_fusion.2 = bf16[1536,1536]{1,0:T(8,128)(2,1)} fusion(bf16[1024,1536]{1,0:T(8,128)(2,1)} %all-gather.5.cloned.1.call-done.normed, bf16[1024,1536]{1,0:T(8,128)(2,1)} %get-tuple-element.40), kind=kOutput, calls=%fused_computation.2 | convolution fusion | flops 4834197504 | bytes 11010048 | tf_op jit(solution)/shard_map/dot_general | solution.py:23
  420.7 3.9 convolution_convert_fusion.3
  424.6 5.4 convolution_convert_fusion.1
  430.0 2.9 pad_maximum_fusion
  434.8 17.1 %all-reduce.11.cloned.1.call-done = f32[36960]{0:T(1024)} async-done(((f32[36960]{0:T(1024)}), f32[36960]{0:T(1024)}) %all-reduce.11.cloned.1.call-update) | async-done | bytes 147856 | tf_op jit(solution)/shard_map/psum | solution.py:535
  451.9 1.6 slice.129
  453.5 1.6 reshape.120
  455.1 1.3 slice.130
  457.8 1.3 fusion.24
  459.8 0.8 fusion.25
  462.0 37.0 %reduce-scatter.12.cloned.1.call-done = bf16[512,1536]{1,0:T(8,128)(2,1)} async-done(((bf16[1024,1536]{1,0:T(8,128)(2,1)}), bf16[512,1536]{1,0:T(8,128)(2,1)}) %reduce-scatter.12.cloned.1.call-update) | async-done | bytes 1572880 | tf_op jit(solution)/shard_map/reduce_scatter | solution.py:527
  499.0 2.1 fusion.14
  501.2 43.5 %reduce-scatter.10.cloned.1.call-done = bf16[512,1536]{1,0:T(8,128)(2,1)} async-done(((bf16[1024,1536]{1,0:T(8,128)(2,1)}), bf16[512,1536]{1,0:T(8,128)(2,1)}) %reduce-scatter.10.cloned.1.call-update) | async-done | bytes 1572880 | tf_op jit(solution)/shard_map/reduce_scatter | solution.py:492
  544.7 5.4 fusion.17
  550.1 74.1 %reduce-scatter.22.cloned.1.call-done = bf16[96,1536]{1,0:T(8,128)(2,1)} async-done(((bf16[1536,1536]{1,0:T(8,128)(2,1)}), bf16[96,1536]{1,0:T(8,128)(2,1)}) %reduce-scatter.22.cloned.1.call-update) | async-done | bytes 294928
  624.2 1.2 copy.49
  625.5 1.1 copy.45
  626.5 76.4 %reduce-scatter.14.cloned.1.call-done = bf16[96,1536]{1,0:T(8,128)(2,1)} async-done(((bf16[1536,1536]{1,0:T(8,128)(2,1)}), bf16[96,1536]{1,0:T(8,128)(2,1)}) %reduce-scatter.14.cloned.1.call-update) | async-done | bytes 294928 | tf_op jit(solution)/shard_map/reduce_scatter | solution.py:491
  702.9 1.0 convert_bitcast_fusion.1
  703.9 1.1 fusion.22
  705.1 83.2 %reduce-scatter.16.cloned.1.call-done = bf16[96,1920]{1,0:T(8,128)(2,1)} async-done(((bf16[1536,1920]{1,0:T(8,128)(2,1)}), bf16[96,1920]{1,0:T(8,128)(2,1)}) %reduce-scatter.16.cloned.1.call-update) | async-done | bytes 368656 | tf_op jit(solution)/shard_map/reduce_scatter | solution.py:523
  788.3 1.0 convert_element_type.79
  789.4 1.2 multiply_reduce_fusion
  792.1 1.5 slice.125
  793.6 4.9 all-reduce.8
  799.1 1.1 pad_maximum_fusion.1
  800.2 12.7 %reduce-scatter.18.cloned.1.call-done = f32[96,128]{1,0:T(8,128)} async-done(((f32[96,256]{1,0:T(8,128)}), f32[96,128]{1,0:T(8,128)}) %reduce-scatter.18.cloned.1.call-update) | async-done | bytes 49168 | tf_op jit(solution)/shard_map/reduce_scatter | solution.py:549
  (111 shorter events, 13.6 us)
Async XLA Ops:
  7.2 5.1 copy-start.14
  7.2 5.2 copy-start.2
  7.2 52.7 %all-gather.5.cloned.1.call-start = ((), (), s32[]{:S(2)}) async-start(), calls=%async_computation.7 | async-start | bytes 4718592 | tf_op jit(solution)/shard_map/all_gather | solution.py:421
  9.1 3.3 copy-start.6
  9.1 3.1 copy-start.10
  12.1 1.9 copy-start.5
  12.1 2.8 copy-start.19
  12.1 3.0 copy-start.15
  12.1 3.2 copy-start.16
  12.2 3.5 copy-start.13
  12.2 4.8 copy-start.8
  12.2 109.9 %all-gather.11.cloned.1.call-start = ((), (), s32[]{:S(2)}) async-start(), calls=%async_computation.10 | async-start | bytes 6266880 | tf_op jit(solution)/shard_map/all_gather | solution.py:420
  13.2 154.0 %all-gather.7.cloned.1.call-start = ((), (), s32[]{:S(2)}) async-start(), calls=%async_computation.8 | async-start | bytes 4718592 | tf_op jit(solution)/shard_map/all_gather | solution.py:423
  14.0 236.9 %all-gather.9.cloned.1.call-start = ((), (), s32[]{:S(2)}) async-start(), calls=%async_computation.9 | async-start | bytes 10027008 | tf_op jit(solution)/shard_map/all_gather | solution.py:422
  14.9 437.0 %all-reduce.11.cloned.1.call-start = ((), (), s32[]{:S(2)}) async-start(), calls=%async_computation.16 | async-start | bytes 303104 | tf_op jit(solution)/shard_map/psum | solution.py:535
  17.6 233.3 %copy-start.12 = (f32[1536]{0:T(1024)S(1)}, f32[1536]{0:T(1024)}, u32[]{:S(2)}) copy-start(f32[1536]{0:T(1024)} %param.23) | copy-start | bytes 18436
  294.6 68.1 %copy-start.9 = (f32[8,1536]{1,0:T(8,128)S(1)}, f32[8,1536]{1,0:T(8,128)}, u32[]{:S(2)}) copy-start(f32[8,1536]{1,0:T(8,128)} %get-tuple-element.54) | copy-start | bytes 147460
  365.3 133.7 %reduce-scatter.12.cloned.1.call-start = ((), (), s32[]{:S(2)}) async-start(), calls=%async_computation.12 | async-start | bytes 4718592 | tf_op jit(solution)/shard_map/reduce_scatter | solution.py:527
  365.4 8.1 copy-start.18
  373.5 7.1 copy-start.4
  385.4 159.3 %reduce-scatter.10.cloned.1.call-start = ((), (), s32[]{:S(2)}) async-start(), calls=%async_computation.11 | async-start | bytes 4718592 | tf_op jit(solution)/shard_map/reduce_scatter | solution.py:492
  395.0 229.2 %reduce-scatter.22.cloned.1.call-start = ((), (), s32[]{:S(2)}) async-start(), calls=%async_computation.18 | async-start | bytes 5013504
  411.0 291.9 %reduce-scatter.14.cloned.1.call-start = ((), (), s32[]{:S(2)}) async-start(), calls=%async_computation.13 | async-start | bytes 5013504 | tf_op jit(solution)/shard_map/reduce_scatter | solution.py:491
  420.4 367.9 %reduce-scatter.16.cloned.1.call-start = ((), (), s32[]{:S(2)}) async-start(), calls=%async_computation.14 | async-start | bytes 6266880 | tf_op jit(solution)/shard_map/reduce_scatter | solution.py:523
  420.7 3.9 copy-start.17
  420.7 3.9 copy-start.21
  432.9 0.7 copy-start.20
  432.9 66.1 %copy-start = (bf16[512,1536]{1,0:T(8,128)(2,1)S(1)}, bf16[512,1536]{1,0:T(8,128)(2,1)}, u32[]{:S(2)}) copy-start(bf16[512,1536]{1,0:T(8,128)(2,1)} %param.13) | copy-start | bytes 4718596
  432.9 66.1 %copy-start.7 = (f32[1536]{0:T(1024)S(1)}, f32[1536]{0:T(1024)}, u32[]{:S(2)}) copy-start(f32[1536]{0:T(1024)} %param.14) | copy-start | bytes 18436
  433.0 111.7 %copy-start.1 = (bf16[512,1536]{1,0:T(8,128)(2,1)S(1)}, bf16[512,1536]{1,0:T(8,128)(2,1)}, u32[]{:S(2)}) copy-start(bf16[512,1536]{1,0:T(8,128)(2,1)} %param.25) | copy-start | bytes 4718596
  433.0 367.2 %reduce-scatter.20.cloned.1.call-start = ((), (), s32[]{:S(2)}) async-start(), calls=%async_computation.17 | async-start | bytes 12288 | tf_op jit(solution)/shard_map/reduce_scatter | solution.py:548
  457.8 87.0 %copy-start.11 = (f32[512]{0:T(512)S(1)}, f32[512]{0:T(512)}, u32[]{:S(2)}) copy-start(f32[512]{0:T(512)} %copy-done.10) | copy-start | bytes 6148
  462.0 350.9 %reduce-scatter.18.cloned.1.call-start = ((), (), s32[]{:S(2)}) async-start(), calls=%async_computation.15 | async-start | bytes 147456 | tf_op jit(solution)/shard_map/reduce_scatter | solution.py:549
  550.1 153.8 %copy-start.3 = (bf16[2,96,1536]{2,1,0:T(8,128)(2,1)S(1)}, bf16[2,96,1536]{2,1,0:T(8,128)(2,1)}, u32[]{:S(2)}) copy-start(bf16[2,96,1536]{2,1,0:T(8,128)(2,1)} %param.15) | copy-start | bytes 1769476
Sparse Core Ops, SparseCore 0:
  12.2 47.6 all-gather.4
  62.8 59.2 all-gather.10
  123.6 43.5 all-gather.6
  170.0 80.8 all-gather.8
  365.5 86.4 all-reduce.10
  454.6 44.4 reduce-scatter.11
  501.3 43.3 reduce-scatter.9
  548.6 75.5 reduce-scatter.21
  628.1 74.7 reduce-scatter.13
  706.7 81.5 reduce-scatter.15
  791.1 9.0 reduce-scatter.19
  802.7 10.0 reduce-scatter.17

commit v2 on v1

--- a/solution.py
+++ b/solution.py
@@ -15,6 +15,7 @@
 LOG2E = 1.4426950408889634
 FAR = -1e30
 norm_eps = 1e-05
+MESH = pl.DeviceIdType.MESH
 f32 = jnp.float32
 bf16 = jnp.bfloat16
 
@@ -370,8 +371,402 @@
         hs_out[...] = jnp.where(lane == 0, bias_sum, jnp.where(lane == 1, decay_sum * rate, 0.0))
 
 
-def const(shape):
-    return pl.BlockSpec(shape, lambda i: (0,) * len(shape))
+class Place:
+    def __init__(self):
+        me = lax.axis_index("dp")
+        self.me = me
+        self.c, self.y, self.z = me % 2, (me // 2) % 2, me // 4
+
+    def at(self, z, y, c):
+        return (z * 2 + y) * 2 + c
+
+    def core(self):
+        return self.at(self.z, self.y, 1 - self.c)
+
+    def side(self):
+        return self.at(self.z, 1 - self.y, self.c)
+
+    def up(self):
+        return self.me + 4
+
+    def down(self):
+        return self.me - 4
+
+
+def greet(here, across):
+    barrier = pltpu.get_barrier_semaphore()
+
+    def signal(**device):
+        pl.semaphore_signal(barrier, 1, device_id=device, device_id_type=MESH)
+
+    signal(dp=here.core())
+    signal(dp=here.side())
+    pl.when(here.z < 3)(lambda: signal(dp=here.up()))
+    pl.when(here.z > 0)(lambda: signal(dp=here.down()))
+    if across:
+        signal(tensor=1 - lax.axis_index("tensor"))
+    ends = (here.z == 0).astype(jnp.int32) + (here.z == 3).astype(jnp.int32)
+    pl.semaphore_wait(barrier, 4 + int(across) - ends)
+
+
+def remote(src, dst, send_sem, recv_sem, **device):
+    return pltpu.make_async_remote_copy(
+        src_ref=src, dst_ref=dst, send_sem=send_sem, recv_sem=recv_sem, device_id=device, device_id_type=MESH
+    )
+
+
+class Gather:
+    def __init__(self, here, own, full, ss, rs):
+        self.here, self.own, self.full, self.ss, self.rs = here, own, full, ss, rs
+        self.rows = own.shape[0]
+
+    def slot(self, origin):
+        return self.full.at[pl.ds(pl.multiple_of(origin * self.rows, self.rows), self.rows)]
+
+    def copy(self, origin, way, src=None):
+        here = self.here
+        target = (here.up, here.down, here.side, here.core)[way]()
+        slot = self.slot(origin)
+        return remote(slot if src is None else src, slot, self.ss.at[origin, way], self.rs.at[origin], dp=target)
+
+    def arrived(self, origin):
+        self.copy(origin, 3).wait_recv()
+
+    def each_send(self, act):
+        here = self.here
+        for hops in range(4):
+            for way, origin_z in ((0, here.z - hops), (1, here.z + hops)):
+                if hops == 0:
+                    if way == 1:
+                        continue
+                    origin = here.me
+                    pl.when(here.z < 3)(lambda o=origin: act(o, 0))
+                    pl.when(here.z > 0)(lambda o=origin: act(o, 1))
+                    act(origin, 2)
+                    act(origin, 3)
+                    continue
+                origin = here.at(origin_z, here.y, here.c)
+
+                def go(o=origin, way=way):
+                    pl.when((here.z < 3) if way == 0 else (here.z > 0))(lambda: act(o, way))
+                    act(o, 2)
+                    act(o, 3)
+
+                pl.when((origin_z >= 0) & (origin_z <= 3))(go)
+
+    def start(self):
+        here = self.here
+        pl.when(here.z < 3)(lambda: self.copy(here.me, 0, self.own).start())
+        pl.when(here.z > 0)(lambda: self.copy(here.me, 1, self.own).start())
+        self.copy(here.me, 2, self.own).start()
+        self.copy(here.me, 3, self.own).start()
+
+    def hop(self, hops):
+        here = self.here
+        for way, origin_z in ((0, here.z - hops), (1, here.z + hops)):
+
+            def go(way=way, origin_z=origin_z):
+                origin = here.at(origin_z, here.y, here.c)
+                self.arrived(origin)
+                pl.when((here.z < 3) if way == 0 else (here.z > 0))(lambda: self.copy(origin, way).start())
+                self.copy(origin, 2).start()
+                self.copy(origin, 3).start()
+
+            pl.when((origin_z >= 0) & (origin_z <= 3))(go)
+
+    def sides(self, hops):
+        here = self.here
+        for way, origin_z in ((0, here.z - hops), (1, here.z + hops)):
+            if hops == 0 and way == 1:
+                continue
+
+            def go(origin_z=origin_z):
+                origin = here.at(origin_z, 1 - here.y, here.c)
+                self.arrived(origin)
+                self.copy(origin, 3).start()
+
+            pl.when((origin_z >= 0) & (origin_z <= 3))(go)
+
+    def finish(self):
+        here = self.here
+        for z in range(4):
+            for y in range(2):
+                self.arrived(here.at(z, y, 1 - here.c))
+        self.each_send(lambda origin, way: self.copy(origin, way).wait_send())
+        for z in range(4):
+            self.copy(here.at(z, 1 - here.y, here.c), 3).wait_send()
+
+
+def gather_kernel(tokens_in, gain, pack, tokens_out, full, low, ss, rs, xs, xr, ls, norm):
+    here = Place()
+    half = lax.axis_index("tensor")
+    rows = tokens_in.shape[0]
+    greet(here, True)
+    moves = Gather(here, pack, full, ss, rs)
+    moves.start()
+    own = pltpu.make_async_copy(pack, moves.slot(here.me), ls.at[0])
+    own.start()
+    part = rows // 4
+    across, local = [], []
+    for n in range(4):
+        piece = slice(n * part, n * part + part)
+        if norm:
+            v = tokens_in[piece].astype(f32)
+            scale = lax.rsqrt(jnp.mean(v * v, axis=1, keepdims=True) + norm_eps)
+            low[piece] = (v * scale * gain[...]).astype(bf16)
+        else:
+            low[piece] = tokens_in[piece]
+        slot = tokens_out.at[pl.ds(pl.multiple_of(half * rows + n * part, part), part)]
+        across.append(remote(low.at[piece], slot, xs.at[n], xr.at[n], tensor=1 - half))
+        across[-1].start()
+        local.append(pltpu.make_async_copy(low.at[piece], slot, ls.at[n + 1]))
+        local[-1].start()
+    moves.hop(1)
+    moves.sides(0)
+    moves.hop(2)
+    moves.sides(1)
+    moves.hop(3)
+    moves.sides(2)
+    moves.sides(3)
+    own.wait()
+    for n in range(4):
+        local[n].wait()
+        across[n].wait()
+    moves.finish()
+
+
+def gather_rows(tokens_in, gain, pack, ways, norm, collective_id):
+    rows, width = tokens_in.shape
+    vmem = pl.BlockSpec(memory_space=pltpu.VMEM)
+    hbm = pl.BlockSpec(memory_space=pl.ANY)
+    return pl.pallas_call(
+        functools.partial(gather_kernel, norm=norm),
+        name="gather_rows",
+        in_specs=[vmem, vmem, vmem],
+        out_specs=[hbm, hbm],
+        out_shape=[sds((2 * rows, width), bf16), sds((ways * pack.shape[0], pack.shape[1]), bf16)],
+        scratch_shapes=[
+            pltpu.VMEM((rows, width), bf16),
+            pltpu.SemaphoreType.DMA((16, 4)), pltpu.SemaphoreType.DMA((16,)),
+            pltpu.SemaphoreType.DMA((4,)), pltpu.SemaphoreType.DMA((4,)), pltpu.SemaphoreType.DMA((5,)),
+        ],
+        compiler_params=pltpu.CompilerParams(
+            collective_id=collective_id, has_side_effects=True, vmem_limit_bytes=60 * 1024 * 1024
+        ),
+    )(tokens_in, gain, pack)
+
+
+class Reduce:
+    def __init__(self, here, grads, out, bufs, sems):
+        self.here, self.grads, self.out = here, grads, out
+        self.mine, self.buf_a, self.buf_b, self.buf_up, self.buf_dn = bufs
+        self.local, self.send_a, self.recv_a, self.send_b, self.recv_b, self.send_c, self.recv_up, self.recv_dn = sems
+        self.rows = out.shape[0]
+        z = here.z
+        self.order = (3 * (1 - z // 2), (3 * z + 2) % 5, 1 + z % 2, z)
+
+    def block(self, z, y, c):
+        at = pl.multiple_of(self.here.at(z, y, c) * self.rows, self.rows)
+        return self.grads.at[pl.ds(at, self.rows)]
+
+    def copy_a(self, z, y):
+        here, at = self.here, z * 2 + y
+        return remote(self.block(z, y, 1 - here.c), self.buf_a.at[at], self.send_a.at[at], self.recv_a.at[at], dp=here.core())
+
+    def take(self, z, y):
+        at = z * 2 + y
+        return pltpu.make_async_copy(self.block(z, y, self.here.c), self.mine.at[at], self.local.at[at])
+
+    def copy_b(self, z):
+        here = self.here
+        return remote(self.mine.at[z * 2 + 1 - here.y], self.buf_b.at[z], self.send_b.at[z], self.recv_b.at[z], dp=here.side())
+
+    def copy_up(self, z):
+        return remote(self.mine.at[z * 2 + self.here.y], self.buf_up.at[z], self.send_c.at[z], self.recv_up.at[z], dp=self.here.up())
+
+    def copy_dn(self, z):
+        return remote(self.mine.at[z * 2 + self.here.y], self.buf_dn.at[z], self.send_c.at[z], self.recv_dn.at[z], dp=self.here.down())
+
+    def add(self, at, buf, slot):
+        def rows(n, carry):
+            piece = pl.ds(pl.multiple_of(n * 16, 16), 16)
+            self.mine[at, piece] = (self.mine[at, piece].astype(f32) + buf[slot, piece].astype(f32)).astype(bf16)
+            return carry
+
+        lax.fori_loop(0, self.rows // 16, rows, 0)
+
+    def start(self):
+        here = self.here
+        for side in (1 - here.y, here.y):
+            for z in self.order:
+                self.copy_a(z, side).start()
+                self.take(z, side).start()
+
+    def cores(self, n):
+        here = self.here
+        z = self.order[n]
+        at = z * 2 + 1 - here.y
+        self.take(z, 1 - here.y).wait()
+        self.copy_a(z, 1 - here.y).wait_recv()
+        self.add(at, self.buf_a, at)
+        self.copy_b(z).start()
+
+    def stay(self, n):
+        here = self.here
+        z = self.order[n]
+        at = z * 2 + here.y
+        self.take(z, here.y).wait()
+        self.copy_a(z, here.y).wait_recv()
+        self.add(at, self.buf_a, at)
+
+    def sides(self, n):
+        z = self.order[n]
+        self.copy_b(z).wait_recv()
+        self.add(z * 2 + self.here.y, self.buf_b, z)
+
+    def pass_on(self, n):
+        here = self.here
+        z = self.order[n]
+        at = z * 2 + here.y
+
+        def up():
+            def below():
+                self.copy_up(z).wait_recv()
+                self.add(at, self.buf_up, z)
+
+            pl.when(here.z > 0)(below)
+            self.copy_up(z).start()
+
+        def down():
+            def above():
+                self.copy_dn(z).wait_recv()
+                self.add(at, self.buf_dn, z)
+
+            pl.when(here.z < 3)(above)
+            self.copy_dn(z).start()
+
+        pl.when(z > here.z)(up)
+        pl.when(z < here.z)(down)
+
+    def finish(self):
+        here = self.here
+        z = here.z
+        at = z * 2 + here.y
+        pl.when(z > 0)(lambda: self.copy_up(z).wait_recv())
+        pl.when(z < 3)(lambda: self.copy_dn(z).wait_recv())
+
+        def rows(n, carry):
+            piece = pl.ds(pl.multiple_of(n * 16, 16), 16)
+            below = jnp.where(z > 0, self.buf_up[z, piece].astype(f32), 0.0)
+            above = jnp.where(z < 3, self.buf_dn[z, piece].astype(f32), 0.0)
+            self.out[piece] = self.mine[at, piece].astype(f32) + below + above
+            return carry
+
+        lax.fori_loop(0, self.rows // 16, rows, 0)
+        for n in range(4):
+            zn = self.order[n]
+            self.copy_a(zn, 0).wait_send()
+            self.copy_a(zn, 1).wait_send()
+            self.copy_b(zn).wait_send()
+            pl.when(zn > z)(lambda zn=zn: self.copy_up(zn).wait_send())
+            pl.when(zn < z)(lambda zn=zn: self.copy_dn(zn).wait_send())
+
+    def all(self):
+        self.start()
+        for n in range(4):
+            self.cores(n)
+        for n in range(4):
+            self.stay(n)
+        for n in range(3):
+            self.sides(n)
+            self.pass_on(n)
+        self.sides(3)
+
+
+def reduce_scratch(rows, cols):
+    sem = pltpu.SemaphoreType.DMA
+    return [
+        pltpu.VMEM((8, rows, cols), bf16), pltpu.VMEM((8, rows, cols), bf16), pltpu.VMEM((4, rows, cols), bf16),
+        pltpu.VMEM((4, rows, cols), bf16), pltpu.VMEM((4, rows, cols), bf16),
+        sem((8,)), sem((8,)), sem((8,)), sem((4,)), sem((4,)), sem((4,)), sem((4,)), sem((4,)),
+    ]
+
+
+def reduce_kernel(grads, out, *scratch):
+    here = Place()
+    greet(here, False)
+    work = Reduce(here, grads, out, scratch[:5], scratch[5:])
+    work.all()
+    work.finish()
+
+
+def reduce_small_kernel(grads, small, out, small_out, *scratch):
+    here = Place()
+    far = pltpu.get_barrier_semaphore()
+    partners = [here.me + bit - 2 * bit * ((here.me // bit) % 2) for bit in (1, 2, 4, 8)]
+    for partner in partners:
+        pl.semaphore_signal(far, 1, device_id={"dp": partner}, device_id_type=MESH)
+    middle = (here.z == 1) | (here.z == 2)
+    pl.when(here.z == 1)(lambda: pl.semaphore_signal(far, 1, device_id={"dp": here.up()}, device_id_type=MESH))
+    pl.when(here.z == 2)(lambda: pl.semaphore_signal(far, 1, device_id={"dp": here.down()}, device_id_type=MESH))
+    pl.semaphore_wait(far, 4 + middle.astype(jnp.int32))
+    work = Reduce(here, grads, out, scratch[:5], scratch[5:13])
+    total, landed, send, recv = scratch[13:]
+    total[0] = small[...]
+    for k in range(4):
+        if k == 0:
+            work.start()
+        swap = remote(total.at[k], landed.at[k], send.at[k], recv.at[k], dp=partners[k])
+        swap.start()
+        if k == 0:
+            for n in range(4):
+                work.cores(n)
+            for n in range(4):
+                work.stay(n)
+        else:
+            work.sides(k - 1)
+            work.pass_on(k - 1)
+        swap.wait()
+        total[k + 1] = total[k] + landed[k]
+    small_out[...] = total[4]
+    work.sides(3)
+    work.finish()
+
+
+def reduce_rows(grads, ways, collective_id, small=None):
+    rows, cols = grads.shape[0] // ways, grads.shape[1]
+    vmem = pl.BlockSpec(memory_space=pltpu.VMEM)
+    hbm = pl.BlockSpec(memory_space=pl.ANY)
+    settings = pltpu.CompilerParams(
+        collective_id=collective_id, has_side_effects=True, vmem_limit_bytes=60 * 1024 * 1024
+    )
+    if small is None:
+        return pl.pallas_call(
+            reduce_kernel, name="reduce_rows", in_specs=[hbm], out_specs=vmem, out_shape=sds((rows, cols)),
+            scratch_shapes=reduce_scratch(rows, cols), compiler_params=settings,
+        )(grads)
+    return pl.pallas_call(
+        reduce_small_kernel, name="reduce_rows_small", in_specs=[hbm, vmem], out_specs=[vmem, vmem],
+        out_shape=[sds((rows, cols)), sds(small.shape)],
+        scratch_shapes=reduce_scratch(rows, cols) + [
+            pltpu.VMEM((5,) + small.shape, f32), pltpu.VMEM((4,) + small.shape, f32),
+            pltpu.SemaphoreType.DMA((4,)), pltpu.SemaphoreType.DMA((4,)),
+        ],
+        compiler_params=settings,
+    )(grads, small)
+
+
+def swap(v):
+    return lax.ppermute(v, "tensor", [(0, 1), (1, 0)])
+
+
+def halves(v, axis):
+    size = v.shape[axis] // 2
+    me = lax.axis_index("tensor")
+    return (
+        lax.dynamic_slice_in_dim(v, me * size, size, axis),
+        lax.dynamic_slice_in_dim(v, (1 - me) * size, size, axis),
+    )
 
 
 def once(shape, at=None):
@@ -411,16 +806,18 @@
     heads = w_step.shape[1]
     blocks = units // BW
     unit_total = units * lax.axis_size("tensor")
+    ways = lax.axis_size("dp")
+    own_links = ways == 16
     rows_in = residual.astype(f32)
     rstd_in = lax.rsqrt(jnp.mean(rows_in * rows_in, axis=1, keepdims=True) + norm_eps)
     scaled = rows_in * rstd_in
-    normed_local = (scaled * norm_gain).astype(bf16)
     pack_a = jnp.concatenate([w_gate_inner[1], w_state_io, spread(w_step)], axis=1)
     pack_b = jnp.concatenate([w_gate_inner[0], w_output.T], axis=1)
-    wa = lax.all_gather(pack_a, "dp", axis=0, tiled=True)
-    normed = lax.all_gather(normed_local, "tensor", axis=0, tiled=True)
-    wb = lax.all_gather(pack_b, "dp", axis=0, tiled=True)
-    cot = lax.all_gather(cotangent, "tensor", axis=0, tiled=True)
+    if own_links:
+        normed, wa = gather_rows(residual, norm_gain[None], pack_a, ways, True, 1)
+    else:
+        wa = lax.all_gather(pack_a, "dp", axis=0, tiled=True)
+        normed = lax.all_gather((scaled * norm_gain).astype(bf16), "tensor", axis=0, tiled=True)
     tokens = normed.shape[0]
     spans = tokens // Q
     rate = -jnp.exp(decay_log)
@@ -457,6 +854,12 @@
         cost_estimate=pl.CostEstimate(flops=2 * tokens * width * (units + 384) + 4 * tokens * 256 * units, bytes_accessed=30_000_000, transcendentals=heads * spans * Q * Q),
     )(normed, wa, wa, kin, kst, hp)
 
+    if own_links:
+        cot, wb = gather_rows(cotangent, norm_gain[None], pack_b, ways, False, 2)
+    else:
+        wb = lax.all_gather(pack_b, "dp", axis=0, tiled=True)
+        cot = lax.all_gather(cotangent, "tensor", axis=0, tiled=True)
+
     gate, ggo, stats = pl.pallas_call(
         gate_forward,
         name="gate_forward",
@@ -471,7 +874,7 @@
         compiler_params=params(),
         cost_estimate=pl.CostEstimate(flops=4 * tokens * width * units, bytes_accessed=35_000_000, transcendentals=tokens * units),
     )(normed, cot, wb, wb, ssd, gain8)
-    stats = lax.psum(stats, "tensor")
+    stats = stats + swap(stats)
 
     dy, dgate, ng, ggg = pl.pallas_call(
         functools.partial(gate_backward, float(unit_total)),
@@ -487,10 +890,13 @@
 
     grad_wo = mm(cot, ng, 0, 0).astype(bf16)
     grad_wg = mm(normed, dgate, 0, 0).astype(bf16)
-    wo_shard = lax.psum_scatter(grad_wo, "dp", scatter_dimension=0, tiled=True)
-    wg_shard = lax.psum_scatter(grad_wg, "dp", scatter_dimension=0, tiled=True)
-    mixed = lax.psum_scatter(mm(ng, wb[:, units:], 1, 1).astype(bf16), "tensor", scatter_dimension=0, tiled=True)
-    output = (rows_in + mixed.astype(f32)).astype(bf16)
+    grad_b = jnp.concatenate([grad_wg, grad_wo], axis=1)
+    if own_links:
+        wb_shard = reduce_rows(grad_b, ways, 3)
+    else:
+        wb_shard = lax.psum_scatter(grad_b, "dp", scatter_dimension=0, tiled=True).astype(f32)
+    mixed, mixed_far = halves(mm(ng, wb[:, units:], 1, 1).astype(bf16), 0)
+    output = (rows_in + mixed.astype(f32) + swap(mixed_far).astype(f32)).astype(bf16)
 
     dinner, gk, dsd, gks, hs = pl.pallas_call(
         mixer_backward,
@@ -520,49 +926,54 @@
 
     grad_wi = mm(normed, dinner, 0, 0).astype(bf16)
     grad_ws = mm(normed, dsd, 0, 0).astype(bf16)
-    wa_shard = lax.psum_scatter(jnp.concatenate([grad_wi, grad_ws], axis=1), "dp", scatter_dimension=0, tiled=True)
-    grad_normed = (
-        mm(dgate, wb[:, :units], 1, 1) + mm(dinner, wa[:, :units], 1, 1) + mm(dsd, wa[:, units:], 1, 1)
-    ).astype(bf16)
-    grad_normed = lax.psum_scatter(grad_normed, "tensor", scatter_dimension=0, tiled=True).astype(f32)
+    grad_a = jnp.concatenate([grad_wi, grad_ws], axis=1)
+    tail = jnp.concatenate([gks[:5].reshape(-1), hs[:, 0], hs[:, 1], jnp.zeros((units - 5 * BW - 96,), f32)])
+    small = jnp.concatenate([gk[:6], ggg[:1], tail[None]], axis=0)
+    if own_links:
+        wa_shard, small = reduce_rows(grad_a, ways, 4, small)
+    else:
+        wa_shard = lax.psum_scatter(grad_a, "dp", scatter_dimension=0, tiled=True).astype(f32)
+        small = lax.psum(small, "dp")
+    near, far = halves(
+        (mm(dgate, wb[:, :units], 1, 1) + mm(dinner, wa[:, :units], 1, 1) + mm(dsd, wa[:, units:], 1, 1)).astype(bf16),
+        0,
+    )
+    grad_normed = near.astype(f32) + swap(far).astype(f32)
     grad_v = grad_normed * norm_gain
     grad_residual = cotangent.astype(f32) + rstd_in * (
         grad_v - scaled * jnp.mean(grad_v * scaled, axis=1, keepdims=True)
     )
 
-    small = jnp.concatenate([gk, ggg, jnp.pad(gks, ((0, 0), (0, units - BW)))], axis=0)
-    small = jnp.concatenate([small.reshape(-1), hs[:, 0], hs[:, 1]])
-    small = lax.psum(small, "dp")
-    table = small[: 24 * units].reshape(24, units)
-    bias_sum = gathered_heads(small[24 * units : 24 * units + 48], heads)
-    decay_sum = gathered_heads(small[24 * units + 48 : 24 * units + 96], heads)
-    skip_sum = jnp.sum(table[5].reshape(heads, HEAD), axis=1)
-
-    wg_f, wa_f, wo_f = wg_shard.astype(f32), wa_shard.astype(f32), wo_shard.astype(f32)
-    gain_rows = jnp.sum(wg_f * w_gate_inner[0].astype(f32), axis=1) + jnp.sum(wa_f * pack_a.astype(f32), axis=1)
-    gain_own = gain_rows / lax.dynamic_slice_in_dim(
-        norm_gain, lax.axis_index("dp") * gain_rows.shape[0], gain_rows.shape[0]
+    conv_state_sum = small[7, : 5 * BW].reshape(5, BW)
+    bias_sum = gathered_heads(small[7, 5 * BW : 5 * BW + 48], heads)
+    decay_sum = gathered_heads(small[7, 5 * BW + 48 : 5 * BW + 96], heads)
+    skip_sum = jnp.sum(small[5].reshape(heads, HEAD), axis=1)
+
+    gain_rows = jnp.sum(wb_shard[:, :units] * w_gate_inner[0].astype(f32), axis=1) + jnp.sum(
+        wa_shard * pack_a.astype(f32), axis=1
     )
-    state_own = wa_f[:, units : units + BW]
-    conv_state_part, state_part, gain_part = (
-        lax.psum_scatter(table[16:21, :BW], "tensor", scatter_dimension=1, tiled=True),
-        lax.psum_scatter(state_own, "tensor", scatter_dimension=1, tiled=True),
-        lax.psum_scatter(gain_own, "tensor", scatter_dimension=0, tiled=True),
-    )
+    count = gain_rows.shape[0]
+    gain_own = gain_rows / lax.dynamic_slice_in_dim(norm_gain, lax.axis_index("dp") * count, count)
+    near_s, far_s = halves(jnp.concatenate([wa_shard[:, units : units + BW], conv_state_sum], axis=0), 1)
+    near_g, far_g = halves(gain_own, 0)
+    far_all = jnp.concatenate([far_s.reshape(-1), far_g])
+    got = swap(far_all)
+    both = near_s + got[: far_s.size].reshape(far_s.shape)
+    gain_part = near_g + got[far_s.size :]
     return (
         output,
         grad_residual,
         gain_part,
-        jnp.stack([wg_f, wa_f[:, :units]]),
-        state_part,
-        gathered_heads(wa_f[:, units + BW :], heads),
-        table[0:5],
-        conv_state_part,
+        jnp.stack([wb_shard[:, :units], wa_shard[:, :units]]),
+        both[:count],
+        gathered_heads(wa_shard[:, units + BW :], heads),
+        small[0:5],
+        both[count:],
         bias_sum,
         decay_sum,
         skip_sum,
-        table[8],
-        wo_f.T,
+        small[6],
+        wb_shard[:, units:].T,
     )
 
 

time: 821 us -> 552 us (0.67)
  waiting for transfers between devices: 543 us -> 62 us
  Pallas kernels: 136 us -> 366 us
  blocking collectives: 14.5 us -> 0 us
  between operations: 15.3 us -> 1.43 us
    reduce_scatter x6 -> x0, waiting for transfers between devices: 253 us -> none  [the longest x1 83.2 us: on_device(): lax.psum_scatter(jnp.concatenate([grad_wi, grad_ws], axis=1), 'dp', scatt...]
    pallas_call x0 -> x4, Pallas kernels: none -> 230 us  [the longest x2 105 us: gather_rows(): pl.pallas_call(functools.partial(gather_kernel, norm=norm), name='gather_...]
    all_gather x4 -> x0, waiting for transfers between devices: 198 us -> none  [the longest x1 83.6 us: on_device(): wb = lax.all_gather(pack_b, 'dp', axis=0, tiled=True)]
    unnamed x13 -> x0, waiting for transfers between devices: 75 us -> none
    ppermute x0 -> x4, waiting for transfers between devices: none -> 62 us  [swap(): return lax.ppermute(v, 'tensor', [(0, 1), (1, 0)])]
    psum x1 -> x0, waiting for transfers between devices: 17.1 us -> none  [on_device(): small = lax.psum(small, 'dp')]
    psum x1 -> x0, blocking collectives: 9.55 us -> none  [on_device(): stats = lax.psum(stats, 'tensor')]
    unnamed x49 -> x43, local copies, waits for them, and re-layouts: 10.8 us -> 1.44 us
  transfers between devices with their start and end apart: 12 -> 4, of which waited for: 11 -> 2; matrix products, arithmetic and copies ran while one was open for 12% -> 2% of each run, Pallas kernels for 4% -> 0%
where the time goes in v2:
time: 552 us; the launch traced here: 543 us
  Pallas kernels  366 us (66%)
  waiting for transfers between devices  62 us (11%)
  matrix products  57.7 us (10%)
  other arithmetic  30.8 us (6%)
  local copies, waits for them, and re-layouts  19.4 us (4%)
  starting transfers between devices  5.78 us (1%)
    pallas_call x2, Pallas kernels, gather_rows(): pl.pallas_call(functools.partial(gather_kernel, norm=norm), name='gather_...  105 us
    pallas_call x1, Pallas kernels, on_device(): pl.pallas_call(mixer_backward, name='mixer_backward', grid=(blocks,), in_...  68.3 us
    pallas_call x1, Pallas kernels, reduce_rows(): pl.pallas_call(reduce_kernel, name='reduce_rows', in_specs=[hbm], out_spe...  67.1 us
    ppermute x4, waiting for transfers between devices, swap(): return lax.ppermute(v, 'tensor', [(0, 1), (1, 0)])  62 us
    dot_general x8, matrix products, mm(): lax.dot_general(a, b, (((ca,), (cb,)), ((), ())), preferred_element_type=...  57.7 us
    pallas_call x1, Pallas kernels, reduce_rows(): pl.pallas_call(reduce_small_kernel, name='reduce_rows_small', in_specs=[h...  57.5 us
    pallas_call x1, Pallas kernels, on_device(): pl.pallas_call(mixer_forward, name='mixer_forward', grid=(blocks,), in_sp...  35.1 us
    pallas_call x1, Pallas kernels, on_device(): pl.pallas_call(gate_forward, name='gate_forward', grid=(blocks,), in_spec...  19.1 us
  transfers between devices with their start and end apart: 4, of which 2 were waited for; matrix products, arithmetic and copies ran while one was open for 2% of the time, Pallas kernels for 0%

profile of v2, /device:TPU:0, one launch (start us, length us, event | category | flops | bytes accessed | tf_op | source)
XLA Modules:
  0.0 543.1 jit_solution(4648586047604952501)
XLA Ops:
  0.6 1.1 slice_bitcast_fusion.3
  1.8 0.7 pad_bitcast_fusion
  2.6 1.3 broadcast_in_dim.20.gain
  3.9 0.7 exponential_negate_fusion
  4.7 0.7 reshape.85
  5.5 0.7 broadcast_in_dim.42
  6.5 1.3 concatenate.36.kst
  7.8 1.8 pad_maximum_fusion.3.pack
  9.6 1.6 fusion.23.pack
  11.2 44.0 %gather_rows.2 = (bf16[1024,1536]{1,0:T(8,128)(2,1)}, bf16[1536,1920]{1,0:T(8,128)(2,1)}) custom-call(bf16[512,1536]{1,0:T(8,128)(2,1)} %tokens_in.2, f32[1,1536]{1,0:T(1,128)} %broadcast_in_dim.20.gain, bf16[96,1920]{1,0:T(8,128)(2,1)} %fusion.23.pack), custom_call_target="tpu_custom_call" | custom-call | tf_op jit(solution)/shard_map/gather_rows/pallas_call | solution.py:542
  55.2 61.0 %gather_rows.3 = (bf16[1024,1536]{1,0:T(8,128)(2,1)}, bf16[1536,3072]{1,0:T(8,128)(2,1)}) custom-call(bf16[512,1536]{1,0:T(8,128)(2,1)} %tokens_in.3, f32[1,1536]{1,0:T(1,128)} %broadcast_in_dim.20.gain, bf16[96,3072]{1,0:T(8,128)(2,1)} %pad_maximum_fusion.3.pack), custom_call_target="tpu_custom_call" | custom-call | tf_op jit(solution)/shard_map/gather_rows/pallas_call | solution.py:542
  116.2 0.7 maximum_maximum_fusion.1.hp
  116.8 0.7 maximum_maximum_fusion.kin
  117.5 35.1 %mixer_forward.1 = (f32[1024,1536]{1,0:T(8,128)}, f32[1024,1536]{1,0:T(8,128)}, f32[4,1536,128]{2,1,0:T(8,128)}, f32[1024,256]{1,0:T(8,128)}, bf16[1024,256]{1,0...) custom-call(bf16[1024,1536]{1,0:T(8,128)(2,1)} %get-tuple-element.41, ...), custom_call_target="tpu_custom_call" | custom-call | flops 7650410496 | bytes 30000000 | tf_op jit(solution)/shard_map/mixer_forward/pallas_call | solution.py:830
  153.3 19.1 %gate_forward.1 = (f32[1024,1536]{1,0:T(8,128)}, f32[1024,1536]{1,0:T(8,128)}, f32[8,1024]{1,0:T(8,128)}) custom-call(bf16[1024,1536]{1,0:T(8,128)(2,1)} %get-tuple-element.41.normed, bf16[1024,1536]{1,0:T(8,128)(2,1)} %get-tuple-element.42.cot, bf16[1536,3072]{1,0:T(8,128)(2,1)} %get-tuple-element.43.wg.wo, bf16[1536,3072]{1,0:T(8,128)(2,1)} %get-tuple-element.43.wg.wo, ...), custom_call_target="tpu_custom_call" | custom-call | flops 9663676416 | bytes 35000000 | tf_op jit(solution)/shard_map/gate_forward/pallas_call | solution.py:863
  172.3 2.1 collective-permute-start
  174.8 1.8 collective-permute-done
  176.6 1.4 add.78.stats
  178.0 14.0 %gate_backward.1 = (bf16[1024,1536]{1,0:T(8,128)(2,1)}, bf16[1024,1536]{1,0:T(8,128)(2,1)}, bf16[1024,1536]{1,0:T(8,128)(2,1)}, f32[8,1536]{1,0:T(8,128)}) custom-call(f32[8,1024]{1,0:T(8,128)} %add.78.stats, f32[1024,1536]{1,0:T(8,128)} %get-tuple-element.47.gate, f32[1024,1536]{1,0:T(8,128)} %get-tuple-element.45.ssd, f32[1024,1536]{1,0:T(8,128)} %get-tuple-element.48.ggo, ...), custom_call_target="tpu_custom_call" | custom-call | flops 31457280 | bytes 30000000 | tf_op jit(solution)/shard_map/gate_backward/pallas_call | solution.py:879
  192.0 0.7 broadcast_in_dim.48.rateT
  192.7 68.3 %mixer_backward.1 = (bf16[1024,1536]{1,0:T(8,128)(2,1)}, f32[8,1536]{1,0:T(8,128)}, bf16[1024,384]{1,0:T(8,128)(2,1)}, f32[8,256]{1,0:T(8,128)}, f32[48,128]{1,0:T(8,128)}) custom-call(f32[1024,1536]{1,0:T(8,128)} %get-tuple-element.51.inner, bf16[1024,1536]{1,0:T(8,128)(2,1)} %get-tuple-element.52.dy, f32[4,1536,128]{2,1,0:T(8,128)} %get-tuple-element.53.states, ...), custom_call_target="tpu_custom_call" | custom-call | flops 40000000000 | bytes 30000000 | tf_op jit(solution)/shard_map/mixer_backward/pallas_call | solution.py:901
  260.9 0.7 reshape.89
  261.6 1.0 slice_reduce_fusion
  262.7 0.8 slice.100
  263.5 7.9 %convolution_convert_fusion = bf16[1536,1536]{1,0:T(8,128)(2,1)S(1)} fusion(bf16[1024,1536]{1,0:T(8,128)(2,1)} %get-tuple-element.41.normed, bf16[1024,1536]{1,0:T(8,128)(2,1)} %get-tuple-element.61), kind=kOutput, calls=%fused_computation.1 | convolution fusion | flops 4834197504 | bytes 11010048 | tf_op jit(solution)/shard_map/dot_general | solution.py:24
  271.5 1.8 convolution_convert_fusion.3
  273.3 3.0 pad_maximum_fusion.1.grads
  277.0 57.5 %reduce_rows_small.1 = (f32[96,1920]{1,0:T(8,128)}, f32[8,1536]{1,0:T(8,128)}) custom-call(bf16[1536,1920]{1,0:T(8,128)(2,1)} %pad_maximum_fusion.1.grads, f32[8,1536]{1,0:T(8,128)} %pad_maximum_fusion.5.small), custom_call_target="tpu_custom_call" | custom-call | tf_op jit(solution)/shard_map/reduce_rows_small/pallas_call | solution.py:748
  334.5 0.9 slice.104
  335.4 1.3 multiply_reduce_fusion
  336.7 9.9 %fusion = f32[1024,1536]{1,0:T(8,128)} fusion(bf16[1024,1536]{1,0:T(8,128)(2,1)} %get-tuple-element.61, bf16[1536,1920]{1,0:T(8,128)(2,1)} %get-tuple-element.44.wi.wsx), kind=kOutput, calls=%fused_computation.9 | convolution fusion | flops 4831838208 | bytes 14155776 | tf_op jit(solution)/shard_map/dot_general | solution.py:24
  346.6 5.9 %fusion.20 = f32[1024,1536]{1,0:T(8,128)} fusion(bf16[1024,384]{1,0:T(8,128)(2,1)S(1)} %copy-done.8, bf16[1536,1920]{1,0:T(8,128)(2,1)} %get-tuple-element.44.wi.wsx), kind=kOutput, calls=%fused_computation.28 | convolution fusion | flops 1207959552 | bytes 8257536 | tf_op jit(solution)/shard_map/dot_general | solution.py:24
  352.5 6.8 %convolution_convert_fusion.1 = bf16[1536,1536]{1,0:T(8,128)(2,1)} fusion(bf16[1024,1536]{1,0:T(8,128)(2,1)S(1)} %copy-done.16, bf16[1024,1536]{1,0:T(8,128)(2,1)S(1)} %copy-done.17), kind=kOutput, calls=%fused_computation.2 | convolution fusion | flops 4834197504 | bytes 11010048 | tf_op jit(solution)/shard_map/dot_general | solution.py:24
  359.4 6.5 %fusion.6 = bf16[1024,1536]{1,0:T(8,128)(2,1)} fusion(bf16[1024,1536]{1,0:T(8,128)(2,1)S(1)} %copy-done.17, bf16[1536,3072]{1,0:T(8,128)(2,1)S(1)} %bitcast.55), kind=kOutput, calls=%fused_computation.15 | convolution fusion | flops 4833411072 | bytes 11010048 | tf_op jit(solution)/shard_map/dot_general | solution.py:24
  366.0 7.9 %convolution_convert_fusion.2 = bf16[1536,1536]{1,0:T(8,128)(2,1)S(1)} fusion(bf16[1024,1536]{1,0:T(8,128)(2,1)} %get-tuple-element.41.normed, bf16[1024,1536]{1,0:T(8,128)(2,1)} %get-tuple-element.50), kind=kOutput, calls=%fused_computation.3 | convolution fusion | flops 4834197504 | bytes 11010048 | tf_op jit(solution)/shard_map/dot_general | solution.py:24
  373.9 4.8 pad_maximum_fusion.grads
  378.7 67.1 %reduce_rows.1 = f32[96,3072]{1,0:T(8,128)} custom-call(bf16[1536,3072]{1,0:T(8,128)(2,1)} %pad_maximum_fusion.grads), custom_call_target="tpu_custom_call" | custom-call | tf_op jit(solution)/shard_map/reduce_rows/pallas_call | solution.py:744
  445.8 2.2 slice_bitcast_fusion
  448.0 10.9 %add_convert_fusion = bf16[1024,1536]{1,0:T(8,128)(2,1)S(1)} fusion(f32[1024,1536]{1,0:T(8,128)} %fusion.20, f32[1024,1536]{1,0:T(8,128)} %fusion, bf16[1024,1536]{1,0:T(8,128)(2,1)} %get-tuple-element.50, bf16[1536,3072]{1,0:T(8,128)(2,1)} %get-tuple-element.43.wg.wo), kind=kOutput, calls=%fused_computation.4 | convolution fusion | flops 4836556800 | bytes 23592960 | tf_op jit(solution)/shard_map/dot_general | solution.py:24
  459.0 1.3 constant_dynamic-slice_fusion
  460.3 1.6 collective-permute-start.2
  461.8 0.7 copy-done.5
  462.6 1.3 constant_dynamic-slice_fusion.1
  463.8 1.6 collective-permute-start.1
  466.8 1.1 pad_maximum_fusion.2
  470.7 60.2 %collective-permute-done.3 = f32[12976]{0:T(1024)S(1)} collective-permute-done((f32[12976]{0:T(1024)S(1)}, f32[12976]{0:T(1024)S(1)}, u32[]{:S(2)}, u32[]{:S(2)}) %collective-permute-start.3) | collective-permute-done | bytes 51936 | tf_op jit(solution)/shard_map/ppermute | solution.py:760
  532.7 2.8 fusion.13
  535.6 6.5 %fusion.16 = (f32[512,1536]{1,0:T(8,128)}, bf16[512,1536]{1,0:T(8,128)(2,1)}) fusion(bf16[512,1536]{1,0:T(8,128)(2,1)S(1)} %copy-done, bf16[512,1536]{1,0:T(8,128)(2,1)S(1)} %copy-done.3, bf16[512,1536]{1,0:T(8,128)(2,1)} %collective-permute-done.2, f32[512]{0:T(512)S(1)} %broadcast_multiply_fusion, f32[1536]{0:T(1024)S(1)} %copy-done.11, ...), kind=kLoop, calls=%fused_computation.21 | loop fusion | flops 12582912 | bytes 14166020 | tf_op jit(solution)/shard_map/add | solution.py:943
  (88 shorter events, 9.1 us)
Async XLA Ops:
  1.7 115.1 %copy-start.13 = (f32[5,1536]{1,0:T(8,128)S(1)}, f32[5,1536]{1,0:T(8,128)}, u32[]{:S(2)}) copy-start(f32[5,1536]{1,0:T(8,128)} %param.18) | copy-start | bytes 92164
  117.5 35.1 %copy-start.14 = (f32[1536]{0:T(1024)S(1)}, f32[1536]{0:T(1024)}, u32[]{:S(2)}) copy-start(f32[1536]{0:T(1024)} %param.23) | copy-start | bytes 18436
  153.3 21.2 %copy-start = (bf16[512,1536]{1,0:T(8,128)(2,1)S(1)}, bf16[512,1536]{1,0:T(8,128)(2,1)}, u32[]{:S(2)}) copy-start(bf16[512,1536]{1,0:T(8,128)(2,1)} %tokens_in.2) | copy-start | bytes 4718596
  172.3 4.3 collective-permute-start
  263.5 7.9 %copy-start.8 = (bf16[1024,384]{1,0:T(8,128)(2,1)S(1)}, bf16[1024,384]{1,0:T(8,128)(2,1)}, u32[]{:S(2)}) copy-start(bf16[1024,384]{1,0:T(8,128)(2,1)} %get-tuple-element.62) | copy-start | bytes 2359300
  263.5 7.9 %copy-start.15 = (bf16[1024,1536]{1,0:T(8,128)(2,1)S(1)}, bf16[1024,1536]{1,0:T(8,128)(2,1)}, u32[]{:S(2)}) copy-start(bf16[1024,1536]{1,0:T(8,128)(2,1)} %get-tuple-element.41.normed) | copy-start | bytes 9437188
  273.3 3.0 copy-start.12
  276.3 59.1 %copy-start.9 = (bf16[96,256]{1,0:T(8,128)(2,1)S(1)}, bf16[96,256]{1,0:T(8,128)(2,1)}, u32[]{:S(2)}) copy-start(bf16[96,256]{1,0:T(8,128)(2,1)} %param.16) | copy-start | bytes 147460
  336.7 15.9 %copy-start.17 = (bf16[1024,1536]{1,0:T(8,128)(2,1)S(1)}, bf16[1024,1536]{1,0:T(8,128)(2,1)}, u32[]{:S(2)}) copy-start(bf16[1024,1536]{1,0:T(8,128)(2,1)} %get-tuple-element.49) | copy-start | bytes 9437188
  346.6 6.0 %copy-start.16 = (bf16[1024,1536]{1,0:T(8,128)(2,1)S(1)}, bf16[1024,1536]{1,0:T(8,128)(2,1)}, u32[]{:S(2)}) copy-start(bf16[1024,1536]{1,0:T(8,128)(2,1)} %get-tuple-element.42.cot) | copy-start | bytes 9437188
  346.6 12.8 %slice-start = ((s8[9437184]{0:T(1024)(128)(4,1)}), s8[4194304]{0:T(1024)(128)(4,1)S(1)}, s32[]{:S(2)}) async-start(s8[9437184]{0:T(1024)(128)(4,1)} %bitcast.54), calls=%async_computation | async-start | bytes 8388608
  352.5 6.8 %slice-start.1 = ((s8[9437184]{0:T(1024)(128)(4,1)}), s8[4194304]{0:T(1024)(128)(4,1)S(1)}, s32[]{:S(2)}) async-start(s8[9437184]{0:T(1024)(128)(4,1)} %bitcast.54), calls=%async_computation.1 | async-start | bytes 8388608
  352.5 6.8 %slice-start.2 = ((s8[9437184]{0:T(1024)(128)(4,1)}), s8[1048576]{0:T(1024)(128)(4,1)S(1)}, s32[]{:S(2)}) async-start(s8[9437184]{0:T(1024)(128)(4,1)} %bitcast.54), calls=%async_computation.2 | async-start | bytes 2097152
  359.4 6.5 %copy-start.10 = (f32[8,1536]{1,0:T(8,128)S(1)}, f32[8,1536]{1,0:T(8,128)}, u32[]{:S(2)}) copy-start(f32[8,1536]{1,0:T(8,128)} %get-tuple-element.68) | copy-start | bytes 147460
  366.0 7.9 %copy-start.4 = (bf16[1536,1536]{1,0:T(8,128)(2,1)S(1)}, bf16[1536,1536]{1,0:T(8,128)(2,1)}, u32[]{:S(2)}) copy-start(bf16[1536,1536]{1,0:T(8,128)(2,1)} %convolution_convert_fusion.1) | copy-start | bytes 14155780
  378.7 67.1 %copy-start.7 = (bf16[2,96,1536]{2,1,0:T(8,128)(2,1)S(1)}, bf16[2,96,1536]{2,1,0:T(8,128)(2,1)}, u32[]{:S(2)}) copy-start(bf16[2,96,1536]{2,1,0:T(8,128)(2,1)} %param.15) | copy-start | bytes 1769476
  459.0 4.9 copy-start.1
  459.0 3.6 copy-start.5
  459.0 6.4 %copy-start.11 = (f32[1536]{0:T(1024)S(1)}, f32[1536]{0:T(1024)}, u32[]{:S(2)}) copy-start(f32[1536]{0:T(1024)} %param.14) | copy-start | bytes 18436
  459.0 6.6 %copy-start.6 = (f32[96,1920]{1,0:T(8,128)S(1)}, f32[96,1920]{1,0:T(8,128)}, u32[]{:S(2)}) copy-start(f32[96,1920]{1,0:T(8,128)} %get-tuple-element.67) | copy-start | bytes 2211844
  460.3 72.5 %collective-permute-start.2 = (bf16[512,1536]{1,0:T(8,128)(2,1)}, bf16[512,1536]{1,0:T(8,128)(2,1)}, u32[]{:S(2)}, u32[]{:S(2)}) collective-permute-start(bf16[512,1536]{1,0:T(8,128)(2,1)} %constant_dynamic-slice_fusion), channel_id=1, source_target_pairs={{0,1},{1,0},{2,3},{3,2},{4,5},{5,4},{6,7},{7,6},{8,9},{9,8},{10,11... | collective-permute-start | bytes 4718600 | tf_op jit(solution)/shard_map/ppermute | solution.py:760
  463.8 71.7 %collective-permute-start.1 = (bf16[512,1536]{1,0:T(8,128)(2,1)}, bf16[512,1536]{1,0:T(8,128)(2,1)}, u32[]{:S(2)}, u32[]{:S(2)}) collective-permute-start(bf16[512,1536]{1,0:T(8,128)(2,1)} %constant_dynamic-slice_fusion.1), channel_id=1, source_target_pairs={{0,1},{1,0},{2,3},{3,2},{4,5},{5,4},{6,7},{7,6},{8,9},{9,8},{10,11... | collective-permute-start | bytes 4718600 | tf_op jit(solution)/shard_map/ppermute | solution.py:760
  465.6 65.3 %collective-permute-start.3 = (f32[12976]{0:T(1024)S(1)}, f32[12976]{0:T(1024)S(1)}, u32[]{:S(2)}, u32[]{:S(2)}) collective-permute-start(f32[12976]{0:T(1024)S(1)} %pad_maximum_fusion.4), channel_id=1, source_target_pairs={{0,1},{1,0},{2,3},{3,2},{4,5},{5,4},{6,7},{7,6},{8,9},{9,8},{10,11... | collective-permute-start | bytes 155720 | tf_op jit(solution)/shard_map/ppermute | solution.py:760
  467.9 67.7 %copy-start.3 = (bf16[512,1536]{1,0:T(8,128)(2,1)S(1)}, bf16[512,1536]{1,0:T(8,128)(2,1)}, u32[]{:S(2)}) copy-start(bf16[512,1536]{1,0:T(8,128)(2,1)} %tokens_in.3) | copy-start | bytes 4718596
  470.7 64.9 %copy-start.2 = (bf16[1024,1536]{1,0:T(8,128)(2,1)S(1)}, bf16[1024,1536]{1,0:T(8,128)(2,1)}, u32[]{:S(2)}) copy-start(bf16[1024,1536]{1,0:T(8,128)(2,1)} %copy-done.1) | copy-start | bytes 9437188

commit v3 on v2

--- a/solution.py
+++ b/solution.py
@@ -81,14 +81,21 @@
     return jnp.exp2(gap)
 
 
-def mixer_forward(
-    normed, wi, wsx, kin, kst, hp,
-    inner_out, ssd_out, states_out, cst_out, bc_out, step_out, cum_out, stepT_out, cumT_out, preT_out,
-    buf, gram, colc, cols, rowp, mst, xst, state,
-):
+def mixer_forward(links, normed, wi, wsx, kin, kst, hp, *refs):
+    refs = list(refs)
+    if links:
+        cot, pack = refs[:2]
+        cot_out, wb = refs[12:14]
+        refs = refs[2:12] + refs[14:]
+    inner_out, ssd_out, states_out, cst_out, bc_out, step_out, cum_out, stepT_out, cumT_out, preT_out = refs[:10]
+    buf, gram, colc, cols, rowp, mst, xst, state = refs[10:18]
     i = pl.program_id(0)
     tokens = normed.shape[0]
     spans = tokens // Q
+    work = BesideForward(cot, pack, cot_out, wb, *refs[18:]) if links else None
+
+    if links:
+        pl.when(i == 0)(work.start)
 
     @pl.when(i == 0)
     def _():
@@ -153,9 +160,54 @@
         for j in range(HB):
             at_j = slice(j * HEAD, j * HEAD + HEAD)
             state[at_j] = fade[:, j : j + 1] * state_in[at_j] + local[at_j]
+        if links:
+            work.step(i * spans + s)
         return carry
 
     lax.fori_loop(0, spans, span, 0)
+    if links:
+        pl.when(i == pl.num_programs(0) - 1)(work.finish)
+
+
+class BesideForward:
+    def __init__(self, cot, pack, cot_out, wb, ss, rs, xs, xr, ls):
+        self.here = Place()
+        self.moves = gathers(self.here, pack, wb, ss, rs)
+        self.own = own_rows(self.here, pack, wb, ls.at[0])
+        half = lax.axis_index("tensor")
+        rows = cot.shape[0]
+        slot = cot_out.at[pl.ds(pl.multiple_of(half * rows, rows), rows)]
+        self.across = remote(cot, slot, xs, xr, tensor=1 - half)
+        self.local = pltpu.make_async_copy(cot, slot, ls.at[1])
+
+    def start(self):
+        greet(self.here, True)
+        for move in self.moves:
+            move.start()
+        self.across.start()
+        self.own.start()
+        self.local.start()
+
+    def step(self, at):
+        for when, chunk, hops in ((7, 0, 1), (11, 1, 1), (15, 0, 2), (19, 1, 2)):
+
+            def go(move=self.moves[chunk], hops=hops):
+                move.hop(hops)
+                move.sides(hops - 1)
+
+            pl.when(at == when)(go)
+
+    def finish(self):
+        for hops in (3, 4):
+            for move in self.moves:
+                if hops < 4:
+                    move.hop(hops)
+                move.sides(hops - 1)
+        self.own.wait()
+        self.local.wait()
+        self.across.wait()
+        for move in self.moves:
+            move.finish()
 
 
 def gate_forward(normed, cot, wg, wo, ssd, gain, gate_out, ggo_out, stats_out, sq, gi):
@@ -416,18 +468,20 @@
 
 
 class Gather:
-    def __init__(self, here, own, full, ss, rs):
-        self.here, self.own, self.full, self.ss, self.rs = here, own, full, ss, rs
-        self.rows = own.shape[0]
+    def __init__(self, here, pack, full, ss, rs, chunk, cols):
+        self.here, self.full, self.ss, self.rs, self.chunk, self.cols = here, full, ss, rs, chunk, cols
+        self.rows = pack.shape[0]
+        self.own = pack.at[:, cols]
 
     def slot(self, origin):
-        return self.full.at[pl.ds(pl.multiple_of(origin * self.rows, self.rows), self.rows)]
+        return self.full.at[pl.ds(pl.multiple_of(origin * self.rows, self.rows), self.rows), self.cols]
 
     def copy(self, origin, way, src=None):
         here = self.here
         target = (here.up, here.down, here.side, here.core)[way]()
         slot = self.slot(origin)
-        return remote(slot if src is None else src, slot, self.ss.at[origin, way], self.rs.at[origin], dp=target)
+        sems = self.ss.at[self.chunk, origin, way], self.rs.at[self.chunk, origin]
+        return remote(slot if src is None else src, slot, *sems, dp=target)
 
     def arrived(self, origin):
         self.copy(origin, 3).wait_recv()
@@ -497,57 +551,69 @@
             self.copy(here.at(z, 1 - here.y, here.c), 3).wait_send()
 
 
-def gather_kernel(tokens_in, gain, pack, tokens_out, full, low, ss, rs, xs, xr, ls, norm):
+def gathers(here, pack, full, ss, rs):
+    cols = pack.shape[1]
+    cut = cols // 256 * 128
+    return [Gather(here, pack, full, ss, rs, n, c) for n, c in enumerate((slice(0, cut), slice(cut, cols)))]
+
+
+def own_rows(here, pack, full, sem):
+    rows = pack.shape[0]
+    return pltpu.make_async_copy(pack, full.at[pl.ds(pl.multiple_of(here.me * rows, rows), rows)], sem)
+
+
+def gather_scratch():
+    sem = pltpu.SemaphoreType.DMA
+    return [sem((2, 16, 4)), sem((2, 16))]
+
+
+def gather_kernel(tokens_in, gain, pack, tokens_out, full, low, ss, rs, xs, xr, ls):
     here = Place()
     half = lax.axis_index("tensor")
     rows = tokens_in.shape[0]
     greet(here, True)
-    moves = Gather(here, pack, full, ss, rs)
-    moves.start()
-    own = pltpu.make_async_copy(pack, moves.slot(here.me), ls.at[0])
+    moves = gathers(here, pack, full, ss, rs)
+    for move in moves:
+        move.start()
+    own = own_rows(here, pack, full, ls.at[0])
     own.start()
     part = rows // 4
     across, local = [], []
     for n in range(4):
         piece = slice(n * part, n * part + part)
-        if norm:
-            v = tokens_in[piece].astype(f32)
-            scale = lax.rsqrt(jnp.mean(v * v, axis=1, keepdims=True) + norm_eps)
-            low[piece] = (v * scale * gain[...]).astype(bf16)
-        else:
-            low[piece] = tokens_in[piece]
+        v = tokens_in[piece].astype(f32)
+        scale = lax.rsqrt(jnp.mean(v * v, axis=1, keepdims=True) + norm_eps)
+        low[piece] = (v * scale * gain[...]).astype(bf16)
         slot = tokens_out.at[pl.ds(pl.multiple_of(half * rows + n * part, part), part)]
         across.append(remote(low.at[piece], slot, xs.at[n], xr.at[n], tensor=1 - half))
         across[-1].start()
         local.append(pltpu.make_async_copy(low.at[piece], slot, ls.at[n + 1]))
         local[-1].start()
-    moves.hop(1)
-    moves.sides(0)
-    moves.hop(2)
-    moves.sides(1)
-    moves.hop(3)
-    moves.sides(2)
-    moves.sides(3)
+    for hops in range(1, 5):
+        for move in moves:
+            if hops < 4:
+                move.hop(hops)
+            move.sides(hops - 1)
     own.wait()
     for n in range(4):
         local[n].wait()
         across[n].wait()
-    moves.finish()
-
-
-def gather_rows(tokens_in, gain, pack, ways, norm, collective_id):
+    for move in moves:
+        move.finish()
+
+
+def gather_rows(tokens_in, gain, pack, ways, collective_id):
     rows, width = tokens_in.shape
     vmem = pl.BlockSpec(memory_space=pltpu.VMEM)
     hbm = pl.BlockSpec(memory_space=pl.ANY)
     return pl.pallas_call(
-        functools.partial(gather_kernel, norm=norm),
+        gather_kernel,
         name="gather_rows",
         in_specs=[vmem, vmem, vmem],
         out_specs=[hbm, hbm],
         out_shape=[sds((2 * rows, width), bf16), sds((ways * pack.shape[0], pack.shape[1]), bf16)],
         scratch_shapes=[
-            pltpu.VMEM((rows, width), bf16),
-            pltpu.SemaphoreType.DMA((16, 4)), pltpu.SemaphoreType.DMA((16,)),
+            pltpu.VMEM((rows, width), bf16), *gather_scratch(),
             pltpu.SemaphoreType.DMA((4,)), pltpu.SemaphoreType.DMA((4,)), pltpu.SemaphoreType.DMA((5,)),
         ],
         compiler_params=pltpu.CompilerParams(
@@ -778,8 +844,11 @@
     return pl.BlockSpec((rows, BW), lambda i: (0, i + offset))
 
 
-def params():
-    return pltpu.CompilerParams(dimension_semantics=("arbitrary",), vmem_limit_bytes=60 * 1024 * 1024)
+def params(collective_id=None):
+    return pltpu.CompilerParams(
+        dimension_semantics=("arbitrary",), vmem_limit_bytes=60 * 1024 * 1024,
+        collective_id=collective_id, has_side_effects=collective_id is not None,
+    )
 
 
 def spread(v):
@@ -814,7 +883,7 @@
     pack_a = jnp.concatenate([w_gate_inner[1], w_state_io, spread(w_step)], axis=1)
     pack_b = jnp.concatenate([w_gate_inner[0], w_output.T], axis=1)
     if own_links:
-        normed, wa = gather_rows(residual, norm_gain[None], pack_a, ways, True, 1)
+        normed, wa = gather_rows(residual, norm_gain[None], pack_a, ways, 1)
     else:
         wa = lax.all_gather(pack_a, "dp", axis=0, tiled=True)
         normed = lax.all_gather((scaled * norm_gain).astype(bf16), "tensor", axis=0, tiled=True)
@@ -827,35 +896,37 @@
     rate_t = jnp.broadcast_to(spread(rate)[:48, None], (48, 128))
     gain8 = jnp.broadcast_to(gate_gain[None], (8, units))
 
-    inner, ssd, states, cst, bc, step, cum, step_t, cum_t, pre_t = pl.pallas_call(
-        mixer_forward,
+    hbm = pl.BlockSpec(memory_space=pl.ANY)
+    sem = pltpu.SemaphoreType.DMA
+    inner, ssd, states, cst, bc, step, cum, step_t, cum_t, pre_t, *sent = pl.pallas_call(
+        functools.partial(mixer_forward, own_links),
         name="mixer_forward",
         grid=(blocks,),
         in_specs=[
             once((tokens, width)), by_cols(width), once((width, 384), (0, units // 384)),
             by_cols(8), once((8, BW)), once((8, 128)),
-        ],
+        ] + [once(cotangent.shape), once(pack_b.shape)] * own_links,
         out_specs=[
             by_cols(tokens), by_cols(tokens), pl.BlockSpec((spans, BW, 128), lambda i: (0, i, 0)),
             once((tokens, BW)), once((tokens, BW)), once((tokens, 128)), once((tokens, 128)),
             once((48, tokens)), once((48, tokens)), once((48, tokens)),
-        ],
+        ] + [hbm, hbm] * own_links,
         out_shape=[
             sds((tokens, units)), sds((tokens, units)), sds((spans, units, 128)),
             sds((tokens, BW)), sds((tokens, BW), bf16), sds((tokens, 128)), sds((tokens, 128)),
             sds((48, tokens)), sds((48, tokens)), sds((48, tokens)),
-        ],
+        ] + [sds((tokens, width), bf16), sds((width, 2 * units), bf16)] * own_links,
         scratch_shapes=[
             pltpu.VMEM((tokens + 8, BW), f32), pltpu.VMEM((spans, Q, Q), f32),
             pltpu.VMEM((tokens, 128), f32), pltpu.VMEM((tokens, 128), f32), pltpu.VMEM((8, tokens), f32),
             pltpu.VMEM((Q, HB * Q), bf16), pltpu.VMEM((HB * Q, BW), bf16), pltpu.VMEM((BW, 128), f32),
-        ],
-        compiler_params=params(),
+        ] + (gather_scratch() + [sem, sem, sem((2,))]) * own_links,
+        compiler_params=params(2 if own_links else None),
         cost_estimate=pl.CostEstimate(flops=2 * tokens * width * (units + 384) + 4 * tokens * 256 * units, bytes_accessed=30_000_000, transcendentals=heads * spans * Q * Q),
-    )(normed, wa, wa, kin, kst, hp)
+    )(normed, wa, wa, kin, kst, hp, *[cotangent, pack_b] * own_links)
 
     if own_links:
-        cot, wb = gather_rows(cotangent, norm_gain[None], pack_b, ways, False, 2)
+        cot, wb = sent
     else:
         wb = lax.all_gather(pack_b, "dp", axis=0, tiled=True)
         cot = lax.all_gather(cotangent, "tensor", axis=0, tiled=True)

time: 552 us -> 507 us (0.918)
  Pallas kernels: 366 us -> 331 us
  waiting for transfers between devices: 62 us -> 55.1 us
    pallas_call x3 -> x2, Pallas kernels: 140 us -> 104 us  [the longest x1 62.3 us: on_device(): pl.pallas_call(functools.partial(mixer_forward, own_links), name='mixer_f...]
    ppermute x4, waiting for transfers between devices: 62 us -> 55.1 us  [swap(): return lax.ppermute(v, 'tensor', [(0, 1), (1, 0)])]
  transfers between devices with their start and end apart: 4 -> 4, of which waited for: 2 -> 2; matrix products, arithmetic and copies ran while one was open for 2% -> 4% of each run, Pallas kernels for 0% -> 0%
where the time goes in v3:
time: 507 us; the launch traced here: 498 us
  Pallas kernels  331 us (65%)
  matrix products  57.1 us (11%)
  waiting for transfers between devices  55.1 us (11%)
  other arithmetic  30 us (6%)
  local copies, waits for them, and re-layouts  20.1 us (4%)
    pallas_call x1, Pallas kernels, on_device(): pl.pallas_call(mixer_backward, name='mixer_backward', grid=(blocks,), in_...  68.3 us
    pallas_call x1, Pallas kernels, reduce_rows(): pl.pallas_call(reduce_kernel, name='reduce_rows', in_specs=[hbm], out_spe...  66.3 us
    pallas_call x1, Pallas kernels, on_device(): pl.pallas_call(functools.partial(mixer_forward, own_links), name='mixer_f...  62.3 us
    pallas_call x1, Pallas kernels, reduce_rows(): pl.pallas_call(reduce_small_kernel, name='reduce_rows_small', in_specs=[h...  58.9 us
    dot_general x8, matrix products, mm(): lax.dot_general(a, b, (((ca,), (cb,)), ((), ())), preferred_element_type=...  57.1 us
    ppermute x4, waiting for transfers between devices, swap(): return lax.ppermute(v, 'tensor', [(0, 1), (1, 0)])  55.1 us
    pallas_call x1, Pallas kernels, gather_rows(): pl.pallas_call(gather_kernel, name='gather_rows', in_specs=[vmem, vmem, v...  42.1 us
    pallas_call x1, Pallas kernels, on_device(): pl.pallas_call(gate_forward, name='gate_forward', grid=(blocks,), in_spec...  19 us
  transfers between devices with their start and end apart: 4, of which 2 were waited for; matrix products, arithmetic and copies ran while one was open for 4% of the time, Pallas kernels for 0%

profile of v3, /device:TPU:0, one launch (start us, length us, event | category | flops | bytes accessed | tf_op | source)
XLA Modules:
  0.0 498.1 jit_solution(207586362337523880)
XLA Ops:
  0.7 1.1 slice_bitcast_fusion.3
  1.8 0.7 pad_bitcast_fusion
  2.6 1.3 broadcast_in_dim.40.gain
  3.9 0.7 exponential_negate_fusion
  4.7 0.7 reshape.85
  5.5 0.7 broadcast_in_dim.41
  6.5 1.3 concatenate.35.kst
  7.8 1.8 pad_maximum_fusion.3.refs_1_
  9.6 1.6 fusion.23.pack
  11.2 42.1 %gather_rows.1 = (bf16[1024,1536]{1,0:T(8,128)(2,1)}, bf16[1536,1920]{1,0:T(8,128)(2,1)}) custom-call(bf16[512,1536]{1,0:T(8,128)(2,1)} %tokens_in.1, f32[1,1536]{1,0:T(1,128)} %broadcast_in_dim.40.gain, bf16[96,1920]{1,0:T(8,128)(2,1)} %fusion.23.pack), custom_call_target="tpu_custom_call" | custom-call | tf_op jit(solution)/shard_map/gather_rows/pallas_call | solution.py:609
  53.3 0.7 maximum_maximum_fusion.1.hp
  54.0 0.7 maximum_maximum_fusion.kin
  54.6 62.3 %mixer_forward.1 = (f32[1024,1536]{1,0:T(8,128)}, f32[1024,1536]{1,0:T(8,128)}, f32[4,1536,128]{2,1,0:T(8,128)}, f32[1024,256]{1,0:T(8,128)}, bf16[1024,256]{1,0...) custom-call(bf16[1024,1536]{1,0:T(8,128)(2,1)} %get-tuple-element.41, ...), custom_call_target="tpu_custom_call" | custom-call | flops 7650410496 | bytes 30000000 | tf_op jit(solution)/shard_map/mixer_forward/pallas_call | solution.py:901
  117.6 19.0 %gate_forward.1 = (f32[1024,1536]{1,0:T(8,128)}, f32[1024,1536]{1,0:T(8,128)}, f32[8,1024]{1,0:T(8,128)}) custom-call(bf16[1024,1536]{1,0:T(8,128)(2,1)} %get-tuple-element.41.normed, bf16[1024,1536]{1,0:T(8,128)(2,1)} %get-tuple-element.43.cot, bf16[1536,3072]{1,0:T(8,128)(2,1)} %get-tuple-element.44.wg.wo, bf16[1536,3072]{1,0:T(8,128)(2,1)} %get-tuple-element.44.wg.wo, ...), custom_call_target="tpu_custom_call" | custom-call | flops 9663676416 | bytes 35000000 | tf_op jit(solution)/shard_map/gate_forward/pallas_call | solution.py:934
  136.6 0.7 collective-permute-start
  137.7 3.0 collective-permute-done
  140.8 1.4 add.78.stats
  142.1 14.0 %gate_backward.1 = (bf16[1024,1536]{1,0:T(8,128)(2,1)}, bf16[1024,1536]{1,0:T(8,128)(2,1)}, bf16[1024,1536]{1,0:T(8,128)(2,1)}, f32[8,1536]{1,0:T(8,128)}) custom-call(f32[8,1024]{1,0:T(8,128)} %add.78.stats, f32[1024,1536]{1,0:T(8,128)} %get-tuple-element.47.gate, f32[1024,1536]{1,0:T(8,128)} %get-tuple-element.45.ssd, f32[1024,1536]{1,0:T(8,128)} %get-tuple-element.48.ggo, ...), custom_call_target="tpu_custom_call" | custom-call | flops 31457280 | bytes 30000000 | tf_op jit(solution)/shard_map/gate_backward/pallas_call | solution.py:950
  156.2 0.7 broadcast_in_dim.47.rateT
  156.9 68.3 %mixer_backward.1 = (bf16[1024,1536]{1,0:T(8,128)(2,1)}, f32[8,1536]{1,0:T(8,128)}, bf16[1024,384]{1,0:T(8,128)(2,1)}, f32[8,256]{1,0:T(8,128)}, f32[48,128]{1,0:T(8,128)}) custom-call(f32[1024,1536]{1,0:T(8,128)} %get-tuple-element.51.inner, bf16[1024,1536]{1,0:T(8,128)(2,1)} %get-tuple-element.52.dy, f32[4,1536,128]{2,1,0:T(8,128)} %get-tuple-element.53.states, ...), custom_call_target="tpu_custom_call" | custom-call | flops 40000000000 | bytes 30000000 | tf_op jit(solution)/shard_map/mixer_backward/pallas_call | solution.py:972
  225.1 0.7 reshape.89
  225.8 1.0 slice_reduce_fusion
  226.9 0.8 slice.100
  227.7 7.9 %convolution_convert_fusion = bf16[1536,1536]{1,0:T(8,128)(2,1)S(1)} fusion(bf16[1024,1536]{1,0:T(8,128)(2,1)} %get-tuple-element.41.normed, bf16[1024,1536]{1,0:T(8,128)(2,1)} %get-tuple-element.61), kind=kOutput, calls=%fused_computation.1 | convolution fusion | flops 4834197504 | bytes 11010048 | tf_op jit(solution)/shard_map/dot_general | solution.py:24
  235.7 1.8 convolution_convert_fusion.3
  237.5 3.0 pad_maximum_fusion.1.grads
  240.5 0.6 pad_maximum_fusion.5.small
  241.1 58.9 %reduce_rows_small.1 = (f32[96,1920]{1,0:T(8,128)}, f32[8,1536]{1,0:T(8,128)}) custom-call(bf16[1536,1920]{1,0:T(8,128)(2,1)} %pad_maximum_fusion.1.grads, f32[8,1536]{1,0:T(8,128)} %pad_maximum_fusion.5.small), custom_call_target="tpu_custom_call" | custom-call | tf_op jit(solution)/shard_map/reduce_rows_small/pallas_call | solution.py:814
  300.1 0.9 slice.104
  301.0 1.3 multiply_reduce_fusion
  302.3 9.3 %convolution_convert_fusion.1 = bf16[1536,1536]{1,0:T(8,128)(2,1)} fusion(bf16[1024,1536]{1,0:T(8,128)(2,1)} %get-tuple-element.43.cot, bf16[1024,1536]{1,0:T(8,128)(2,1)} %get-tuple-element.49), kind=kOutput, calls=%fused_computation.2 | convolution fusion | flops 4834197504 | bytes 11010048 | tf_op jit(solution)/shard_map/dot_general | solution.py:24
  311.6 8.9 %fusion.6 = bf16[1024,1536]{1,0:T(8,128)(2,1)} fusion(bf16[1024,1536]{1,0:T(8,128)(2,1)S(1)} %copy-done.15, bf16[1536,3072]{1,0:T(8,128)(2,1)} %get-tuple-element.44.wg.wo), kind=kOutput, calls=%fused_computation.15 | convolution fusion | flops 4833411072 | bytes 11010048 | tf_op jit(solution)/shard_map/dot_general | solution.py:24
  320.5 7.0 %fusion = f32[1024,1536]{1,0:T(8,128)} fusion(bf16[1024,1536]{1,0:T(8,128)(2,1)S(1)} %copy-done.16, bf16[1536,1920]{1,0:T(8,128)(2,1)S(1)} %bitcast.49), kind=kOutput, calls=%fused_computation.9 | convolution fusion | flops 4831838208 | bytes 14155776 | tf_op jit(solution)/shard_map/dot_general | solution.py:24
  327.5 4.4 fusion.20
  332.0 7.9 %convolution_convert_fusion.2 = bf16[1536,1536]{1,0:T(8,128)(2,1)S(1)} fusion(bf16[1024,1536]{1,0:T(8,128)(2,1)} %get-tuple-element.41.normed, bf16[1024,1536]{1,0:T(8,128)(2,1)} %get-tuple-element.50), kind=kOutput, calls=%fused_computation.3 | convolution fusion | flops 4834197504 | bytes 11010048 | tf_op jit(solution)/shard_map/dot_general | solution.py:24
  339.9 4.8 pad_maximum_fusion.grads
  344.7 66.3 %reduce_rows.1 = f32[96,3072]{1,0:T(8,128)} custom-call(bf16[1536,3072]{1,0:T(8,128)(2,1)} %pad_maximum_fusion.grads), custom_call_target="tpu_custom_call" | custom-call | tf_op jit(solution)/shard_map/reduce_rows/pallas_call | solution.py:810
  411.1 2.4 slice_bitcast_fusion
  413.5 2.7 constant_dynamic-slice_fusion.1
  416.2 0.6 collective-permute-start.1
  416.8 9.8 %add_convert_fusion = bf16[1024,1536]{1,0:T(8,128)(2,1)S(1)} fusion(f32[1024,1536]{1,0:T(8,128)} %fusion.20, f32[1024,1536]{1,0:T(8,128)} %fusion, bf16[1024,1536]{1,0:T(8,128)(2,1)S(1)} %copy-done.14, bf16[1536,3072]{1,0:T(8,128)(2,1)} %get-tuple-element.44.wg.wo), kind=kOutput, calls=%fused_computation.4 | convolution fusion | flops 4836556800 | bytes 23592960 | tf_op jit(solution)/shard_map/dot_general | solution.py:24
  426.7 1.3 constant_dynamic-slice_fusion
  427.9 1.4 collective-permute-start.2
  429.5 0.7 collective-permute-start.3
  430.9 1.1 pad_maximum_fusion.2
  434.8 52.0 %collective-permute-done.3 = f32[12976]{0:T(1024)S(1)} collective-permute-done((f32[12976]{0:T(1024)S(1)}, f32[12976]{0:T(1024)S(1)}, u32[]{:S(2)}, u32[]{:S(2)}) %collective-permute-start.3) | collective-permute-done | bytes 51936 | tf_op jit(solution)/shard_map/ppermute | solution.py:826
  488.7 2.3 fusion.13
  491.0 6.0 %fusion.16 = (f32[512,1536]{1,0:T(8,128)}, bf16[512,1536]{1,0:T(8,128)(2,1)}) fusion(bf16[512,1536]{1,0:T(8,128)(2,1)S(1)} %copy-done, bf16[512,1536]{1,0:T(8,128)(2,1)S(1)} %copy-done.4, bf16[512,1536]{1,0:T(8,128)(2,1)S(1)} %collective-permute-done.2, f32[512]{0:T(512)S(1)} %broadcast_multiply_fusion, f32[1536]{0:T(1024)S(1)} %copy-done.9, ...), kind=kLoop, calls=%fused_computation.21 | loop fusion | flops 12582912 | bytes 14166020 | tf_op jit(solution)/shard_map/add | solution.py:1014
  (88 shorter events, 7.9 us)
Async XLA Ops:
  0.6 53.3 %copy-start.11 = (f32[5,1536]{1,0:T(8,128)S(1)}, f32[5,1536]{1,0:T(8,128)}, u32[]{:S(2)}) copy-start(f32[5,1536]{1,0:T(8,128)} %param.18) | copy-start | bytes 92164
  54.6 62.3 %copy-start.12 = (f32[1536]{0:T(1024)S(1)}, f32[1536]{0:T(1024)}, u32[]{:S(2)}) copy-start(f32[1536]{0:T(1024)} %param.23) | copy-start | bytes 18436
  117.6 19.8 %copy-start = (bf16[512,1536]{1,0:T(8,128)(2,1)S(1)}, bf16[512,1536]{1,0:T(8,128)(2,1)}, u32[]{:S(2)}) copy-start(bf16[512,1536]{1,0:T(8,128)(2,1)} %tokens_in.1) | copy-start | bytes 4718596
  136.6 4.1 collective-permute-start
  227.7 7.9 %copy-start.6 = (bf16[1024,384]{1,0:T(8,128)(2,1)S(1)}, bf16[1024,384]{1,0:T(8,128)(2,1)}, u32[]{:S(2)}) copy-start(bf16[1024,384]{1,0:T(8,128)(2,1)} %get-tuple-element.62) | copy-start | bytes 2359300
  227.7 7.9 %copy-start.13 = (bf16[1024,1536]{1,0:T(8,128)(2,1)S(1)}, bf16[1024,1536]{1,0:T(8,128)(2,1)}, u32[]{:S(2)}) copy-start(bf16[1024,1536]{1,0:T(8,128)(2,1)} %get-tuple-element.41.normed) | copy-start | bytes 9437188
  237.5 3.0 copy-start.10
  240.5 60.5 %copy-start.7 = (bf16[96,256]{1,0:T(8,128)(2,1)S(1)}, bf16[96,256]{1,0:T(8,128)(2,1)}, u32[]{:S(2)}) copy-start(bf16[96,256]{1,0:T(8,128)(2,1)} %param.16) | copy-start | bytes 147460
  302.3 9.3 %copy-start.15 = (bf16[1024,1536]{1,0:T(8,128)(2,1)S(1)}, bf16[1024,1536]{1,0:T(8,128)(2,1)}, u32[]{:S(2)}) copy-start(bf16[1024,1536]{1,0:T(8,128)(2,1)} %get-tuple-element.49) | copy-start | bytes 9437188
  302.3 18.3 %slice-start.2 = ((s8[5898240]{0:T(1024)(128)(4,1)}), s8[4194304]{0:T(1024)(128)(4,1)S(1)}, s32[]{:S(2)}) async-start(s8[5898240]{0:T(1024)(128)(4,1)} %bitcast.48), calls=%async_computation.2 | async-start | bytes 8388608
  311.6 8.9 %slice-start.3 = ((s8[5898240]{0:T(1024)(128)(4,1)}), s8[1703936]{0:T(1024)(128)(4,1)S(1)}, s32[]{:S(2)}) async-start(s8[5898240]{0:T(1024)(128)(4,1)} %bitcast.48), calls=%async_computation.3 | async-start | bytes 3407872
  311.6 8.9 %copy-start.16 = (bf16[1024,1536]{1,0:T(8,128)(2,1)S(1)}, bf16[1024,1536]{1,0:T(8,128)(2,1)}, u32[]{:S(2)}) copy-start(bf16[1024,1536]{1,0:T(8,128)(2,1)} %get-tuple-element.61) | copy-start | bytes 9437188
  327.5 4.4 copy-start.8
  327.5 12.4 %slice-start = ((s8[4718592]{0:T(1024)(128)(4,1)}), s8[524288]{0:T(1024)(128)(4,1)S(1)}, s32[]{:S(2)}) async-start(s8[4718592]{0:T(1024)(128)(4,1)} %bitcast.45), calls=%async_computation | async-start | bytes 1048576
  332.0 7.9 %slice-start.1 = ((s8[4718592]{0:T(1024)(128)(4,1)}), s8[4194304]{0:T(1024)(128)(4,1)S(1)}, s32[]{:S(2)}) async-start(s8[4718592]{0:T(1024)(128)(4,1)} %bitcast.45), calls=%async_computation.1 | async-start | bytes 8388608
  344.7 66.3 %copy-start.5 = (bf16[2,96,1536]{2,1,0:T(8,128)(2,1)S(1)}, bf16[2,96,1536]{2,1,0:T(8,128)(2,1)}, u32[]{:S(2)}) copy-start(bf16[2,96,1536]{2,1,0:T(8,128)(2,1)} %param.15) | copy-start | bytes 1769476
  411.1 5.8 %copy-start.14 = (bf16[1024,1536]{1,0:T(8,128)(2,1)S(1)}, bf16[1024,1536]{1,0:T(8,128)(2,1)}, u32[]{:S(2)}) copy-start(bf16[1024,1536]{1,0:T(8,128)(2,1)} %get-tuple-element.50) | copy-start | bytes 9437188
  416.2 74.8 %collective-permute-start.1 = (bf16[512,1536]{1,0:T(8,128)(2,1)}, bf16[512,1536]{1,0:T(8,128)(2,1)}, u32[]{:S(2)}, u32[]{:S(2)}) collective-permute-start(bf16[512,1536]{1,0:T(8,128)(2,1)} %constant_dynamic-slice_fusion.1), channel_id=1, source_target_pairs={{0,1},{1,0},{2,3},{3,2},{4,5},{5,4},{6,7},{7,6},{8,9},{9,8},{10,11... | collective-permute-start | bytes 4718600 | tf_op jit(solution)/shard_map/ppermute | solution.py:826
  426.6 5.3 %copy-start.1 = (bf16[1024,1536]{1,0:T(8,128)(2,1)}, bf16[1024,1536]{1,0:T(8,128)(2,1)S(1)}, u32[]{:S(2)}) copy-start(bf16[1024,1536]{1,0:T(8,128)(2,1)S(1)} %add_convert_fusion) | copy-start | bytes 9437188
  426.6 2.7 copy-start.9
  426.7 2.8 copy-start.3
  427.9 60.7 %collective-permute-start.2 = (bf16[512,1536]{1,0:T(8,128)(2,1)}, bf16[512,1536]{1,0:T(8,128)(2,1)S(1)}, u32[]{:S(2)}, u32[]{:S(2)}) collective-permute-start(bf16[512,1536]{1,0:T(8,128)(2,1)} %constant_dynamic-slice_fusion), channel_id=1, source_target_pairs={{0,1},{1,0},{2,3},{3,2},{4,5},{5,4},{6,7},{7,6},{8,9},{9,8},{10,11... | collective-permute-start | bytes 4718600 | tf_op jit(solution)/shard_map/ppermute | solution.py:826
  429.5 57.3 %collective-permute-start.3 = (f32[12976]{0:T(1024)S(1)}, f32[12976]{0:T(1024)S(1)}, u32[]{:S(2)}, u32[]{:S(2)}) collective-permute-start(f32[12976]{0:T(1024)S(1)} %pad_maximum_fusion.4), channel_id=1, source_target_pairs={{0,1},{1,0},{2,3},{3,2},{4,5},{5,4},{6,7},{7,6},{8,9},{9,8},{10,11... | collective-permute-start | bytes 155720 | tf_op jit(solution)/shard_map/ppermute | solution.py:826
  434.8 56.2 %copy-start.2 = (bf16[1024,1536]{1,0:T(8,128)(2,1)S(1)}, bf16[1024,1536]{1,0:T(8,128)(2,1)}, u32[]{:S(2)}) copy-start(bf16[1024,1536]{1,0:T(8,128)(2,1)} %copy-done.1) | copy-start | bytes 9437188
  434.8 56.2 %copy-start.4 = (bf16[512,1536]{1,0:T(8,128)(2,1)S(1)}, bf16[512,1536]{1,0:T(8,128)(2,1)}, u32[]{:S(2)}) copy-start(bf16[512,1536]{1,0:T(8,128)(2,1)} %refs_0_.1) | copy-start | bytes 4718596

commit v4 on v3

--- a/solution.py
+++ b/solution.py
@@ -210,11 +210,16 @@
             move.finish()
 
 
-def gate_forward(normed, cot, wg, wo, ssd, gain, gate_out, ggo_out, stats_out, sq, gi):
+def gate_forward(links, normed, cot, wg, wo, ssd, gain, gate_out, ggo_out, stats_out, sq, gi, *refs):
     i = pl.program_id(0)
 
     @pl.when(i == 0)
     def _():
+        if links:
+            barrier = pltpu.get_barrier_semaphore()
+            other = {"tensor": 1 - lax.axis_index("tensor")}
+            pl.semaphore_signal(barrier, 1, device_id=other, device_id_type=MESH)
+            pl.semaphore_wait(barrier, 1)
         sq[...] = jnp.zeros(sq.shape, f32)
         gi[...] = jnp.zeros(gi.shape, f32)
 
@@ -236,14 +241,32 @@
             jnp.sum(sq[...], axis=1, keepdims=True),
             jnp.where(lane == 1, jnp.sum(gi[...], axis=1, keepdims=True), 0.0),
         )
-        stats_out[...] = jnp.transpose(both)[:8]
-
-
-def gate_backward(unit_total, stats, gate, ssd, ggo, gain, dy_out, dgate_out, ng_out, gg_out, cols):
+        if not links:
+            stats_out[...] = jnp.transpose(both)[:8]
+            return
+        mine, landed, send, recv = refs
+        mine[...] = jnp.transpose(both)[:8]
+        swap = remote(mine, landed, send, recv, tensor=1 - lax.axis_index("tensor"))
+        swap.start()
+        swap.wait()
+        stats_out[...] = mine[...] + landed[...]
+
+
+def gate_backward(
+    unit_total, stats, gate, ssd, ggo, gain, normed, cot, dy_out, dgate_out, ng_out, gg_out, grads_out, cols, normed_t, cot_t
+):
     @pl.when(pl.program_id(0) == 0)
     def _():
         full = jnp.concatenate([stats[...], jnp.zeros((120, stats.shape[1]), f32)], axis=0)
         cols[...] = jnp.transpose(full)
+
+        def turn(n, carry):
+            here = pl.ds(pl.multiple_of(n * 128, 128), 128)
+            normed_t[here] = jnp.transpose(normed[:, here])
+            cot_t[here] = jnp.transpose(cot[:, here])
+            return carry
+
+        lax.fori_loop(0, normed.shape[1] // 128, turn, 0)
 
     rstd = lax.rsqrt(cols[:, 0:1] / unit_total + norm_eps)
     pull = rstd * rstd * rstd * (cols[:, 1:2] / unit_total)
@@ -253,20 +276,61 @@
     y = ssd[...]
     gated = y * act
     scaled = gated * rstd
-    ng_out[...] = (scaled * gain[0:1]).astype(bf16)
+    ng = (scaled * gain[0:1]).astype(bf16)
+    ng_out[...] = ng
+    grads_out[1] = mm(cot_t[...], ng).astype(bf16)
     gg = ggo[...]
     gg_out[...] = jnp.broadcast_to(jnp.sum(gg * scaled, axis=0, keepdims=True), gg_out.shape)
     grad = rstd * (gg * gain[0:1]) - gated * pull
     dy_out[...] = (grad * act).astype(bf16)
-    dgate_out[...] = (grad * y * (sig * (1.0 + v * (1.0 - sig)))).astype(bf16)
-
-
-def mixer_backward(
-    inner, dy, states, kin, kst, hp, cst, bc_in, step_in, cum_in, stepT, cumT, preT, rateT,
-    dinner_out, gk_out, dsd_out, gks_out, hs_out,
-    buf, dbuf, gram, gg, gb, gc, colc, cols, rowp, mst, dyst, gmix, sgrad, rs_t, cs_t, dr_t, wg_t, gt_t, gtaps,
-):
+    dgate = (grad * y * (sig * (1.0 + v * (1.0 - sig)))).astype(bf16)
+    dgate_out[...] = dgate
+    grads_out[0] = mm(normed_t[...], dgate).astype(bf16)
+
+
+class BesideBackward:
+    def __init__(self, mixed, grads, far_out, shard_out, scratch):
+        self.here = Place()
+        half = lax.axis_index("tensor")
+        rows = far_out.shape[0]
+        other = mixed.at[pl.ds(pl.multiple_of((1 - half) * rows, rows), rows)]
+        self.across = remote(other, far_out, scratch[0], scratch[1], tensor=1 - half)
+        self.sum = Reduce(self.here, grads, shard_out, scratch[2:7], scratch[7:15])
+
+    def start(self):
+        greet(self.here, True)
+        self.sum.start()
+        self.across.start()
+
+    def step(self, at):
+        total = self.sum
+        z = self.here.z
+        ends = (z == 0) | (z == 3)
+        for n in range(4):
+            pl.when(at == n)(lambda n=n: total.cores(n))
+            pl.when(at == (4, 6, 7, 8)[n])(lambda n=n: total.stay(n))
+            pl.when(at == (5, 10, 15, 19)[n])(lambda n=n: total.sides(n))
+        for n in range(3):
+            when = jnp.where(ends, (5, 10, 15)[n], (11, 16, 17)[n])
+            pl.when(at == when)(lambda n=n: total.pass_on(n))
+
+    def finish(self):
+        self.sum.finish()
+        self.across.wait()
+
+
+def mixer_backward(links, inner, dy, states, kin, kst, hp, cst, bc_in, step_in, cum_in, stepT, cumT, preT, rateT, *refs):
+    refs = list(refs)
+    if links:
+        beside = refs[:2] + refs[7:9]
+        refs = refs[2:7] + refs[9:]
+        work = BesideBackward(*beside, refs[24:])
+    dinner_out, gk_out, dsd_out, gks_out, hs_out = refs[:5]
+    buf, dbuf, gram, gg, gb, gc, colc, cols, rowp, mst, dyst, gmix, sgrad = refs[5:18]
+    rs_t, cs_t, dr_t, wg_t, gt_t, gtaps = refs[18:24]
     i = pl.program_id(0)
+    if links:
+        pl.when(i == 0)(work.start)
     tokens = inner.shape[0]
     spans = tokens // Q
     masks = head_masks()
@@ -376,6 +440,8 @@
             sgrad[at_j] = fade[:, j : j + 1] * state_grad[at_j] + local[at_j]
         gtaps[5:6] += jnp.sum(dy_f * xs, axis=0, keepdims=True)
         dinner_out[rows] = conv_rows(at, kin[...], grad_xs).astype(bf16)
+        if links:
+            work.step(i * spans + back)
         return carry
 
     lax.fori_loop(0, spans, span, 0)
@@ -421,6 +487,8 @@
         gks_out[...] = gtaps[...]
         lane = iota((48, 128), 1)
         hs_out[...] = jnp.where(lane == 0, bias_sum, jnp.where(lane == 1, decay_sum * rate, 0.0))
+        if links:
+            work.finish()
 
 
 class Place:
@@ -627,13 +695,13 @@
         self.here, self.grads, self.out = here, grads, out
         self.mine, self.buf_a, self.buf_b, self.buf_up, self.buf_dn = bufs
         self.local, self.send_a, self.recv_a, self.send_b, self.recv_b, self.send_c, self.recv_up, self.recv_dn = sems
-        self.rows = out.shape[0]
+        self.parts, self.rows = out.shape[:2]
         z = here.z
         self.order = (3 * (1 - z // 2), (3 * z + 2) % 5, 1 + z % 2, z)
 
     def block(self, z, y, c):
         at = pl.multiple_of(self.here.at(z, y, c) * self.rows, self.rows)
-        return self.grads.at[pl.ds(at, self.rows)]
+        return self.grads.at[:, pl.ds(at, self.rows)]
 
     def copy_a(self, z, y):
         here, at = self.here, z * 2 + y
@@ -656,7 +724,9 @@
     def add(self, at, buf, slot):
         def rows(n, carry):
             piece = pl.ds(pl.multiple_of(n * 16, 16), 16)
-            self.mine[at, piece] = (self.mine[at, piece].astype(f32) + buf[slot, piece].astype(f32)).astype(bf16)
+            for part in range(self.parts):
+                total = self.mine[at, part, piece].astype(f32) + buf[slot, part, piece].astype(f32)
+                self.mine[at, part, piece] = total.astype(bf16)
             return carry
 
         lax.fori_loop(0, self.rows // 16, rows, 0)
@@ -723,9 +793,10 @@
 
         def rows(n, carry):
             piece = pl.ds(pl.multiple_of(n * 16, 16), 16)
-            below = jnp.where(z > 0, self.buf_up[z, piece].astype(f32), 0.0)
-            above = jnp.where(z < 3, self.buf_dn[z, piece].astype(f32), 0.0)
-            self.out[piece] = self.mine[at, piece].astype(f32) + below + above
+            for part in range(self.parts):
+                below = jnp.where(z > 0, self.buf_up[z, part, piece].astype(f32), 0.0)
+                above = jnp.where(z < 3, self.buf_dn[z, part, piece].astype(f32), 0.0)
+                self.out[part, piece] = self.mine[at, part, piece].astype(f32) + below + above
             return carry
 
         lax.fori_loop(0, self.rows // 16, rows, 0)
@@ -737,47 +808,34 @@
             pl.when(zn > z)(lambda zn=zn: self.copy_up(zn).wait_send())
             pl.when(zn < z)(lambda zn=zn: self.copy_dn(zn).wait_send())
 
-    def all(self):
-        self.start()
-        for n in range(4):
-            self.cores(n)
-        for n in range(4):
-            self.stay(n)
-        for n in range(3):
-            self.sides(n)
-            self.pass_on(n)
-        self.sides(3)
-
-
-def reduce_scratch(rows, cols):
+
+def reduce_scratch(*block):
     sem = pltpu.SemaphoreType.DMA
     return [
-        pltpu.VMEM((8, rows, cols), bf16), pltpu.VMEM((8, rows, cols), bf16), pltpu.VMEM((4, rows, cols), bf16),
-        pltpu.VMEM((4, rows, cols), bf16), pltpu.VMEM((4, rows, cols), bf16),
+        pltpu.VMEM((8,) + block, bf16), pltpu.VMEM((8,) + block, bf16), pltpu.VMEM((4,) + block, bf16),
+        pltpu.VMEM((4,) + block, bf16), pltpu.VMEM((4,) + block, bf16),
         sem((8,)), sem((8,)), sem((8,)), sem((4,)), sem((4,)), sem((4,)), sem((4,)), sem((4,)),
     ]
 
 
-def reduce_kernel(grads, out, *scratch):
+def tail_kernel(grads, small, mixed, out, small_out, far_out, *scratch):
     here = Place()
-    greet(here, False)
-    work = Reduce(here, grads, out, scratch[:5], scratch[5:])
-    work.all()
-    work.finish()
-
-
-def reduce_small_kernel(grads, small, out, small_out, *scratch):
-    here = Place()
+    half = lax.axis_index("tensor")
     far = pltpu.get_barrier_semaphore()
     partners = [here.me + bit - 2 * bit * ((here.me // bit) % 2) for bit in (1, 2, 4, 8)]
     for partner in partners:
         pl.semaphore_signal(far, 1, device_id={"dp": partner}, device_id_type=MESH)
+    pl.semaphore_signal(far, 1, device_id={"tensor": 1 - half}, device_id_type=MESH)
     middle = (here.z == 1) | (here.z == 2)
     pl.when(here.z == 1)(lambda: pl.semaphore_signal(far, 1, device_id={"dp": here.up()}, device_id_type=MESH))
     pl.when(here.z == 2)(lambda: pl.semaphore_signal(far, 1, device_id={"dp": here.down()}, device_id_type=MESH))
-    pl.semaphore_wait(far, 4 + middle.astype(jnp.int32))
+    pl.semaphore_wait(far, 5 + middle.astype(jnp.int32))
     work = Reduce(here, grads, out, scratch[:5], scratch[5:13])
-    total, landed, send, recv = scratch[13:]
+    total, landed, send, recv, send_x, recv_x = scratch[13:]
+    rows = far_out.shape[0]
+    other = mixed.at[pl.ds(pl.multiple_of((1 - half) * rows, rows), rows)]
+    across = remote(other, far_out, send_x, recv_x, tensor=1 - half)
+    across.start()
     total[0] = small[...]
     for k in range(4):
         if k == 0:
@@ -797,29 +855,25 @@
     small_out[...] = total[4]
     work.sides(3)
     work.finish()
-
-
-def reduce_rows(grads, ways, collective_id, small=None):
-    rows, cols = grads.shape[0] // ways, grads.shape[1]
+    across.wait()
+
+
+def reduce_tail(grads, ways, small, mixed, collective_id):
+    parts, rows, cols = grads.shape[0], grads.shape[1] // ways, grads.shape[2]
+    tokens, width = mixed.shape
     vmem = pl.BlockSpec(memory_space=pltpu.VMEM)
     hbm = pl.BlockSpec(memory_space=pl.ANY)
-    settings = pltpu.CompilerParams(
-        collective_id=collective_id, has_side_effects=True, vmem_limit_bytes=60 * 1024 * 1024
-    )
-    if small is None:
-        return pl.pallas_call(
-            reduce_kernel, name="reduce_rows", in_specs=[hbm], out_specs=vmem, out_shape=sds((rows, cols)),
-            scratch_shapes=reduce_scratch(rows, cols), compiler_params=settings,
-        )(grads)
+    sem = pltpu.SemaphoreType.DMA
     return pl.pallas_call(
-        reduce_small_kernel, name="reduce_rows_small", in_specs=[hbm, vmem], out_specs=[vmem, vmem],
-        out_shape=[sds((rows, cols)), sds(small.shape)],
-        scratch_shapes=reduce_scratch(rows, cols) + [
-            pltpu.VMEM((5,) + small.shape, f32), pltpu.VMEM((4,) + small.shape, f32),
-            pltpu.SemaphoreType.DMA((4,)), pltpu.SemaphoreType.DMA((4,)),
+        tail_kernel, name="tail", in_specs=[hbm, vmem, hbm], out_specs=[vmem, vmem, hbm],
+        out_shape=[sds((parts, rows, cols)), sds(small.shape), sds((tokens // 2, width), bf16)],
+        scratch_shapes=reduce_scratch(parts, rows, cols) + [
+            pltpu.VMEM((5,) + small.shape, f32), pltpu.VMEM((4,) + small.shape, f32), sem((4,)), sem((4,)), sem, sem,
         ],
-        compiler_params=settings,
-    )(grads, small)
+        compiler_params=pltpu.CompilerParams(
+            collective_id=collective_id, has_side_effects=True, vmem_limit_bytes=60 * 1024 * 1024
+        ),
+    )(grads, small, mixed)
 
 
 def swap(v):
@@ -932,7 +986,7 @@
         cot = lax.all_gather(cotangent, "tensor", axis=0, tiled=True)
 
     gate, ggo, stats = pl.pallas_call(
-        gate_forward,
+        functools.partial(gate_forward, own_links),
         name="gate_forward",
         grid=(blocks,),
         in_specs=[
@@ -941,36 +995,40 @@
         ],
         out_specs=[by_cols(tokens), by_cols(tokens), once((8, tokens))],
         out_shape=[sds((tokens, units)), sds((tokens, units)), sds((8, tokens))],
-        scratch_shapes=[pltpu.VMEM((tokens, 128), f32), pltpu.VMEM((tokens, 128), f32)],
-        compiler_params=params(),
+        scratch_shapes=[pltpu.VMEM((tokens, 128), f32), pltpu.VMEM((tokens, 128), f32)]
+        + [pltpu.VMEM((8, tokens), f32), pltpu.VMEM((8, tokens), f32), sem, sem] * own_links,
+        compiler_params=params(3 if own_links else None),
         cost_estimate=pl.CostEstimate(flops=4 * tokens * width * units, bytes_accessed=35_000_000, transcendentals=tokens * units),
     )(normed, cot, wb, wb, ssd, gain8)
-    stats = stats + swap(stats)
-
-    dy, dgate, ng, ggg = pl.pallas_call(
+    if not own_links:
+        stats = stats + swap(stats)
+
+    dy, dgate, ng, ggg, grad_b = pl.pallas_call(
         functools.partial(gate_backward, float(unit_total)),
         name="gate_backward",
         grid=(blocks,),
-        in_specs=[once((8, tokens)), by_cols(tokens), by_cols(tokens), by_cols(tokens), by_cols(8)],
-        out_specs=[by_cols(tokens), by_cols(tokens), by_cols(tokens), by_cols(8)],
-        out_shape=[sds((tokens, units), bf16), sds((tokens, units), bf16), sds((tokens, units), bf16), sds((8, units))],
-        scratch_shapes=[pltpu.VMEM((tokens, 128), f32)],
+        in_specs=[
+            once((8, tokens)), by_cols(tokens), by_cols(tokens), by_cols(tokens), by_cols(8),
+            once((tokens, width)), once((tokens, width)),
+        ],
+        out_specs=[
+            by_cols(tokens), by_cols(tokens), by_cols(tokens), by_cols(8),
+            pl.BlockSpec((2, width, BW), lambda i: (0, 0, i)),
+        ],
+        out_shape=[
+            sds((tokens, units), bf16), sds((tokens, units), bf16), sds((tokens, units), bf16), sds((8, units)),
+            sds((2, width, units), bf16),
+        ],
+        scratch_shapes=[pltpu.VMEM((tokens, 128), f32), pltpu.VMEM((width, tokens), bf16), pltpu.VMEM((width, tokens), bf16)],
         compiler_params=params(),
-        cost_estimate=pl.CostEstimate(flops=20 * tokens * units, bytes_accessed=30_000_000, transcendentals=tokens * units),
-    )(stats, gate, ssd, ggo, gain8)
-
-    grad_wo = mm(cot, ng, 0, 0).astype(bf16)
-    grad_wg = mm(normed, dgate, 0, 0).astype(bf16)
-    grad_b = jnp.concatenate([grad_wg, grad_wo], axis=1)
-    if own_links:
-        wb_shard = reduce_rows(grad_b, ways, 3)
-    else:
-        wb_shard = lax.psum_scatter(grad_b, "dp", scatter_dimension=0, tiled=True).astype(f32)
-    mixed, mixed_far = halves(mm(ng, wb[:, units:], 1, 1).astype(bf16), 0)
-    output = (rows_in + mixed.astype(f32) + swap(mixed_far).astype(f32)).astype(bf16)
-
-    dinner, gk, dsd, gks, hs = pl.pallas_call(
-        mixer_backward,
+        cost_estimate=pl.CostEstimate(flops=4 * tokens * units * width, bytes_accessed=45_000_000, transcendentals=tokens * units),
+    )(stats, gate, ssd, ggo, gain8, normed, cot)
+
+    mixed = mm(ng, wb[:, units:], 1, 1).astype(bf16)
+    mixed_near, mixed_far = halves(mixed, 0)
+
+    dinner, gk, dsd, gks, hs, *sent = pl.pallas_call(
+        functools.partial(mixer_backward, own_links),
         name="mixer_backward",
         grid=(blocks,),
         in_specs=[
@@ -978,9 +1036,11 @@
             by_cols(8), once((8, BW)), once((8, 128)),
             once((tokens, BW)), once((tokens, BW)), once((tokens, 128)), once((tokens, 128)),
             once((48, tokens)), once((48, tokens)), once((48, tokens)), once((48, 128)),
-        ],
-        out_specs=[by_cols(tokens), by_cols(8), once((tokens, 384)), once((8, BW)), once((48, 128))],
-        out_shape=[sds((tokens, units), bf16), sds((8, units)), sds((tokens, 384), bf16), sds((8, BW)), sds((48, 128))],
+        ] + [hbm, hbm] * own_links,
+        out_specs=[by_cols(tokens), by_cols(8), once((tokens, 384)), once((8, BW)), once((48, 128))]
+        + [hbm, once((2, width // ways, units))] * own_links,
+        out_shape=[sds((tokens, units), bf16), sds((8, units)), sds((tokens, 384), bf16), sds((8, BW)), sds((48, 128))]
+        + [sds((tokens // 2, width), bf16), sds((2, width // ways, units))] * own_links,
         scratch_shapes=[
             pltpu.VMEM((tokens + 8, BW), f32), pltpu.VMEM((tokens + 8, BW), f32),
             pltpu.VMEM((spans, Q, Q), f32), pltpu.VMEM((spans, Q, Q), f32),
@@ -990,26 +1050,32 @@
             pltpu.VMEM((BW, 128), f32),
             pltpu.VMEM((48, tokens), f32), pltpu.VMEM((48, tokens), f32), pltpu.VMEM((48, tokens), f32),
             pltpu.VMEM((48, tokens), f32), pltpu.VMEM((48, 128), f32), pltpu.VMEM((8, BW), f32),
-        ],
-        compiler_params=params(),
+        ] + ([sem, sem] + reduce_scratch(2, width // ways, units)) * own_links,
+        compiler_params=params(4 if own_links else None),
         cost_estimate=pl.CostEstimate(flops=40_000_000_000, bytes_accessed=30_000_000, transcendentals=heads * spans * Q * Q),
-    )(inner, dy, states, kin, kst, hp, cst, bc, step, cum, step_t, cum_t, pre_t, rate_t)
+    )(inner, dy, states, kin, kst, hp, cst, bc, step, cum, step_t, cum_t, pre_t, rate_t, *[mixed, grad_b] * own_links)
+    if own_links:
+        mixed_got, wb_shard = sent
+    else:
+        mixed_got = swap(mixed_far)
+        wb_shard = lax.psum_scatter(grad_b, "dp", scatter_dimension=1, tiled=True).astype(f32)
+    output = (rows_in + mixed_near.astype(f32) + mixed_got.astype(f32)).astype(bf16)
 
     grad_wi = mm(normed, dinner, 0, 0).astype(bf16)
     grad_ws = mm(normed, dsd, 0, 0).astype(bf16)
     grad_a = jnp.concatenate([grad_wi, grad_ws], axis=1)
     tail = jnp.concatenate([gks[:5].reshape(-1), hs[:, 0], hs[:, 1], jnp.zeros((units - 5 * BW - 96,), f32)])
     small = jnp.concatenate([gk[:6], ggg[:1], tail[None]], axis=0)
+    pulled = (mm(dgate, wb[:, :units], 1, 1) + mm(dinner, wa[:, :units], 1, 1) + mm(dsd, wa[:, units:], 1, 1)).astype(bf16)
+    near, far = halves(pulled, 0)
     if own_links:
-        wa_shard, small = reduce_rows(grad_a, ways, 4, small)
+        wa_shard, small, got = reduce_tail(grad_a[None], ways, small, pulled, 5)
+        wa_shard = wa_shard[0]
     else:
         wa_shard = lax.psum_scatter(grad_a, "dp", scatter_dimension=0, tiled=True).astype(f32)
         small = lax.psum(small, "dp")
-    near, far = halves(
-        (mm(dgate, wb[:, :units], 1, 1) + mm(dinner, wa[:, :units], 1, 1) + mm(dsd, wa[:, units:], 1, 1)).astype(bf16),
-        0,
-    )
-    grad_normed = near.astype(f32) + swap(far).astype(f32)
+        got = swap(far)
+    grad_normed = near.astype(f32) + got.astype(f32)
     grad_v = grad_normed * norm_gain
     grad_residual = cotangent.astype(f32) + rstd_in * (
         grad_v - scaled * jnp.mean(grad_v * scaled, axis=1, keepdims=True)
@@ -1020,7 +1086,7 @@
     decay_sum = gathered_heads(small[7, 5 * BW + 48 : 5 * BW + 96], heads)
     skip_sum = jnp.sum(small[5].reshape(heads, HEAD), axis=1)
 
-    gain_rows = jnp.sum(wb_shard[:, :units] * w_gate_inner[0].astype(f32), axis=1) + jnp.sum(
+    gain_rows = jnp.sum(wb_shard[0] * w_gate_inner[0].astype(f32), axis=1) + jnp.sum(
         wa_shard * pack_a.astype(f32), axis=1
     )
     count = gain_rows.shape[0]
@@ -1035,7 +1101,7 @@
         output,
         grad_residual,
         gain_part,
-        jnp.stack([wb_shard[:, :units], wa_shard[:, :units]]),
+        jnp.stack([wb_shard[0], wa_shard[:, :units]]),
         both[:count],
         gathered_heads(wa_shard[:, units + BW :], heads),
         small[0:5],
@@ -1044,7 +1110,7 @@
         decay_sum,
         skip_sum,
         small[6],
-        wb_shard[:, units:].T,
+        wb_shard[1].T,
     )
 
 

time: 507 us -> 383 us (0.76); the launches traced: 498 us -> 382 us
  waiting for transfers between devices: 55.1 us -> 0.01 us
  Pallas kernels: 331 us -> 288 us
  matrix products: 57.1 us -> 46.9 us
  other arithmetic: 30 us -> 24.9 us
    ppermute x4 -> x1, waiting for transfers between devices: 55.1 us -> 0.01 us  [swap(): return lax.ppermute(v, 'tensor', [(0, 1), (1, 0)])]
    pallas_call x4 -> x3, Pallas kernels: 213 us -> 159 us  [the longest x1 76.6 us: on_device(): pl.pallas_call(functools.partial(mixer_backward, own_links), name='mixer_...]
    dot_general x8 -> x6, matrix products: 57.1 us -> 46.9 us  [mm(): lax.dot_general(a, b, (((ca,), (cb,)), ((), ())), preferred_element_type=...]
    pallas_call x1, Pallas kernels: 14 us -> 24 us  [on_device(): pl.pallas_call(functools.partial(gate_backward, float(unit_total)), name=...]
    concatenate x2 -> x0, other arithmetic: 7.78 us -> none  [the longest x1 4.79 us: on_device(): grad_b = jnp.concatenate([grad_wg, grad_wo], axis=1)]
  transfers between devices with their start and end apart: 4 -> 1, of which waited for: 2 -> 0; matrix products, arithmetic and copies ran while one was open for 4% -> 5% of each run, Pallas kernels for 0% -> 0%
where the time goes in v4:
time: 383 us; the launch traced here: 382 us
  Pallas kernels  288 us (75%)
  matrix products  46.9 us (12%)
  other arithmetic  24.9 us (7%)
  local copies, waits for them, and re-layouts  20.4 us (5%)
    pallas_call x1, Pallas kernels, on_device(): pl.pallas_call(functools.partial(mixer_backward, own_links), name='mixer_...  76.6 us
    pallas_call x1, Pallas kernels, on_device(): pl.pallas_call(functools.partial(mixer_forward, own_links), name='mixer_f...  62.5 us
    pallas_call x1, Pallas kernels, reduce_tail(): pl.pallas_call(tail_kernel, name='tail', in_specs=[hbm, vmem, hbm], out_s...  59.5 us
    dot_general x6, matrix products, mm(): lax.dot_general(a, b, (((ca,), (cb,)), ((), ())), preferred_element_type=...  46.9 us
    pallas_call x1, Pallas kernels, gather_rows(): pl.pallas_call(gather_kernel, name='gather_rows', in_specs=[vmem, vmem, v...  42.1 us
    pallas_call x1, Pallas kernels, on_device(): pl.pallas_call(functools.partial(gate_backward, float(unit_total)), name=...  24 us
    pallas_call x1, Pallas kernels, on_device(): pl.pallas_call(functools.partial(gate_forward, own_links), name='gate_for...  22.9 us
  transfers between devices with their start and end apart: 1, of which 0 were waited for; matrix products, arithmetic and copies ran while one was open for 5% of the time, Pallas kernels for 0%

profile of v4, /device:TPU:0, one launch (start us, length us, event | category | flops | bytes accessed | tf_op | source)
XLA Modules:
  0.0 381.9 jit_solution(4104738703695045002)
XLA Ops:
  0.7 1.1 slice_bitcast_fusion.2
  1.8 0.7 pad_bitcast_fusion
  2.6 1.3 broadcast_in_dim.43.gain
  3.9 0.7 exponential_negate_fusion
  4.7 0.7 reshape.85
  5.5 0.7 broadcast_in_dim.44
  6.5 1.3 concatenate.32.kst
  7.8 1.8 pad_maximum_fusion.1.refs_1_
  9.6 1.6 fusion.21.pack
  11.2 42.1 %gather_rows.1 = (bf16[1024,1536]{1,0:T(8,128)(2,1)}, bf16[1536,1920]{1,0:T(8,128)(2,1)}) custom-call(bf16[512,1536]{1,0:T(8,128)(2,1)} %tokens_in.1, f32[1,1536]{1,0:T(1,128)} %broadcast_in_dim.43.gain, bf16[96,1920]{1,0:T(8,128)(2,1)} %fusion.21.pack), custom_call_target="tpu_custom_call" | custom-call | tf_op jit(solution)/shard_map/gather_rows/pallas_call | solution.py:677
  53.3 0.7 maximum_maximum_fusion.1.hp
  54.0 0.7 maximum_maximum_fusion.kin
  54.6 62.5 %mixer_forward.1 = (f32[1024,1536]{1,0:T(8,128)}, f32[1024,1536]{1,0:T(8,128)}, f32[4,1536,128]{2,1,0:T(8,128)}, f32[1024,256]{1,0:T(8,128)}, bf16[1024,256]{1,0...) custom-call(bf16[1024,1536]{1,0:T(8,128)(2,1)} %get-tuple-element.45, ...), custom_call_target="tpu_custom_call" | custom-call | flops 7650410496 | bytes 30000000 | tf_op jit(solution)/shard_map/mixer_forward/pallas_call | solution.py:955
  117.1 0.6 broadcast_in_dim.49.gain
  117.8 22.9 %gate_forward.1 = (f32[1024,1536]{1,0:T(8,128)}, f32[1024,1536]{1,0:T(8,128)}, f32[8,1024]{1,0:T(8,128)}) custom-call(bf16[1024,1536]{1,0:T(8,128)(2,1)} %get-tuple-element.45.normed, bf16[1024,1536]{1,0:T(8,128)(2,1)} %get-tuple-element.47.cot, bf16[1536,3072]{1,0:T(8,128)(2,1)} %get-tuple-element.48.wg.wo, bf16[1536,3072]{1,0:T(8,128)(2,1)} %get-tuple-element.48.wg.wo, ...), custom_call_target="tpu_custom_call" | custom-call | flops 9663676416 | bytes 35000000 | tf_op jit(solution)/shard_map/gate_forward/pallas_call | solution.py:988
  140.7 24.0 %gate_backward.1 = (bf16[1024,1536]{1,0:T(8,128)(2,1)}, bf16[1024,1536]{1,0:T(8,128)(2,1)}, bf16[1024,1536]{1,0:T(8,128)(2,1)}, f32[8,1536]{1,0:T(8,128)}, bf16[2,1536,1536]{2,1,0:T(8,128)(2,1)}) custom-call(f32[8,1024]{1,0:T(8,128)} %get-tuple-element.50.stats, f32[1024,1536]{1,0:T(8,128)} %get-tuple-element.51.gate, f32[1024,1536]{1,0:T(8,128)} %get-tuple-element.49.ssd, ...), custom_call_target="tpu_custom_call" | custom-call | flops 9663676416 | bytes 45000000 | tf_op jit(solution)/shard_map/gate_backward/pallas_call | solution.py:1006
  164.7 9.3 %fusion.6.refs_0_ = bf16[1024,1536]{1,0:T(8,128)(2,1)} fusion(bf16[1024,1536]{1,0:T(8,128)(2,1)} %get-tuple-element.53, bf16[1536,3072]{1,0:T(8,128)(2,1)} %get-tuple-element.48.wg.wo), kind=kOutput, calls=%fused_computation.12 | convolution fusion | flops 4833411072 | bytes 11010048 | tf_op jit(solution)/shard_map/dot_general | solution.py:24
  174.0 0.7 broadcast_in_dim.50.rateT
  174.6 76.6 %mixer_backward.1 = (bf16[1024,1536]{1,0:T(8,128)(2,1)}, f32[8,1536]{1,0:T(8,128)}, bf16[1024,384]{1,0:T(8,128)(2,1)}, f32[8,256]{1,0:T(8,128)}, f32[48,128]{1,0...) custom-call(f32[1024,1536]{1,0:T(8,128)} %get-tuple-element.54.inner, ...), custom_call_target="tpu_custom_call" | custom-call | flops 40000000000 | bytes 30000000 | tf_op jit(solution)/shard_map/mixer_backward/pallas_call | solution.py:1030
  251.3 9.9 %fusion = f32[1024,1536]{1,0:T(8,128)} fusion(bf16[1024,1536]{1,0:T(8,128)(2,1)} %get-tuple-element.67, bf16[1536,1920]{1,0:T(8,128)(2,1)} %get-tuple-element.46.wi.wsx), kind=kOutput, calls=%fused_computation.6 | convolution fusion | flops 4831838208 | bytes 14155776 | tf_op jit(solution)/shard_map/dot_general | solution.py:24
  261.2 6.9 %convolution_convert_fusion = bf16[1536,1536]{1,0:T(8,128)(2,1)} fusion(bf16[1024,1536]{1,0:T(8,128)(2,1)S(1)} %copy-done.16, bf16[1024,1536]{1,0:T(8,128)(2,1)S(1)} %copy-done.17), kind=kOutput, calls=%fused_computation | convolution fusion | flops 4834197504 | bytes 11010048 | tf_op jit(solution)/shard_map/dot_general | solution.py:24
  268.1 10.0 %fusion.2 = f32[1024,1536]{1,0:T(8,128)} fusion(bf16[1024,1536]{1,0:T(8,128)(2,1)} %get-tuple-element.66, bf16[1536,3072]{1,0:T(8,128)(2,1)} %get-tuple-element.48.wg.wo), kind=kOutput, calls=%fused_computation.8 | convolution fusion | flops 4831838208 | bytes 14155776 | tf_op jit(solution)/shard_map/dot_general | solution.py:24
  278.5 0.8 slice.99
  279.3 3.9 %convolution_convert_fusion.1 = bf16[1536,384]{1,0:T(8,128)(2,1)S(1)} fusion(bf16[1024,1536]{1,0:T(8,128)(2,1)} %get-tuple-element.45.normed, bf16[1024,384]{1,0:T(8,128)(2,1)S(1)} %copy-done.7), kind=kOutput, calls=%fused_computation.23 | convolution fusion | flops 1208549376 | bytes 5111808 | tf_op jit(solution)/shard_map/dot_general | solution.py:24
  283.2 6.9 %add_convert_fusion.mixed = bf16[1024,1536]{1,0:T(8,128)(2,1)} fusion(f32[1024,1536]{1,0:T(8,128)} %fusion.2, f32[1024,1536]{1,0:T(8,128)S(1)} %copy-done.2, bf16[1024,384]{1,0:T(8,128)(2,1)S(1)} %copy-done.7, bf16[1536,1920]{1,0:T(8,128)(2,1)} %get-tuple-element.46.wi.wsx), kind=kOutput, calls=%fused_computation.1 | convolution fusion | flops 1212678144 | bytes 17694720 | tf_op jit(solution)/shard_map/dot_general | solution.py:24
  290.1 2.9 maximum_bitcast_fusion.grads
  293.0 0.6 pad_maximum_fusion.3.small
  293.6 59.5 %tail.1 = (f32[1,96,1920]{2,1,0:T(8,128)}, f32[8,1536]{1,0:T(8,128)}, bf16[512,1536]{1,0:T(8,128)(2,1)}) custom-call(bf16[1,1536,1920]{2,1,0:T(8,128)(2,1)} %maximum_bitcast_fusion.grads, f32[8,1536]{1,0:T(8,128)} %pad_maximum_fusion.3.small, bf16[1024,1536]{1,0:T(8,128)(2,1)} %add_convert_fusion.mixed), custom_call_target="tpu_custom_call" | custom-call | tf_op jit(solution)/shard_map/tail/pallas_call | solution.py:867
  353.2 1.3 multiply_reduce_fusion
  354.5 0.9 slice.121
  355.4 0.8 slice_reduce_fusion.4
  356.2 1.5 fusion.20
  357.9 1.1 collective-permute-start
  359.0 1.9 slice_bitcast_fusion
  360.9 2.3 slice_bitcast_fusion.1
  363.3 1.8 fusion.17
  365.1 0.6 slice_reduce_fusion.2
  365.7 2.9 fusion.11
  368.7 1.1 pad_maximum_fusion
  369.8 6.0 %fusion.14 = (f32[512,1536]{1,0:T(8,128)}, bf16[512,1536]{1,0:T(8,128)(2,1)}) fusion(bf16[512,1536]{1,0:T(8,128)(2,1)S(1)} %copy-done.1, bf16[512,1536]{1,0:T(8,128)(2,1)S(1)} %copy-done.6, bf16[512,1536]{1,0:T(8,128)(2,1)S(1)} %copy-done.3, f32[512]{0:T(512)S(1)} %broadcast_multiply_fusion, f32[1536]{0:T(1024)S(1)} %copy-done.11, f32[512]{0:T(512)S(1)} %add_rsqrt_fusion, ...), kind=kLoop, calls=%fused_computation.18 | loop fusion | flops 12582912 | bytes 14166020 | tf_op jit(solution)/shard_map/add | solution.py:1080
  375.9 0.8 slice.126
  376.8 0.6 slice.127
  377.5 0.6 reduce_sum.49
  378.2 0.6 reshape.94
  378.9 0.6 reshape.95
  379.5 0.6 slice.125
  380.1 0.6 slice.128
  381.3 0.6 copy.37
  (73 shorter events, 2.1 us)
Async XLA Ops:
  0.6 53.3 %copy-start.13 = (f32[5,1536]{1,0:T(8,128)S(1)}, f32[5,1536]{1,0:T(8,128)}, u32[]{:S(2)}) copy-start(f32[5,1536]{1,0:T(8,128)} %param.18) | copy-start | bytes 92164
  54.6 62.5 %copy-start.14 = (f32[1536]{0:T(1024)S(1)}, f32[1536]{0:T(1024)}, u32[]{:S(2)}) copy-start(f32[1536]{0:T(1024)} %param.23) | copy-start | bytes 18436
  251.3 9.9 %copy-start.16 = (bf16[1024,1536]{1,0:T(8,128)(2,1)S(1)}, bf16[1024,1536]{1,0:T(8,128)(2,1)}, u32[]{:S(2)}) copy-start(bf16[1024,1536]{1,0:T(8,128)(2,1)} %get-tuple-element.45.normed) | copy-start | bytes 9437188
  251.3 9.9 %copy-start.17 = (bf16[1024,1536]{1,0:T(8,128)(2,1)S(1)}, bf16[1024,1536]{1,0:T(8,128)(2,1)}, u32[]{:S(2)}) copy-start(bf16[1024,1536]{1,0:T(8,128)(2,1)} %get-tuple-element.67) | copy-start | bytes 9437188
  268.1 10.1 %copy-start.15 = (f32[8,256]{1,0:T(8,128)S(1)}, f32[8,256]{1,0:T(8,128)}, u32[]{:S(2)}) copy-start(f32[8,256]{1,0:T(8,128)} %get-tuple-element.71) | copy-start | bytes 24580
  268.1 10.1 %copy-start.9 = (f32[48,128]{1,0:T(8,128)S(1)}, f32[48,128]{1,0:T(8,128)}, u32[]{:S(2)}) copy-start(f32[48,128]{1,0:T(8,128)} %get-tuple-element.72) | copy-start | bytes 73732
  268.1 11.1 %copy-start.7 = (bf16[1024,384]{1,0:T(8,128)(2,1)S(1)}, bf16[1024,384]{1,0:T(8,128)(2,1)}, u32[]{:S(2)}) copy-start(bf16[1024,384]{1,0:T(8,128)(2,1)} %get-tuple-element.68) | copy-start | bytes 2359300
  279.3 3.9 %copy-start.2 = (f32[1024,1536]{1,0:T(8,128)S(1)}, f32[1024,1536]{1,0:T(8,128)}, u32[]{:S(2)}) copy-start(f32[1024,1536]{1,0:T(8,128)} %fusion) | copy-start | bytes 18874372
  279.3 10.8 %slice-start = ((s8[4718592]{0:T(1024)(128)(4,1)}), s8[4194304]{0:T(1024)(128)(4,1)S(1)}, s32[]{:S(2)}) async-start(s8[4718592]{0:T(1024)(128)(4,1)} %bitcast.49), calls=%async_computation | async-start | bytes 8388608
  283.2 6.9 %slice-start.1 = ((s8[4718592]{0:T(1024)(128)(4,1)}), s8[524288]{0:T(1024)(128)(4,1)S(1)}, s32[]{:S(2)}) async-start(s8[4718592]{0:T(1024)(128)(4,1)} %bitcast.49), calls=%async_computation.1 | async-start | bytes 1048576
  290.1 2.9 copy-start.12
  293.6 59.5 %copy-start.8 = (bf16[96,256]{1,0:T(8,128)(2,1)S(1)}, bf16[96,256]{1,0:T(8,128)(2,1)}, u32[]{:S(2)}) copy-start(bf16[96,256]{1,0:T(8,128)(2,1)} %param.16) | copy-start | bytes 147460
  293.6 64.0 %copy-start.11 = (f32[1536]{0:T(1024)S(1)}, f32[1536]{0:T(1024)}, u32[]{:S(2)}) copy-start(f32[1536]{0:T(1024)} %param.14) | copy-start | bytes 18436
  356.2 8.9 %copy-start.10 = (f32[8,1536]{1,0:T(8,128)S(1)}, f32[8,1536]{1,0:T(8,128)}, u32[]{:S(2)}) copy-start(f32[8,1536]{1,0:T(8,128)} %get-tuple-element.76) | copy-start | bytes 147460
  356.2 9.5 %copy-start = (bf16[1024,1536]{1,0:T(8,128)(2,1)S(1)}, bf16[1024,1536]{1,0:T(8,128)(2,1)}, u32[]{:S(2)}) copy-start(bf16[1024,1536]{1,0:T(8,128)(2,1)} %add_convert_fusion.mixed) | copy-start | bytes 9437188
  357.9 21.6 %collective-permute-start = (f32[12976]{0:T(1024)S(1)}, f32[12976]{0:T(1024)S(1)}, u32[]{:S(2)}, u32[]{:S(2)}) collective-permute-start(f32[12976]{0:T(1024)S(1)} %pad_maximum_fusion.2), channel_id=1, source_target_pairs={{0,1},{1,0},{2,3},{3,2},{4,5},{5,4},{6,7},{7,6},{8,9},{9,8},{10,11... | collective-permute-start | bytes 155720 | tf_op jit(solution)/shard_map/ppermute | solution.py:880
  365.7 3.0 copy-start.4
  365.7 3.0 copy-start.5
  365.7 4.1 %copy-start.1 = (bf16[512,1536]{1,0:T(8,128)(2,1)S(1)}, bf16[512,1536]{1,0:T(8,128)(2,1)}, u32[]{:S(2)}) copy-start(bf16[512,1536]{1,0:T(8,128)(2,1)} %tokens_in.1) | copy-start | bytes 4718596
  365.7 4.1 %copy-start.3 = (bf16[512,1536]{1,0:T(8,128)(2,1)S(1)}, bf16[512,1536]{1,0:T(8,128)(2,1)}, u32[]{:S(2)}) copy-start(bf16[512,1536]{1,0:T(8,128)(2,1)} %get-tuple-element.73) | copy-start | bytes 4718596
  365.7 4.1 %copy-start.6 = (bf16[512,1536]{1,0:T(8,128)(2,1)S(1)}, bf16[512,1536]{1,0:T(8,128)(2,1)}, u32[]{:S(2)}) copy-start(bf16[512,1536]{1,0:T(8,128)(2,1)} %refs_0_.1) | copy-start | bytes 4718596

commit v5 on v4

--- a/solution.py
+++ b/solution.py
@@ -253,7 +253,7 @@
 
 
 def gate_backward(
-    unit_total, stats, gate, ssd, ggo, gain, normed, cot, dy_out, dgate_out, ng_out, gg_out, grads_out, cols, normed_t, cot_t
+    unit_total, stats, gate, ssd, ggo, gain, normed, cot, dy_out, dgate_out, ng_out, gg_out, grads_out, normed_t, cols, cot_t
 ):
     @pl.when(pl.program_id(0) == 0)
     def _():
@@ -306,13 +306,13 @@
         total = self.sum
         z = self.here.z
         ends = (z == 0) | (z == 3)
-        for n in range(4):
-            pl.when(at == n)(lambda n=n: total.cores(n))
-            pl.when(at == (4, 6, 7, 8)[n])(lambda n=n: total.stay(n))
-            pl.when(at == (5, 10, 15, 19)[n])(lambda n=n: total.sides(n))
-        for n in range(3):
+        for n, block in enumerate(total.order):
+            pl.when(at == n)(lambda z=block: total.cores(z))
+            pl.when(at == (4, 6, 7, 8)[n])(lambda z=block: total.stay(z))
+            pl.when(at == (5, 10, 15, 19)[n])(lambda z=block: total.sides(z))
+        for n, block in enumerate(total.order[:3]):
             when = jnp.where(ends, (5, 10, 15)[n], (11, 16, 17)[n])
-            pl.when(at == when)(lambda n=n: total.pass_on(n))
+            pl.when(at == when)(lambda z=block: total.pass_on(z))
 
     def finish(self):
         self.sum.finish()
@@ -693,13 +693,24 @@
 class Reduce:
     def __init__(self, here, grads, out, bufs, sems):
         self.here, self.grads, self.out = here, grads, out
-        self.mine, self.buf_a, self.buf_b, self.buf_up, self.buf_dn = bufs
+        self.held, self.buf_a, self.buf_b, self.buf_up, self.buf_dn = bufs
         self.local, self.send_a, self.recv_a, self.send_b, self.recv_b, self.send_c, self.recv_up, self.recv_dn = sems
         self.parts, self.rows = out.shape[:2]
         z = here.z
         self.order = (3 * (1 - z // 2), (3 * z + 2) % 5, 1 + z % 2, z)
 
+    def spot(self, z, y, c):
+        if self.grads is None:
+            return z, (y * 2 + c) * self.rows
+        return z * 2 + y, 0
+
+    def own(self, z, y, c=None):
+        at, base = self.spot(z, y, self.here.c if c is None else c)
+        return self.held.at[at, :, pl.ds(pl.multiple_of(base, 16), self.rows)]
+
     def block(self, z, y, c):
+        if self.grads is None:
+            return self.own(z, y, c)
         at = pl.multiple_of(self.here.at(z, y, c) * self.rows, self.rows)
         return self.grads.at[:, pl.ds(at, self.rows)]
 
@@ -708,25 +719,27 @@
         return remote(self.block(z, y, 1 - here.c), self.buf_a.at[at], self.send_a.at[at], self.recv_a.at[at], dp=here.core())
 
     def take(self, z, y):
-        at = z * 2 + y
-        return pltpu.make_async_copy(self.block(z, y, self.here.c), self.mine.at[at], self.local.at[at])
+        return pltpu.make_async_copy(self.block(z, y, self.here.c), self.own(z, y), self.local.at[z * 2 + y])
 
     def copy_b(self, z):
         here = self.here
-        return remote(self.mine.at[z * 2 + 1 - here.y], self.buf_b.at[z], self.send_b.at[z], self.recv_b.at[z], dp=here.side())
+        return remote(self.own(z, 1 - here.y), self.buf_b.at[z], self.send_b.at[z], self.recv_b.at[z], dp=here.side())
 
     def copy_up(self, z):
-        return remote(self.mine.at[z * 2 + self.here.y], self.buf_up.at[z], self.send_c.at[z], self.recv_up.at[z], dp=self.here.up())
+        return remote(self.own(z, self.here.y), self.buf_up.at[z], self.send_c.at[z], self.recv_up.at[z], dp=self.here.up())
 
     def copy_dn(self, z):
-        return remote(self.mine.at[z * 2 + self.here.y], self.buf_dn.at[z], self.send_c.at[z], self.recv_dn.at[z], dp=self.here.down())
-
-    def add(self, at, buf, slot):
+        return remote(self.own(z, self.here.y), self.buf_dn.at[z], self.send_c.at[z], self.recv_dn.at[z], dp=self.here.down())
+
+    def add(self, z, y, buf, slot):
+        at, base = self.spot(z, y, self.here.c)
+
         def rows(n, carry):
             piece = pl.ds(pl.multiple_of(n * 16, 16), 16)
+            held = pl.ds(pl.multiple_of(base + n * 16, 16), 16)
             for part in range(self.parts):
-                total = self.mine[at, part, piece].astype(f32) + buf[slot, part, piece].astype(f32)
-                self.mine[at, part, piece] = total.astype(bf16)
+                total = self.held[at, part, held].astype(f32) + buf[slot, part, piece].astype(f32)
+                self.held[at, part, held] = total.astype(bf16)
             return carry
 
         lax.fori_loop(0, self.rows // 16, rows, 0)
@@ -738,37 +751,30 @@
                 self.copy_a(z, side).start()
                 self.take(z, side).start()
 
-    def cores(self, n):
+    def join(self, z, y):
+        if self.grads is not None:
+            self.take(z, y).wait()
+        self.copy_a(z, y).wait_recv()
+        self.add(z, y, self.buf_a, z * 2 + y)
+
+    def cores(self, z):
+        self.join(z, 1 - self.here.y)
+        self.copy_b(z).start()
+
+    def stay(self, z):
+        self.join(z, self.here.y)
+
+    def sides(self, z):
+        self.copy_b(z).wait_recv()
+        self.add(z, self.here.y, self.buf_b, z)
+
+    def pass_on(self, z):
         here = self.here
-        z = self.order[n]
-        at = z * 2 + 1 - here.y
-        self.take(z, 1 - here.y).wait()
-        self.copy_a(z, 1 - here.y).wait_recv()
-        self.add(at, self.buf_a, at)
-        self.copy_b(z).start()
-
-    def stay(self, n):
-        here = self.here
-        z = self.order[n]
-        at = z * 2 + here.y
-        self.take(z, here.y).wait()
-        self.copy_a(z, here.y).wait_recv()
-        self.add(at, self.buf_a, at)
-
-    def sides(self, n):
-        z = self.order[n]
-        self.copy_b(z).wait_recv()
-        self.add(z * 2 + self.here.y, self.buf_b, z)
-
-    def pass_on(self, n):
-        here = self.here
-        z = self.order[n]
-        at = z * 2 + here.y
 
         def up():
             def below():
                 self.copy_up(z).wait_recv()
-                self.add(at, self.buf_up, z)
+                self.add(z, here.y, self.buf_up, z)
 
             pl.when(here.z > 0)(below)
             self.copy_up(z).start()
@@ -776,7 +782,7 @@
         def down():
             def above():
                 self.copy_dn(z).wait_recv()
-                self.add(at, self.buf_dn, z)
+                self.add(z, here.y, self.buf_dn, z)
 
             pl.when(here.z < 3)(above)
             self.copy_dn(z).start()
@@ -787,21 +793,21 @@
     def finish(self):
         here = self.here
         z = here.z
-        at = z * 2 + here.y
+        at, base = self.spot(z, here.y, here.c)
         pl.when(z > 0)(lambda: self.copy_up(z).wait_recv())
         pl.when(z < 3)(lambda: self.copy_dn(z).wait_recv())
 
         def rows(n, carry):
             piece = pl.ds(pl.multiple_of(n * 16, 16), 16)
+            held = pl.ds(pl.multiple_of(base + n * 16, 16), 16)
             for part in range(self.parts):
                 below = jnp.where(z > 0, self.buf_up[z, part, piece].astype(f32), 0.0)
                 above = jnp.where(z < 3, self.buf_dn[z, part, piece].astype(f32), 0.0)
-                self.out[part, piece] = self.mine[at, part, piece].astype(f32) + below + above
+                self.out[part, piece] = self.held[at, part, held].astype(f32) + below + above
             return carry
 
         lax.fori_loop(0, self.rows // 16, rows, 0)
-        for n in range(4):
-            zn = self.order[n]
+        for zn in self.order:
             self.copy_a(zn, 0).wait_send()
             self.copy_a(zn, 1).wait_send()
             self.copy_b(zn).wait_send()
@@ -809,18 +815,31 @@
             pl.when(zn < z)(lambda zn=zn: self.copy_dn(zn).wait_send())
 
 
-def reduce_scratch(*block):
+def reduce_scratch(parts, rows, cols, by_z=False):
     sem = pltpu.SemaphoreType.DMA
+    block = (parts, rows, cols)
+    held = (4, parts, 4 * rows, cols) if by_z else (8,) + block
     return [
-        pltpu.VMEM((8,) + block, bf16), pltpu.VMEM((8,) + block, bf16), pltpu.VMEM((4,) + block, bf16),
+        pltpu.VMEM(held, bf16), pltpu.VMEM((8,) + block, bf16), pltpu.VMEM((4,) + block, bf16),
         pltpu.VMEM((4,) + block, bf16), pltpu.VMEM((4,) + block, bf16),
         sem((8,)), sem((8,)), sem((8,)), sem((4,)), sem((4,)), sem((4,)), sem((4,)), sem((4,)),
     ]
 
 
-def tail_kernel(grads, small, mixed, out, small_out, far_out, *scratch):
+def tail_kernel(
+    normed_t, dinner, dsd, dgate, wb, wa, small, gn_out, shard_out, small_out,
+    nt_v, dinner_v, dsd_v, dgate_v, wg_v, wa_v, away, came, total, landed, loads, send_x, recv_x, send, recv, *scratch,
+):
     here = Place()
     half = lax.axis_index("tensor")
+    units = dgate.shape[1]
+    sources = (normed_t, dinner, dsd, dgate, wb.at[:, :units], wa)
+    pending = [
+        pltpu.make_async_copy(src, dst, loads.at[n])
+        for n, (src, dst) in enumerate(zip(sources, (nt_v, dinner_v, dsd_v, dgate_v, wg_v, wa_v)))
+    ]
+    for copy in pending:
+        copy.start()
     far = pltpu.get_barrier_semaphore()
     partners = [here.me + bit - 2 * bit * ((here.me // bit) % 2) for bit in (1, 2, 4, 8)]
     for partner in partners:
@@ -830,50 +849,117 @@
     pl.when(here.z == 1)(lambda: pl.semaphore_signal(far, 1, device_id={"dp": here.up()}, device_id_type=MESH))
     pl.when(here.z == 2)(lambda: pl.semaphore_signal(far, 1, device_id={"dp": here.down()}, device_id_type=MESH))
     pl.semaphore_wait(far, 5 + middle.astype(jnp.int32))
-    work = Reduce(here, grads, out, scratch[:5], scratch[5:13])
-    total, landed, send, recv, send_x, recv_x = scratch[13:]
-    rows = far_out.shape[0]
-    other = mixed.at[pl.ds(pl.multiple_of((1 - half) * rows, rows), rows)]
-    across = remote(other, far_out, send_x, recv_x, tensor=1 - half)
-    across.start()
+    work = Reduce(here, None, shard_out, scratch[:5], scratch[5:])
+    order = work.order
+    rows = gn_out.shape[0]
+    chunks, _, wide = away.shape
+
+    def swap(k):
+        return remote(total.at[k], landed.at[k], send.at[k], recv.at[k], dp=partners[k])
+
+    def swapped(k):
+        swap(k).wait()
+        total[k + 1] = total[k] + landed[k]
+        if k < 3:
+            swap(k + 1).start()
+
+    def across(n):
+        return remote(away.at[n], came.at[n], send_x.at[n], recv_x.at[n], tensor=1 - half)
+
+    def pulled(which, n):
+        mine = pl.ds(pl.multiple_of(which * rows, rows), rows)
+        at = pl.ds(pl.multiple_of(n * wide, wide), wide)
+        return (
+            mm(dgate_v[mine], wg_v[at], 1, 1)
+            + mm(dinner_v[mine], wa_v[at, :units], 1, 1)
+            + mm(dsd_v[mine], wa_v[at, units:], 1, 1)
+        )
+
+    def far_chunk(n, carry):
+        away[n] = pulled(1 - half, n).astype(bf16)
+        across(n).start()
+        return carry
+
+    def near_chunk(n, carry):
+        gn_out[:, pl.ds(pl.multiple_of(n * wide, wide), wide)] = pulled(half, n)
+        return carry
+
+    def grads(n, carry):
+        z = jnp.where(n == 0, order[0], jnp.where(n == 1, order[1], jnp.where(n == 2, order[2], order[3])))
+        count = 4 * work.rows
+        left = nt_v[pl.ds(pl.multiple_of(z * count, count), count)]
+        work.held[z, 0, :, :units] = mm(left, dinner_v[...]).astype(bf16)
+        work.held[z, 0, :, units:] = mm(left, dsd_v[...]).astype(bf16)
+        work.copy_a(z, 1 - here.y).start()
+        work.copy_a(z, here.y).start()
+
+        @pl.when(n == 0)
+        def _():
+            for copy in pending[3:]:
+                copy.wait()
+
+        far_chunk(n, carry)
+        work.cores(z)
+        return carry
+
     total[0] = small[...]
-    for k in range(4):
-        if k == 0:
-            work.start()
-        swap = remote(total.at[k], landed.at[k], send.at[k], recv.at[k], dp=partners[k])
-        swap.start()
-        if k == 0:
-            for n in range(4):
-                work.cores(n)
-            for n in range(4):
-                work.stay(n)
-        else:
-            work.sides(k - 1)
-            work.pass_on(k - 1)
-        swap.wait()
-        total[k + 1] = total[k] + landed[k]
+    swap(0).start()
+    for copy in pending[:3]:
+        copy.wait()
+    lax.fori_loop(0, 4, grads, 0)
+    swapped(0)
+    work.stay(order[0])
+    work.sides(order[0])
+    pl.when(~middle)(lambda: work.pass_on(order[0]))
+    lax.fori_loop(4, chunks, far_chunk, 0)
+    swapped(1)
+    for n in range(1, 4):
+        work.stay(order[n])
+    work.sides(order[1])
+    pl.when(~middle)(lambda: work.pass_on(order[1]))
+    lax.fori_loop(0, 3, near_chunk, 0)
+    swapped(2)
+    pl.when(middle)(lambda: work.pass_on(order[0]))
+    work.sides(order[2])
+    pl.when(~middle)(lambda: work.pass_on(order[2]))
+    lax.fori_loop(3, chunks, near_chunk, 0)
+    swapped(3)
     small_out[...] = total[4]
-    work.sides(3)
+    pl.when(middle)(lambda: work.pass_on(order[1]))
+    work.sides(order[3])
+    pl.when(middle)(lambda: work.pass_on(order[2]))
     work.finish()
-    across.wait()
-
-
-def reduce_tail(grads, ways, small, mixed, collective_id):
-    parts, rows, cols = grads.shape[0], grads.shape[1] // ways, grads.shape[2]
-    tokens, width = mixed.shape
+
+    def arrive(n, carry):
+        across(n).wait()
+        at = pl.ds(pl.multiple_of(n * wide, wide), wide)
+        gn_out[:, at] = gn_out[:, at] + came[n].astype(f32)
+        return carry
+
+    lax.fori_loop(0, chunks, arrive, 0)
+
+
+def reduce_tail(normed_t, dinner, dsd, dgate, wb, wa, small, ways, collective_id):
+    width, tokens = normed_t.shape
+    units, cols, rows = dgate.shape[1], wa.shape[1], width // ways
+    chunks = width // BW
     vmem = pl.BlockSpec(memory_space=pltpu.VMEM)
     hbm = pl.BlockSpec(memory_space=pl.ANY)
     sem = pltpu.SemaphoreType.DMA
     return pl.pallas_call(
-        tail_kernel, name="tail", in_specs=[hbm, vmem, hbm], out_specs=[vmem, vmem, hbm],
-        out_shape=[sds((parts, rows, cols)), sds(small.shape), sds((tokens // 2, width), bf16)],
-        scratch_shapes=reduce_scratch(parts, rows, cols) + [
-            pltpu.VMEM((5,) + small.shape, f32), pltpu.VMEM((4,) + small.shape, f32), sem((4,)), sem((4,)), sem, sem,
-        ],
+        tail_kernel, name="tail", in_specs=[hbm] * 6 + [vmem], out_specs=[vmem] * 3,
+        out_shape=[sds((tokens // 2, width)), sds((1, rows, cols)), sds(small.shape)],
+        scratch_shapes=[
+            pltpu.VMEM(normed_t.shape, bf16), pltpu.VMEM(dinner.shape, bf16), pltpu.VMEM(dsd.shape, bf16),
+            pltpu.VMEM(dgate.shape, bf16), pltpu.VMEM((width, units), bf16), pltpu.VMEM(wa.shape, bf16),
+            pltpu.VMEM((chunks, tokens // 2, BW), bf16), pltpu.VMEM((chunks, tokens // 2, BW), bf16),
+            pltpu.VMEM((5,) + small.shape, f32), pltpu.VMEM((4,) + small.shape, f32),
+            sem((6,)), sem((chunks,)), sem((chunks,)), sem((4,)), sem((4,)),
+        ] + reduce_scratch(1, rows, cols, True),
         compiler_params=pltpu.CompilerParams(
-            collective_id=collective_id, has_side_effects=True, vmem_limit_bytes=60 * 1024 * 1024
+            collective_id=collective_id, has_side_effects=True, vmem_limit_bytes=62 * 1024 * 1024
         ),
-    )(grads, small, mixed)
+    )(normed_t, dinner, dsd, dgate, wb, wa, small)
 
 
 def swap(v):
@@ -1003,7 +1089,7 @@
     if not own_links:
         stats = stats + swap(stats)
 
-    dy, dgate, ng, ggg, grad_b = pl.pallas_call(
+    dy, dgate, ng, ggg, grad_b, normed_t = pl.pallas_call(
         functools.partial(gate_backward, float(unit_total)),
         name="gate_backward",
         grid=(blocks,),
@@ -1013,13 +1099,13 @@
         ],
         out_specs=[
             by_cols(tokens), by_cols(tokens), by_cols(tokens), by_cols(8),
-            pl.BlockSpec((2, width, BW), lambda i: (0, 0, i)),
+            pl.BlockSpec((2, width, BW), lambda i: (0, 0, i)), once((width, tokens)),
         ],
         out_shape=[
             sds((tokens, units), bf16), sds((tokens, units), bf16), sds((tokens, units), bf16), sds((8, units)),
-            sds((2, width, units), bf16),
+            sds((2, width, units), bf16), sds((width, tokens), bf16),
         ],
-        scratch_shapes=[pltpu.VMEM((tokens, 128), f32), pltpu.VMEM((width, tokens), bf16), pltpu.VMEM((width, tokens), bf16)],
+        scratch_shapes=[pltpu.VMEM((tokens, 128), f32), pltpu.VMEM((width, tokens), bf16)],
         compiler_params=params(),
         cost_estimate=pl.CostEstimate(flops=4 * tokens * units * width, bytes_accessed=45_000_000, transcendentals=tokens * units),
     )(stats, gate, ssd, ggo, gain8, normed, cot)
@@ -1061,21 +1147,18 @@
         wb_shard = lax.psum_scatter(grad_b, "dp", scatter_dimension=1, tiled=True).astype(f32)
     output = (rows_in + mixed_near.astype(f32) + mixed_got.astype(f32)).astype(bf16)
 
-    grad_wi = mm(normed, dinner, 0, 0).astype(bf16)
-    grad_ws = mm(normed, dsd, 0, 0).astype(bf16)
-    grad_a = jnp.concatenate([grad_wi, grad_ws], axis=1)
-    tail = jnp.concatenate([gks[:5].reshape(-1), hs[:, 0], hs[:, 1], jnp.zeros((units - 5 * BW - 96,), f32)])
-    small = jnp.concatenate([gk[:6], ggg[:1], tail[None]], axis=0)
-    pulled = (mm(dgate, wb[:, :units], 1, 1) + mm(dinner, wa[:, :units], 1, 1) + mm(dsd, wa[:, units:], 1, 1)).astype(bf16)
-    near, far = halves(pulled, 0)
+    last = jnp.concatenate([gks[:5].reshape(-1), hs[:, 0], hs[:, 1], jnp.zeros((units - 5 * BW - 96,), f32)])
+    small = jnp.concatenate([gk[:6], ggg[:1], last[None]], axis=0)
     if own_links:
-        wa_shard, small, got = reduce_tail(grad_a[None], ways, small, pulled, 5)
+        grad_normed, wa_shard, small = reduce_tail(normed_t, dinner, dsd, dgate, wb, wa, small, ways, 5)
         wa_shard = wa_shard[0]
     else:
+        grad_a = jnp.concatenate([mm(normed_t, dinner).astype(bf16), mm(normed_t, dsd).astype(bf16)], axis=1)
+        pulled = mm(dgate, wb[:, :units], 1, 1) + mm(dinner, wa[:, :units], 1, 1) + mm(dsd, wa[:, units:], 1, 1)
+        near, far = halves(pulled.astype(bf16), 0)
         wa_shard = lax.psum_scatter(grad_a, "dp", scatter_dimension=0, tiled=True).astype(f32)
         small = lax.psum(small, "dp")
-        got = swap(far)
-    grad_normed = near.astype(f32) + got.astype(f32)
+        grad_normed = near.astype(f32) + swap(far).astype(f32)
     grad_v = grad_normed * norm_gain
     grad_residual = cotangent.astype(f32) + rstd_in * (
         grad_v - scaled * jnp.mean(grad_v * scaled, axis=1, keepdims=True)

time: 383 us -> 350 us (0.914)
  matrix products: 46.9 us -> 9.26 us
  Pallas kernels: 288 us -> 295 us
    dot_general x6 -> x1, matrix products: 46.9 us -> 9.26 us  [mm(): lax.dot_general(a, b, (((ca,), (cb,)), ((), ())), preferred_element_type=...]
    pallas_call x1, Pallas kernels: 59.5 us -> 67.1 us  [reduce_tail(): pl.pallas_call(tail_kernel, name='tail', in_specs=[hbm] * 6 + [vmem], out...]
  transfers between devices with their start and end apart: 1 -> 1, of which waited for: 0 -> 0; matrix products, arithmetic and copies ran while one was open for 5% -> 4% of each run, Pallas kernels for 0% -> 0%
where the time goes in v5:
time: 350 us; the launch traced here: 349 us
  Pallas kernels  295 us (84%)
  other arithmetic  21.9 us (6%)
  local copies, waits for them, and re-layouts  19.8 us (6%)
  matrix products  9.26 us (3%)
    pallas_call x1, Pallas kernels, on_device(): pl.pallas_call(functools.partial(mixer_backward, own_links), name='mixer_...  76.7 us
    pallas_call x1, Pallas kernels, reduce_tail(): pl.pallas_call(tail_kernel, name='tail', in_specs=[hbm] * 6 + [vmem], out...  67.1 us
    pallas_call x1, Pallas kernels, on_device(): pl.pallas_call(functools.partial(mixer_forward, own_links), name='mixer_f...  62.5 us
    pallas_call x1, Pallas kernels, gather_rows(): pl.pallas_call(gather_kernel, name='gather_rows', in_specs=[vmem, vmem, v...  42.1 us
    pallas_call x1, Pallas kernels, on_device(): pl.pallas_call(functools.partial(gate_backward, float(unit_total)), name=...  24.1 us
    pallas_call x1, Pallas kernels, on_device(): pl.pallas_call(functools.partial(gate_forward, own_links), name='gate_for...  22.9 us
    dot_general x1, matrix products, mm(): lax.dot_general(a, b, (((ca,), (cb,)), ((), ())), preferred_element_type=...  9.26 us
  transfers between devices with their start and end apart: 1, of which 0 were waited for; matrix products, arithmetic and copies ran while one was open for 4% of the time, Pallas kernels for 0%

profile of v5, /device:TPU:0, one launch (start us, length us, event | category | flops | bytes accessed | tf_op | source)
XLA Modules:
  0.0 348.7 jit_solution(4144902133830580138)
XLA Ops:
  0.7 1.1 slice_bitcast_fusion.2
  1.8 0.7 pad_bitcast_fusion
  2.5 0.1 copy.28
  2.6 1.3 broadcast_in_dim.40.gain
  3.9 0.7 exponential_negate_fusion
  4.7 0.7 reshape.85
  5.5 0.7 broadcast_in_dim.41
  6.5 1.3 concatenate.29.kst
  7.8 1.8 pad_maximum_fusion.1.refs_1_
  9.6 1.6 fusion.16.pack
  11.2 42.1 %gather_rows.1 = (bf16[1024,1536]{1,0:T(8,128)(2,1)}, bf16[1536,1920]{1,0:T(8,128)(2,1)}) custom-call(bf16[512,1536]{1,0:T(8,128)(2,1)} %tokens_in.1, f32[1,1536]{1,0:T(1,128)} %broadcast_in_dim.40.gain, bf16[96,1920]{1,0:T(8,128)(2,1)} %fusion.16.pack), custom_call_target="tpu_custom_call" | custom-call | tf_op jit(solution)/shard_map/gather_rows/pallas_call | solution.py:677
  53.3 0.7 maximum_maximum_fusion.1.hp
  54.0 0.7 maximum_maximum_fusion.kin
  54.6 62.5 %mixer_forward.1 = (f32[1024,1536]{1,0:T(8,128)}, f32[1024,1536]{1,0:T(8,128)}, f32[4,1536,128]{2,1,0:T(8,128)}, f32[1024,256]{1,0:T(8,128)}, bf16[1024,256]{1,0...) custom-call(bf16[1024,1536]{1,0:T(8,128)(2,1)} %get-tuple-element.46, ...), custom_call_target="tpu_custom_call" | custom-call | flops 7650410496 | bytes 30000000 | tf_op jit(solution)/shard_map/mixer_forward/pallas_call | solution.py:1041
  117.1 0.6 broadcast_in_dim.46.gain
  117.8 22.9 %gate_forward.1 = (f32[1024,1536]{1,0:T(8,128)}, f32[1024,1536]{1,0:T(8,128)}, f32[8,1024]{1,0:T(8,128)}) custom-call(bf16[1024,1536]{1,0:T(8,128)(2,1)} %get-tuple-element.46.normed, bf16[1024,1536]{1,0:T(8,128)(2,1)} %get-tuple-element.48.cot, bf16[1536,3072]{1,0:T(8,128)(2,1)} %get-tuple-element.49.wg.wo.wb, ...), custom_call_target="tpu_custom_call" | custom-call | flops 9663676416 | bytes 35000000 | tf_op jit(solution)/shard_map/gate_forward/pallas_call | solution.py:1074
  140.7 24.1 %gate_backward.1 = (bf16[1024,1536]{1,0:T(8,128)(2,1)}, bf16[1024,1536]{1,0:T(8,128)(2,1)}, bf16[1024,1536]{1,0:T(8,128)(2,1)}, f32[8,1536]{1,0:T(8,128)}, bf16[...) custom-call(f32[8,1024]{1,0:T(8,128)} %get-tuple-element.51.stats, f32[1024,1536]{1,0:T(8,128)} %get-tuple-element.52.gate, ...), custom_call_target="tpu_custom_call" | custom-call | flops 9663676416 | bytes 45000000 | tf_op jit(solution)/shard_map/gate_backward/pallas_call | solution.py:1092
  164.8 9.3 %fusion.2.refs_0_ = bf16[1024,1536]{1,0:T(8,128)(2,1)} fusion(bf16[1024,1536]{1,0:T(8,128)(2,1)} %get-tuple-element.54, bf16[1536,3072]{1,0:T(8,128)(2,1)} %get-tuple-element.49.wg.wo.wb), kind=kOutput, calls=%fused_computation.5 | convolution fusion | flops 4833411072 | bytes 11010048 | tf_op jit(solution)/shard_map/dot_general | solution.py:24
  174.0 0.7 broadcast_in_dim.47.rateT
  174.7 76.7 %mixer_backward.1 = (bf16[1024,1536]{1,0:T(8,128)(2,1)}, f32[8,1536]{1,0:T(8,128)}, bf16[1024,384]{1,0:T(8,128)(2,1)}, f32[8,256]{1,0:T(8,128)}, f32[48,128]{1,0...) custom-call(f32[1024,1536]{1,0:T(8,128)} %get-tuple-element.55.inner, ...), custom_call_target="tpu_custom_call" | custom-call | flops 40000000000 | bytes 30000000 | tf_op jit(solution)/shard_map/mixer_backward/pallas_call | solution.py:1116
  251.4 0.7 reshape.89
  252.1 1.0 slice_reduce_fusion
  253.2 0.8 slice.87
  254.0 1.4 pad_maximum_fusion.3.small
  255.4 67.1 %tail.1 = (f32[512,1536]{1,0:T(8,128)}, f32[1,96,1920]{2,1,0:T(8,128)}, f32[8,1536]{1,0:T(8,128)}) custom-call(bf16[1536,1024]{1,0:T(8,128)(2,1)} %get-tuple-element.67.normed_t, bf16[1024,1536]{1,0:T(8,128)(2,1)} %get-tuple-element.68.dinner, bf16[1024,384]{1,0:T(8,128)(2,1)} %get-tuple-element.69.dsd, bf16[1024,1536]{1,0:T(8,128)(2,1)} %get-tuple-element.70.dgate, ...), custom_call_target="tpu_custom_call" | custom-call | tf_op jit(solution)/shard_map/tail/pallas_call | solution.py:949
  322.6 1.4 multiply_reduce_fusion
  324.0 0.9 slice.109
  324.9 0.8 slice_reduce_fusion.4
  325.7 1.1 fusion.15
  327.1 0.6 pad_maximum_fusion.2
  327.7 1.5 collective-permute-start
  329.2 1.1 slice_bitcast_fusion
  330.3 1.1 slice_bitcast_fusion.1
  331.4 0.4 fusion.13
  331.8 0.6 slice_reduce_fusion.2
  332.4 0.7 fusion.7
  333.2 1.1 pad_maximum_fusion
  334.2 6.9 %fusion.10 = (f32[512,1536]{1,0:T(8,128)}, bf16[512,1536]{1,0:T(8,128)(2,1)}) fusion(bf16[512,1536]{1,0:T(8,128)(2,1)S(1)} %copy-done, bf16[512,1536]{1,0:T(8,128)(2,1)} %refs_0_.1, f32[512,1536]{1,0:T(8,128)} %get-tuple-element.75, f32[512]{0:T(512)S(1)} %broadcast_multiply_fusion, f32[1536]{0:T(1024)S(1)} %copy-done.6, f32[512]{0:T(512)S(1)} %add_rsqrt_fusion, ...), kind=kLoop, calls=%fused_computation.11 | loop fusion | flops 10223616 | bytes 14166020 | tf_op jit(solution)/shard_map/add | solution.py:1163
  341.2 0.8 slice.114
  342.1 0.6 slice.115
  342.8 0.6 reduce_sum.49
  343.5 0.6 reshape.94
  344.2 0.6 reshape.95
  344.8 0.8 fusion.18
  345.6 0.6 slice.113
  346.2 0.6 slice.116
  346.8 1.2 slice_add_fusion
  348.0 0.6 copy.31
  (44 shorter events, 1.2 us)
Async XLA Ops:
  0.6 53.3 %copy-start.7 = (f32[5,1536]{1,0:T(8,128)S(1)}, f32[5,1536]{1,0:T(8,128)}, u32[]{:S(2)}) copy-start(f32[5,1536]{1,0:T(8,128)} %param.18) | copy-start | bytes 92164
  54.6 62.5 %copy-start.8 = (f32[1536]{0:T(1024)S(1)}, f32[1536]{0:T(1024)}, u32[]{:S(2)}) copy-start(f32[1536]{0:T(1024)} %param.23) | copy-start | bytes 18436
  255.4 67.1 %copy-start.4 = (bf16[96,256]{1,0:T(8,128)(2,1)S(1)}, bf16[96,256]{1,0:T(8,128)(2,1)}, u32[]{:S(2)}) copy-start(bf16[96,256]{1,0:T(8,128)(2,1)} %param.16) | copy-start | bytes 147460
  255.4 70.3 %copy-start.2 = (f32[2,96,1536]{2,1,0:T(8,128)S(1)}, f32[2,96,1536]{2,1,0:T(8,128)}, u32[]{:S(2)}) copy-start(f32[2,96,1536]{2,1,0:T(8,128)} %get-tuple-element.76) | copy-start | bytes 3538948
  255.4 71.4 %copy-start.6 = (f32[1536]{0:T(1024)S(1)}, f32[1536]{0:T(1024)}, u32[]{:S(2)}) copy-start(f32[1536]{0:T(1024)} %param.14) | copy-start | bytes 18436
  322.5 8.9 %copy-start = (bf16[512,1536]{1,0:T(8,128)(2,1)S(1)}, bf16[512,1536]{1,0:T(8,128)(2,1)}, u32[]{:S(2)}) copy-start(bf16[512,1536]{1,0:T(8,128)(2,1)} %tokens_in.1) | copy-start | bytes 4718596
  325.7 6.1 %copy-start.5 = (f32[8,1536]{1,0:T(8,128)S(1)}, f32[8,1536]{1,0:T(8,128)}, u32[]{:S(2)}) copy-start(f32[8,1536]{1,0:T(8,128)} %get-tuple-element.78) | copy-start | bytes 147460
  326.9 5.6 %copy-start.1 = (f32[512,1536]{1,0:T(8,128)S(1)}, f32[512,1536]{1,0:T(8,128)}, u32[]{:S(2)}) copy-start(f32[512,1536]{1,0:T(8,128)} %get-tuple-element.75) | copy-start | bytes 9437188
  327.7 17.1 %collective-permute-start = (f32[12976]{0:T(1024)}, f32[12976]{0:T(1024)}, u32[]{:S(2)}, u32[]{:S(2)}) collective-permute-start(f32[12976]{0:T(1024)} %pad_maximum_fusion.2), channel_id=1, source_target_pairs={{0,1},{1,0},{2,3},{3,2},{4,5},{5,4},{6,7},{7,6},{8,9},{9,8},{10,11... | collective-permute-start | bytes 155720 | tf_op jit(solution)/shard_map/ppermute | solution.py:966
  331.4 1.7 copy-start.3

commit v6 on v5

--- a/solution.py
+++ b/solution.py
@@ -61,6 +61,25 @@
     return out
 
 
+def head_row(ref):
+    return jnp.broadcast_to(ref[...][None, :], (8, ref.shape[0]))
+
+
+def lay(rows, pick):
+    parts = split3(rows)
+    return mm(parts[0], pick) + mm(parts[1], pick) + mm(parts[2], pick)
+
+
+def as_places(heads):
+    lane = iota((heads, 128), 1)
+    place = lane % 8
+    return ((lane // 8 * HB + place == iota((heads, 128), 0)) & (place < HB)).astype(f32).astype(bf16)
+
+
+def as_units(heads, block):
+    return (iota((heads, BW), 1) // HEAD + HB * block == iota((heads, BW), 0)).astype(f32).astype(bf16)
+
+
 def head_masks():
     lane = iota((1, BW), 1) // HEAD
     return [(lane == j).astype(f32).astype(bf16) for j in range(HB)]
@@ -81,18 +100,19 @@
     return jnp.exp2(gap)
 
 
-def mixer_forward(links, normed, wi, wsx, kin, kst, hp, *refs):
+def mixer_forward(links, normed, wi, wsx, kin, kst, bias, log_rate, skip_in, *refs):
     refs = list(refs)
     if links:
-        cot, pack = refs[:2]
-        cot_out, wb = refs[12:14]
-        refs = refs[2:12] + refs[14:]
+        sent = refs[:3] + refs[13:15]
+        refs = refs[3:13] + refs[15:]
     inner_out, ssd_out, states_out, cst_out, bc_out, step_out, cum_out, stepT_out, cumT_out, preT_out = refs[:10]
     buf, gram, colc, cols, rowp, mst, xst, state = refs[10:18]
     i = pl.program_id(0)
     tokens = normed.shape[0]
     spans = tokens // Q
-    work = BesideForward(cot, pack, cot_out, wb, *refs[18:]) if links else None
+    work = BesideForward(*sent, *refs[18:]) if links else None
+    heads = bias.shape[0]
+    skip = lay(head_row(skip_in), as_units(heads, i))[0:1]
 
     if links:
         pl.when(i == 0)(work.start)
@@ -104,10 +124,11 @@
         cst_out[...] = proj[:, :BW]
         buf[8 : 8 + tokens] = proj[:, :BW]
         tri = (iota((Q, Q), 0) >= iota((Q, Q), 1)).astype(f32).astype(bf16)
-        pre = proj[:, BW:] + hp[0:1]
+        places = as_places(heads)
+        pre = proj[:, BW:] + lay(head_row(bias), places)[0:1]
         step = jnp.maximum(pre, 0.0) + jnp.log1p(jnp.exp(-jnp.abs(pre)))
         step_out[...] = step
-        scaled = step * (hp[1:2] * LOG2E)
+        scaled = step * (lay(-jnp.exp(head_row(log_rate)), places)[0:1] * LOG2E)
         for s in range(spans):
             parts = split3(scaled[s * Q : s * Q + Q])
             cum_out[s * Q : s * Q + Q] = mm(tri, parts[0]) + mm(tri, parts[1]) + mm(tri, parts[2])
@@ -154,7 +175,7 @@
         states_out[s] = state_in
         bc = bc_out[rows]
         readout = mm(bc[:, 128:], state_in.astype(bf16), 1, 1)
-        ssd_out[rows] = intra + growth * readout + kin[5:6] * xs
+        ssd_out[rows] = intra + growth * readout + skip * xs
         local = mm(xw_low, bc[:, :128], 0, 0)
         fade = jnp.exp2(total)
         for j in range(HB):
@@ -170,22 +191,24 @@
 
 
 class BesideForward:
-    def __init__(self, cot, pack, cot_out, wb, ss, rs, xs, xr, ls):
+    def __init__(self, cot, w_gate_inner, w_output_t, cot_out, wb, ss, rs, ls, xs, xr, xl):
         self.here = Place()
-        self.moves = gathers(self.here, pack, wb, ss, rs)
-        self.own = own_rows(self.here, pack, wb, ls.at[0])
+        units = w_output_t.shape[1]
+        self.moves = [
+            Gather(self.here, own, wb, ss, rs, ls, n, slice(n * units, n * units + units))
+            for n, own in enumerate((w_gate_inner.at[0], w_output_t))
+        ]
         half = lax.axis_index("tensor")
         rows = cot.shape[0]
         slot = cot_out.at[pl.ds(pl.multiple_of(half * rows, rows), rows)]
         self.across = remote(cot, slot, xs, xr, tensor=1 - half)
-        self.local = pltpu.make_async_copy(cot, slot, ls.at[1])
+        self.local = pltpu.make_async_copy(cot, slot, xl)
 
     def start(self):
         greet(self.here, True)
         for move in self.moves:
             move.start()
         self.across.start()
-        self.own.start()
         self.local.start()
 
     def step(self, at):
@@ -203,7 +226,6 @@
                 if hops < 4:
                     move.hop(hops)
                 move.sides(hops - 1)
-        self.own.wait()
         self.local.wait()
         self.across.wait()
         for move in self.moves:
@@ -319,7 +341,7 @@
         self.across.wait()
 
 
-def mixer_backward(links, inner, dy, states, kin, kst, hp, cst, bc_in, step_in, cum_in, stepT, cumT, preT, rateT, *refs):
+def mixer_backward(links, inner, dy, states, kin, kst, log_rate, skip_in, cst, bc_in, step_in, cum_in, stepT, cumT, preT, *refs):
     refs = list(refs)
     if links:
         beside = refs[:2] + refs[7:9]
@@ -331,6 +353,8 @@
     i = pl.program_id(0)
     if links:
         pl.when(i == 0)(work.start)
+    heads = log_rate.shape[0]
+    skip = lay(head_row(skip_in), as_units(heads, i))[0:1]
     tokens = inner.shape[0]
     spans = tokens // Q
     masks = head_masks()
@@ -356,20 +380,18 @@
     gtaps[...] = jnp.zeros(gtaps.shape, f32)
     pick = (iota((8, BW), 1) // HEAD == iota((8, BW), 0)).astype(f32).astype(bf16)
 
-    def conv_rows(at, kernel, grad_act):
-        window = buf[pl.ds(at, Q + 8)]
-        conv = conv_taps(window, kernel)
-        sig = sigmoid(conv)
+    def conv_rows(at, kernel, grad_act, conv, sig):
         gco = grad_act * (sig * (1.0 + conv * (1.0 - sig)))
         dbuf[pl.ds(at, Q)] = gco
-        for k in range(4):
-            prod = gco * (window[8:] if k == 3 else pltpu.roll(window, 3 - k, 0)[8:])
-            gtaps[k : k + 1] += jnp.sum(prod, axis=0, keepdims=True)
+        into = buf[pl.ds(pl.multiple_of(at + 8, 8), Q)]
         gtaps[4:5] += jnp.sum(gco, axis=0, keepdims=True)
         after = dbuf[pl.ds(at, Q + 8)]
         grad_in = kernel[3:4] * gco
+        gtaps[3:4] += jnp.sum(gco * into, axis=0, keepdims=True)
         for k in range(3):
-            grad_in = grad_in + kernel[k : k + 1] * pltpu.roll(after, Q + 8 - (3 - k), 0)[:Q]
+            later = pltpu.roll(after, Q + 8 - (3 - k), 0)[:Q]
+            gtaps[k : k + 1] += jnp.sum(later * into, axis=0, keepdims=True)
+            grad_in = grad_in + kernel[k : k + 1] * later
         return grad_in
 
     def span(back, carry):
@@ -377,7 +399,8 @@
         at = pl.multiple_of(s * Q, Q)
         rows = pl.ds(at, Q)
         conv = conv_taps(buf[pl.ds(at, Q + 8)], kin[...])
-        xs = conv * sigmoid(conv)
+        sig = sigmoid(conv)
+        xs = conv * sig
         x_low = xs.astype(bf16)
         dy_s = dy[rows]
         dy_f = dy_s.astype(f32)
@@ -411,7 +434,7 @@
             row_sums = jnp.where(lane == j, sums, row_sums)
             cs_t[pl.ds(8 * i + j, 1), rows] = jnp.concatenate(col_sum, axis=1)
         rs_t[rows8, rows] = jnp.transpose(row_sums)[:8]
-        grad_xs = mm(mst[...], dyst[...], 0, 0) + kin[5:6] * dy_f
+        grad_xs = mm(mst[...], dyst[...], 0, 0) + skip * dy_f
 
         growth = expand(jnp.exp2(col[:, :8]))
         weight = expand(jnp.exp2(total[:, :8] - col[:, :8]) * cols[rows][:, :8])
@@ -439,7 +462,7 @@
             at_j = slice(j * HEAD, j * HEAD + HEAD)
             sgrad[at_j] = fade[:, j : j + 1] * state_grad[at_j] + local[at_j]
         gtaps[5:6] += jnp.sum(dy_f * xs, axis=0, keepdims=True)
-        dinner_out[rows] = conv_rows(at, kin[...], grad_xs).astype(bf16)
+        dinner_out[rows] = conv_rows(at, kin[...], grad_xs, conv, sig).astype(bf16)
         if links:
             work.step(i * spans + back)
         return carry
@@ -451,7 +474,8 @@
     def _():
         buf[8 : 8 + tokens] = cst[...]
         gtaps[...] = jnp.zeros(gtaps.shape, f32)
-        rate = rateT[:, 0:1]
+        rates = lay(-jnp.exp(head_row(log_rate)), as_places(heads))[0:1]
+        rate = jnp.transpose(jnp.broadcast_to(rates, (128, 128)))[:48, 0:1]
         later = (iota((Q, Q), 0) >= iota((Q, Q), 1)).astype(f32).astype(bf16)
         last = iota((48, Q), 1) == Q - 1
         bias_sum = jnp.zeros((48, 1), f32)
@@ -464,7 +488,8 @@
             grad_c = gc[rows] + mm(gl, bc[:, :128])
             grad_b = gb[rows] + mm(gl, bc[:, 128:], 0, 0)
             both = jnp.concatenate([grad_b, grad_c], axis=1)
-            dsd_out[rows, :BW] = conv_rows(s * Q, kst[...], both).astype(bf16)
+            conv = conv_taps(buf[s * Q : s * Q + Q + 8], kst[...])
+            dsd_out[rows, :BW] = conv_rows(s * Q, kst[...], both, conv, sigmoid(conv)).astype(bf16)
 
             cum, step, pre = cumT[:, rows], stepT[:, rows], preT[:, rows]
             total = cum[:, Q - 1 : Q]
@@ -486,7 +511,8 @@
             dsd_out[rows, BW:] = jnp.transpose(full).astype(bf16)
         gks_out[...] = gtaps[...]
         lane = iota((48, 128), 1)
-        hs_out[...] = jnp.where(lane == 0, bias_sum, jnp.where(lane == 1, decay_sum * rate, 0.0))
+        both = jnp.where(lane == 0, bias_sum, jnp.where(lane == 1, decay_sum * rate, 0.0))
+        hs_out[...] = jnp.transpose(jnp.concatenate([both, jnp.zeros((80, 128), f32)], axis=0))[:8]
         if links:
             work.finish()
 
@@ -536,10 +562,11 @@
 
 
 class Gather:
-    def __init__(self, here, pack, full, ss, rs, chunk, cols):
+    def __init__(self, here, own, full, ss, rs, ls, chunk, cols):
         self.here, self.full, self.ss, self.rs, self.chunk, self.cols = here, full, ss, rs, chunk, cols
-        self.rows = pack.shape[0]
-        self.own = pack.at[:, cols]
+        self.rows = own.shape[0]
+        self.own = own
+        self.local = pltpu.make_async_copy(own, self.slot(here.me), ls.at[chunk])
 
     def slot(self, origin):
         return self.full.at[pl.ds(pl.multiple_of(origin * self.rows, self.rows), self.rows), self.cols]
@@ -582,6 +609,7 @@
         pl.when(here.z > 0)(lambda: self.copy(here.me, 1, self.own).start())
         self.copy(here.me, 2, self.own).start()
         self.copy(here.me, 3, self.own).start()
+        self.local.start()
 
     def hop(self, hops):
         here = self.here
@@ -611,6 +639,7 @@
 
     def finish(self):
         here = self.here
+        self.local.wait()
         for z in range(4):
             for y in range(2):
                 self.arrived(here.at(z, y, 1 - here.c))
@@ -619,50 +648,43 @@
             self.copy(here.at(z, 1 - here.y, here.c), 3).wait_send()
 
 
-def gathers(here, pack, full, ss, rs):
-    cols = pack.shape[1]
-    cut = cols // 256 * 128
-    return [Gather(here, pack, full, ss, rs, n, c) for n, c in enumerate((slice(0, cut), slice(cut, cols)))]
-
-
-def own_rows(here, pack, full, sem):
-    rows = pack.shape[0]
-    return pltpu.make_async_copy(pack, full.at[pl.ds(pl.multiple_of(here.me * rows, rows), rows)], sem)
-
-
 def gather_scratch():
     sem = pltpu.SemaphoreType.DMA
-    return [sem((2, 16, 4)), sem((2, 16))]
-
-
-def gather_kernel(tokens_in, gain, pack, tokens_out, full, low, ss, rs, xs, xr, ls):
+    return [sem((2, 16, 4)), sem((2, 16)), sem((2,))]
+
+
+def gather_kernel(tokens_in, gain, w_gate_inner, w_state_io, w_step, tokens_out, full, pack, low, ss, rs, ls, xs, xr, xl):
     here = Place()
     half = lax.axis_index("tensor")
     rows = tokens_in.shape[0]
+    units, cols = w_gate_inner.shape[2], full.shape[1]
+    pack[:, :units] = w_gate_inner[1]
+    pack[:, units : units + BW] = w_state_io[...]
+    pack[:, units + BW :] = mm(w_step[...], as_places(w_step.shape[1])).astype(bf16)
     greet(here, True)
-    moves = gathers(here, pack, full, ss, rs)
+    cut = cols // 256 * 128
+    moves = [
+        Gather(here, pack.at[:, c], full, ss, rs, ls, n, c) for n, c in enumerate((slice(0, cut), slice(cut, cols)))
+    ]
     for move in moves:
         move.start()
-    own = own_rows(here, pack, full, ls.at[0])
-    own.start()
     part = rows // 4
     across, local = [], []
     for n in range(4):
         piece = slice(n * part, n * part + part)
         v = tokens_in[piece].astype(f32)
         scale = lax.rsqrt(jnp.mean(v * v, axis=1, keepdims=True) + norm_eps)
-        low[piece] = (v * scale * gain[...]).astype(bf16)
+        low[piece] = (v * scale * gain[0:1]).astype(bf16)
         slot = tokens_out.at[pl.ds(pl.multiple_of(half * rows + n * part, part), part)]
         across.append(remote(low.at[piece], slot, xs.at[n], xr.at[n], tensor=1 - half))
         across[-1].start()
-        local.append(pltpu.make_async_copy(low.at[piece], slot, ls.at[n + 1]))
+        local.append(pltpu.make_async_copy(low.at[piece], slot, xl.at[n]))
         local[-1].start()
     for hops in range(1, 5):
         for move in moves:
             if hops < 4:
                 move.hop(hops)
             move.sides(hops - 1)
-    own.wait()
     for n in range(4):
         local[n].wait()
         across[n].wait()
@@ -670,24 +692,27 @@
         move.finish()
 
 
-def gather_rows(tokens_in, gain, pack, ways, collective_id):
+def gather_rows(tokens_in, gain, w_gate_inner, w_state_io, w_step, ways, collective_id):
     rows, width = tokens_in.shape
+    _, own, units = w_gate_inner.shape
+    cols = units + BW + 128
     vmem = pl.BlockSpec(memory_space=pltpu.VMEM)
     hbm = pl.BlockSpec(memory_space=pl.ANY)
+    sem = pltpu.SemaphoreType.DMA
     return pl.pallas_call(
         gather_kernel,
         name="gather_rows",
-        in_specs=[vmem, vmem, vmem],
+        in_specs=[vmem] * 5,
         out_specs=[hbm, hbm],
-        out_shape=[sds((2 * rows, width), bf16), sds((ways * pack.shape[0], pack.shape[1]), bf16)],
+        out_shape=[sds((2 * rows, width), bf16), sds((ways * own, cols), bf16)],
         scratch_shapes=[
-            pltpu.VMEM((rows, width), bf16), *gather_scratch(),
-            pltpu.SemaphoreType.DMA((4,)), pltpu.SemaphoreType.DMA((4,)), pltpu.SemaphoreType.DMA((5,)),
+            pltpu.VMEM((own, cols), bf16), pltpu.VMEM((rows, width), bf16), *gather_scratch(),
+            sem((4,)), sem((4,)), sem((4,)),
         ],
         compiler_params=pltpu.CompilerParams(
             collective_id=collective_id, has_side_effects=True, vmem_limit_bytes=60 * 1024 * 1024
         ),
-    )(tokens_in, gain, pack)
+    )(tokens_in, gain, w_gate_inner, w_state_io, w_step)
 
 
 class Reduce:
@@ -827,7 +852,7 @@
 
 
 def tail_kernel(
-    normed_t, dinner, dsd, dgate, wb, wa, small, gn_out, shard_out, small_out,
+    normed_t, dinner, dsd, dgate, wb, wa, gk, ggg, gks, hs, gn_out, shard_out, small_out,
     nt_v, dinner_v, dsd_v, dgate_v, wg_v, wa_v, away, came, total, landed, loads, send_x, recv_x, send, recv, *scratch,
 ):
     here = Place()
@@ -841,7 +866,7 @@
     for copy in pending:
         copy.start()
     far = pltpu.get_barrier_semaphore()
-    partners = [here.me + bit - 2 * bit * ((here.me // bit) % 2) for bit in (1, 2, 4, 8)]
+    partners = [here.me + bit - 2 * bit * ((here.me // bit) % 2) for bit in (2, 4, 8, 1)]
     for partner in partners:
         pl.semaphore_signal(far, 1, device_id={"dp": partner}, device_id_type=MESH)
     pl.semaphore_signal(far, 1, device_id={"tensor": 1 - half}, device_id_type=MESH)
@@ -902,23 +927,28 @@
         work.cores(z)
         return carry
 
-    total[0] = small[...]
+    total[0, 0:6] = gk[0:6]
+    total[0, 6:7] = ggg[0:1]
+    for k in range(5):
+        total[0, 7:8, k * BW : k * BW + BW] = gks[k : k + 1]
+    for k in range(2):
+        total[0, 7:8, 5 * BW + k * 128 : 5 * BW + k * 128 + 128] = hs[k : k + 1]
     swap(0).start()
     for copy in pending[:3]:
         copy.wait()
+    swapped(0)
     lax.fori_loop(0, 4, grads, 0)
-    swapped(0)
+    swapped(1)
     work.stay(order[0])
     work.sides(order[0])
     pl.when(~middle)(lambda: work.pass_on(order[0]))
     lax.fori_loop(4, chunks, far_chunk, 0)
-    swapped(1)
+    swapped(2)
     for n in range(1, 4):
         work.stay(order[n])
     work.sides(order[1])
     pl.when(~middle)(lambda: work.pass_on(order[1]))
     lax.fori_loop(0, 3, near_chunk, 0)
-    swapped(2)
     pl.when(middle)(lambda: work.pass_on(order[0]))
     work.sides(order[2])
     pl.when(~middle)(lambda: work.pass_on(order[2]))
@@ -939,15 +969,16 @@
     lax.fori_loop(0, chunks, arrive, 0)
 
 
-def reduce_tail(normed_t, dinner, dsd, dgate, wb, wa, small, ways, collective_id):
+def reduce_tail(normed_t, dinner, dsd, dgate, wb, wa, sums, ways, collective_id):
     width, tokens = normed_t.shape
+    small = sums[0]
     units, cols, rows = dgate.shape[1], wa.shape[1], width // ways
     chunks = width // BW
     vmem = pl.BlockSpec(memory_space=pltpu.VMEM)
     hbm = pl.BlockSpec(memory_space=pl.ANY)
     sem = pltpu.SemaphoreType.DMA
     return pl.pallas_call(
-        tail_kernel, name="tail", in_specs=[hbm] * 6 + [vmem], out_specs=[vmem] * 3,
+        tail_kernel, name="tail", in_specs=[hbm] * 6 + [vmem] * 4, out_specs=[vmem] * 3,
         out_shape=[sds((tokens // 2, width)), sds((1, rows, cols)), sds(small.shape)],
         scratch_shapes=[
             pltpu.VMEM(normed_t.shape, bf16), pltpu.VMEM(dinner.shape, bf16), pltpu.VMEM(dsd.shape, bf16),
@@ -959,7 +990,7 @@
         compiler_params=pltpu.CompilerParams(
             collective_id=collective_id, has_side_effects=True, vmem_limit_bytes=62 * 1024 * 1024
         ),
-    )(normed_t, dinner, dsd, dgate, wb, wa, small)
+    )(normed_t, dinner, dsd, dgate, wb, wa, *sums)
 
 
 def swap(v):
@@ -1021,19 +1052,16 @@
     rstd_in = lax.rsqrt(jnp.mean(rows_in * rows_in, axis=1, keepdims=True) + norm_eps)
     scaled = rows_in * rstd_in
     pack_a = jnp.concatenate([w_gate_inner[1], w_state_io, spread(w_step)], axis=1)
-    pack_b = jnp.concatenate([w_gate_inner[0], w_output.T], axis=1)
+    w_output_t = w_output.T
     if own_links:
-        normed, wa = gather_rows(residual, norm_gain[None], pack_a, ways, 1)
+        normed, wa = gather_rows(
+            residual, jnp.broadcast_to(norm_gain[None], (8, width)), w_gate_inner, w_state_io, w_step, ways, 1
+        )
     else:
         wa = lax.all_gather(pack_a, "dp", axis=0, tiled=True)
         normed = lax.all_gather((scaled * norm_gain).astype(bf16), "tensor", axis=0, tiled=True)
     tokens = normed.shape[0]
     spans = tokens // Q
-    rate = -jnp.exp(decay_log)
-    kin = jnp.concatenate([conv_inner, jnp.repeat(skip_gain, HEAD)[None], jnp.zeros((2, units), f32)], axis=0)
-    kst = jnp.concatenate([conv_state, jnp.zeros((3, BW), f32)], axis=0)
-    hp = jnp.concatenate([spread(step_bias)[None], spread(rate)[None], jnp.zeros((6, 128), f32)], axis=0)
-    rate_t = jnp.broadcast_to(spread(rate)[:48, None], (48, 128))
     gain8 = jnp.broadcast_to(gate_gain[None], (8, units))
 
     hbm = pl.BlockSpec(memory_space=pl.ANY)
@@ -1044,8 +1072,8 @@
         grid=(blocks,),
         in_specs=[
             once((tokens, width)), by_cols(width), once((width, 384), (0, units // 384)),
-            by_cols(8), once((8, BW)), once((8, 128)),
-        ] + [once(cotangent.shape), once(pack_b.shape)] * own_links,
+            by_cols(5), once((5, BW)), once((heads,)), once((heads,)), once((heads,)),
+        ] + [once(v.shape) for v in (cotangent, w_gate_inner, w_output_t)] * own_links,
         out_specs=[
             by_cols(tokens), by_cols(tokens), pl.BlockSpec((spans, BW, 128), lambda i: (0, i, 0)),
             once((tokens, BW)), once((tokens, BW)), once((tokens, 128)), once((tokens, 128)),
@@ -1060,15 +1088,18 @@
             pltpu.VMEM((tokens + 8, BW), f32), pltpu.VMEM((spans, Q, Q), f32),
             pltpu.VMEM((tokens, 128), f32), pltpu.VMEM((tokens, 128), f32), pltpu.VMEM((8, tokens), f32),
             pltpu.VMEM((Q, HB * Q), bf16), pltpu.VMEM((HB * Q, BW), bf16), pltpu.VMEM((BW, 128), f32),
-        ] + (gather_scratch() + [sem, sem, sem((2,))]) * own_links,
+        ] + (gather_scratch() + [sem, sem, sem]) * own_links,
         compiler_params=params(2 if own_links else None),
         cost_estimate=pl.CostEstimate(flops=2 * tokens * width * (units + 384) + 4 * tokens * 256 * units, bytes_accessed=30_000_000, transcendentals=heads * spans * Q * Q),
-    )(normed, wa, wa, kin, kst, hp, *[cotangent, pack_b] * own_links)
+    )(
+        normed, wa, wa, conv_inner, conv_state, step_bias, decay_log, skip_gain,
+        *[cotangent, w_gate_inner, w_output_t] * own_links,
+    )
 
     if own_links:
         cot, wb = sent
     else:
-        wb = lax.all_gather(pack_b, "dp", axis=0, tiled=True)
+        wb = lax.all_gather(jnp.concatenate([w_gate_inner[0], w_output_t], axis=1), "dp", axis=0, tiled=True)
         cot = lax.all_gather(cotangent, "tensor", axis=0, tiled=True)
 
     gate, ggo, stats = pl.pallas_call(
@@ -1119,13 +1150,13 @@
         grid=(blocks,),
         in_specs=[
             by_cols(tokens), by_cols(tokens), pl.BlockSpec((spans, BW, 128), lambda i: (0, i, 0)),
-            by_cols(8), once((8, BW)), once((8, 128)),
+            by_cols(5), once((5, BW)), once((heads,)), once((heads,)),
             once((tokens, BW)), once((tokens, BW)), once((tokens, 128)), once((tokens, 128)),
-            once((48, tokens)), once((48, tokens)), once((48, tokens)), once((48, 128)),
+            once((48, tokens)), once((48, tokens)), once((48, tokens)),
         ] + [hbm, hbm] * own_links,
-        out_specs=[by_cols(tokens), by_cols(8), once((tokens, 384)), once((8, BW)), once((48, 128))]
+        out_specs=[by_cols(tokens), by_cols(8), once((tokens, 384)), once((8, BW)), once((8, 128))]
         + [hbm, once((2, width // ways, units))] * own_links,
-        out_shape=[sds((tokens, units), bf16), sds((8, units)), sds((tokens, 384), bf16), sds((8, BW)), sds((48, 128))]
+        out_shape=[sds((tokens, units), bf16), sds((8, units)), sds((tokens, 384), bf16), sds((8, BW)), sds((8, 128))]
         + [sds((tokens // 2, width), bf16), sds((2, width // ways, units))] * own_links,
         scratch_shapes=[
             pltpu.VMEM((tokens + 8, BW), f32), pltpu.VMEM((tokens + 8, BW), f32),
@@ -1139,7 +1170,10 @@
         ] + ([sem, sem] + reduce_scratch(2, width // ways, units)) * own_links,
         compiler_params=params(4 if own_links else None),
         cost_estimate=pl.CostEstimate(flops=40_000_000_000, bytes_accessed=30_000_000, transcendentals=heads * spans * Q * Q),
-    )(inner, dy, states, kin, kst, hp, cst, bc, step, cum, step_t, cum_t, pre_t, rate_t, *[mixed, grad_b] * own_links)
+    )(
+        inner, dy, states, conv_inner, conv_state, decay_log, skip_gain, cst, bc, step, cum, step_t, cum_t, pre_t,
+        *[mixed, grad_b] * own_links,
+    )
     if own_links:
         mixed_got, wb_shard = sent
     else:
@@ -1147,12 +1181,12 @@
         wb_shard = lax.psum_scatter(grad_b, "dp", scatter_dimension=1, tiled=True).astype(f32)
     output = (rows_in + mixed_near.astype(f32) + mixed_got.astype(f32)).astype(bf16)
 
-    last = jnp.concatenate([gks[:5].reshape(-1), hs[:, 0], hs[:, 1], jnp.zeros((units - 5 * BW - 96,), f32)])
-    small = jnp.concatenate([gk[:6], ggg[:1], last[None]], axis=0)
     if own_links:
-        grad_normed, wa_shard, small = reduce_tail(normed_t, dinner, dsd, dgate, wb, wa, small, ways, 5)
+        grad_normed, wa_shard, small = reduce_tail(normed_t, dinner, dsd, dgate, wb, wa, (gk, ggg, gks, hs), ways, 5)
         wa_shard = wa_shard[0]
     else:
+        last = jnp.concatenate([gks[:5].reshape(-1), hs[0], hs[1]])
+        small = jnp.concatenate([gk[:6], ggg[:1], last[None]], axis=0)
         grad_a = jnp.concatenate([mm(normed_t, dinner).astype(bf16), mm(normed_t, dsd).astype(bf16)], axis=1)
         pulled = mm(dgate, wb[:, :units], 1, 1) + mm(dinner, wa[:, :units], 1, 1) + mm(dsd, wa[:, units:], 1, 1)
         near, far = halves(pulled.astype(bf16), 0)
@@ -1165,8 +1199,8 @@
     )
 
     conv_state_sum = small[7, : 5 * BW].reshape(5, BW)
-    bias_sum = gathered_heads(small[7, 5 * BW : 5 * BW + 48], heads)
-    decay_sum = gathered_heads(small[7, 5 * BW + 48 : 5 * BW + 96], heads)
+    bias_sum = gathered_heads(small[7, 5 * BW : 5 * BW + 128], heads)
+    decay_sum = gathered_heads(small[7, 5 * BW + 128 : 5 * BW + 256], heads)
     skip_sum = jnp.sum(small[5].reshape(heads, HEAD), axis=1)
 
     gain_rows = jnp.sum(wb_shard[0] * w_gate_inner[0].astype(f32), axis=1) + jnp.sum(

time: 350 us -> 325 us (0.929)
  Pallas kernels: 295 us -> 279 us
  local copies, waits for them, and re-layouts: 19.8 us -> 13.9 us
    pallas_call x2, Pallas kernels: 109 us -> 95.1 us  [the longest x1 52.8 us: reduce_tail(): pl.pallas_call(tail_kernel, name='tail', in_specs=[hbm] * 6 + [vmem] * 4,...]
    concatenate x5 -> x0, other arithmetic: 6.17 us -> none  [the longest x1 1.82 us: on_device(): pack_b = jnp.concatenate([w_gate_inner[0], w_output.T], axis=1)]
  transfers between devices with their start and end apart: 1 -> 1, of which waited for: 0 -> 0; matrix products, arithmetic and copies ran while one was open for 4% -> 5% of each run, Pallas kernels for 0% -> 0%
where the time goes in v6:
time: 325 us; the launch traced here: 323 us
  Pallas kernels  279 us (86%)
  other arithmetic  19.7 us (6%)
  local copies, waits for them, and re-layouts  13.9 us (4%)
  matrix products  9.26 us (3%)
    pallas_call x1, Pallas kernels, on_device(): pl.pallas_call(functools.partial(mixer_backward, own_links), name='mixer_...  74.3 us
    pallas_call x1, Pallas kernels, on_device(): pl.pallas_call(functools.partial(mixer_forward, own_links), name='mixer_f...  62.5 us
    pallas_call x1, Pallas kernels, reduce_tail(): pl.pallas_call(tail_kernel, name='tail', in_specs=[hbm] * 6 + [vmem] * 4,...  52.8 us
    pallas_call x1, Pallas kernels, gather_rows(): pl.pallas_call(gather_kernel, name='gather_rows', in_specs=[vmem] * 5, ou...  42.4 us
    pallas_call x1, Pallas kernels, on_device(): pl.pallas_call(functools.partial(gate_backward, float(unit_total)), name=...  24.1 us
    pallas_call x1, Pallas kernels, on_device(): pl.pallas_call(functools.partial(gate_forward, own_links), name='gate_for...  22.9 us
    dot_general x1, matrix products, mm(): lax.dot_general(a, b, (((ca,), (cb,)), ((), ())), preferred_element_type=...  9.26 us
    add x1, other arithmetic, on_device(): cotangent.astype(f32)  6.92 us
  transfers between devices with their start and end apart: 1, of which 0 were waited for; matrix products, arithmetic and copies ran while one was open for 5% of the time, Pallas kernels for 0%

profile of v6, /device:TPU:0, one launch (start us, length us, event | category | flops | bytes accessed | tf_op | source)
XLA Modules:
  0.0 322.7 jit_solution(5404792968767310617)
XLA Ops:
  0.6 1.4 copy.29.w_step
  2.0 1.7 slice_bitcast_fusion.2
  3.7 1.3 broadcast_in_dim.4.gain
  5.1 42.4 %gather_rows.1 = (bf16[1024,1536]{1,0:T(8,128)(2,1)}, bf16[1536,1920]{1,0:T(8,128)(2,1)}) custom-call(bf16[512,1536]{1,0:T(8,128)(2,1)} %tokens_in.1, f32[8,1536]{1,0:T(8,128)} %broadcast_in_dim.4.gain, bf16[2,96,1536]{2,1,0:T(8,128)(2,1)} %refs_1_.1, bf16[96,256]{1,0:T(8,128)(2,1)} %w_state_io.1, bf16[96,24]{1,0:T(8,128)(2,1)} %copy.29.w_step), custom_call_target="tpu_custom_call" | custom-call | tf_op jit(solution)/shard_map/gather_rows/pallas_call | solution.py:702
  47.4 0.0 copy-start.8
  47.4 62.5 %mixer_forward.1 = (f32[1024,1536]{1,0:T(8,128)}, f32[1024,1536]{1,0:T(8,128)}, f32[4,1536,128]{2,1,0:T(8,128)}, f32[1024,256]{1,0:T(8,128)}, bf16[1024,256]{1,0...) custom-call(bf16[1024,1536]{1,0:T(8,128)(2,1)} %get-tuple-element.46, ...), custom_call_target="tpu_custom_call" | custom-call | flops 7650410496 | bytes 30000000 | tf_op jit(solution)/shard_map/mixer_forward/pallas_call | solution.py:1069
  110.0 0.0 copy-done.8
  110.0 0.6 broadcast_in_dim.5.gain
  110.6 22.9 %gate_forward.1 = (f32[1024,1536]{1,0:T(8,128)}, f32[1024,1536]{1,0:T(8,128)}, f32[8,1024]{1,0:T(8,128)}) custom-call(bf16[1024,1536]{1,0:T(8,128)(2,1)} %get-tuple-element.46.normed, bf16[1024,1536]{1,0:T(8,128)(2,1)} %get-tuple-element.48.cot, bf16[1536,3072]{1,0:T(8,128)(2,1)} %get-tuple-element.49.wg.wo.wb, ...), custom_call_target="tpu_custom_call" | custom-call | flops 9663676416 | bytes 35000000 | tf_op jit(solution)/shard_map/gate_forward/pallas_call | solution.py:1105
  133.6 24.1 %gate_backward.1 = (bf16[1024,1536]{1,0:T(8,128)(2,1)}, bf16[1024,1536]{1,0:T(8,128)(2,1)}, bf16[1024,1536]{1,0:T(8,128)(2,1)}, f32[8,1536]{1,0:T(8,128)}, bf16[...) custom-call(f32[8,1024]{1,0:T(8,128)} %get-tuple-element.51.stats, f32[1024,1536]{1,0:T(8,128)} %get-tuple-element.52.gate, ...), custom_call_target="tpu_custom_call" | custom-call | flops 9663676416 | bytes 45000000 | tf_op jit(solution)/shard_map/gate_backward/pallas_call | solution.py:1123
  157.6 9.3 %fusion.2.refs_0_ = bf16[1024,1536]{1,0:T(8,128)(2,1)} fusion(bf16[1024,1536]{1,0:T(8,128)(2,1)} %get-tuple-element.54, bf16[1536,3072]{1,0:T(8,128)(2,1)} %get-tuple-element.49.wg.wo.wb), kind=kOutput, calls=%fused_computation.5 | convolution fusion | flops 4833411072 | bytes 11010048 | tf_op jit(solution)/shard_map/dot_general | solution.py:24
  166.9 74.3 %mixer_backward.1 = (bf16[1024,1536]{1,0:T(8,128)(2,1)}, f32[8,1536]{1,0:T(8,128)}, bf16[1024,384]{1,0:T(8,128)(2,1)}, f32[8,256]{1,0:T(8,128)}, f32[8,128]{1,0:...) custom-call(f32[1024,1536]{1,0:T(8,128)} %get-tuple-element.55.inner, ...), custom_call_target="tpu_custom_call" | custom-call | flops 40000000000 | bytes 30000000 | tf_op jit(solution)/shard_map/mixer_backward/pallas_call | solution.py:1147
  241.2 0.0 copy-start.7
  241.2 0.0 copy-start.2
  241.2 0.0 copy-start.4
  241.3 52.8 %tail.1 = (f32[512,1536]{1,0:T(8,128)}, f32[1,96,1920]{2,1,0:T(8,128)}, f32[8,1536]{1,0:T(8,128)}) custom-call(bf16[1536,1024]{1,0:T(8,128)(2,1)} %get-tuple-element.67.normed_t, bf16[1024,1536]{1,0:T(8,128)(2,1)} %get-tuple-element.68.dinner, bf16[1024,384]{1,0:T(8,128)(2,1)} %get-tuple-element.69.dsd, bf16[1024,1536]{1,0:T(8,128)(2,1)} %get-tuple-element.70.dgate, ...), custom_call_target="tpu_custom_call" | custom-call | tf_op jit(solution)/shard_map/tail/pallas_call | solution.py:980
  294.0 0.0 copy-start.1
  294.0 0.0 copy-start.6
  294.1 0.0 copy-start
  294.1 1.7 slice.93
  295.8 0.8 slice_reduce_fusion.2
  296.6 0.7 copy.30
  297.3 2.8 slice_bitcast_fusion.1
  300.1 1.2 multiply_reduce_fusion
  301.3 0.7 dynamic-slice_divide_fusion
  302.0 0.1 dynamic_slice.22
  302.1 0.8 fusion.19
  302.9 0.6 pad_maximum_fusion.1
  303.5 0.0 collective-permute-start
  303.6 0.4 fusion.13
  304.0 1.5 slice_reduce_fusion
  305.5 2.5 fusion.7
  308.0 1.1 pad_maximum_fusion
  309.1 6.9 %fusion.10 = (f32[512,1536]{1,0:T(8,128)}, bf16[512,1536]{1,0:T(8,128)(2,1)}) fusion(bf16[512,1536]{1,0:T(8,128)(2,1)S(1)} %copy-done, bf16[512,1536]{1,0:T(8,128)(2,1)} %refs_0_.1, f32[512,1536]{1,0:T(8,128)} %get-tuple-element.75, f32[512]{0:T(512)S(1)} %broadcast_multiply_fusion, f32[1536]{0:T(1024)S(1)} %copy-done.6, f32[512]{0:T(512)S(1)} %add_rsqrt_fusion, ...), kind=kLoop, calls=%fused_computation.11 | loop fusion | flops 10223616 | bytes 14166020 | tf_op jit(solution)/shard_map/add | solution.py:1197
  316.1 0.1 copy.31
  316.1 0.6 slice.99
  316.8 0.1 reshape_squeeze.7
  316.8 0.1 reshape.82
  316.9 0.6 reshape.83
  317.5 0.1 reshape.84
  317.6 0.6 reshape.85
  318.2 0.6 reduce_sum.49
  318.8 0.0 collective-permute-done
  318.8 0.8 fusion.17
  319.6 0.6 slice.97
  320.2 0.6 slice.100
  320.8 1.3 slice_add_fusion
  322.1 0.6 copy.33
  (17 shorter events, 0.1 us)
Async XLA Ops:
  47.4 62.6 %copy-start.8 = (f32[1536]{0:T(1024)S(1)}, f32[1536]{0:T(1024)}, u32[]{:S(2)}) copy-start(f32[1536]{0:T(1024)} %param.23) | copy-start | bytes 18436
  241.2 55.4 %copy-start.7 = (bf16[96,24]{0,1:T(8,128)(2,1)S(1)}, bf16[96,24]{0,1:T(8,128)(2,1)}, u32[]{:S(2)}) copy-start(bf16[96,24]{0,1:T(8,128)(2,1)} %param.17) | copy-start | bytes 13828
  241.2 56.1 %copy-start.2 = (bf16[2,96,1536]{2,1,0:T(8,128)(2,1)S(1)}, bf16[2,96,1536]{2,1,0:T(8,128)(2,1)}, u32[]{:S(2)}) copy-start(bf16[2,96,1536]{2,1,0:T(8,128)(2,1)} %refs_1_.1) | copy-start | bytes 1769476
  241.2 58.8 %copy-start.4 = (bf16[96,256]{1,0:T(8,128)(2,1)S(1)}, bf16[96,256]{1,0:T(8,128)(2,1)}, u32[]{:S(2)}) copy-start(bf16[96,256]{1,0:T(8,128)(2,1)} %w_state_io.1) | copy-start | bytes 147460
  294.0 6.0 %copy-start.1 = (f32[1,96,1920]{2,1,0:T(8,128)S(1)}, f32[1,96,1920]{2,1,0:T(8,128)}, u32[]{:S(2)}) copy-start(f32[1,96,1920]{2,1,0:T(8,128)} %get-tuple-element.77) | copy-start | bytes 2211844
  294.0 7.2 %copy-start.6 = (f32[1536]{0:T(1024)S(1)}, f32[1536]{0:T(1024)}, u32[]{:S(2)}) copy-start(f32[1536]{0:T(1024)} %param.14) | copy-start | bytes 18436
  294.1 9.5 %copy-start = (bf16[512,1536]{1,0:T(8,128)(2,1)S(1)}, bf16[512,1536]{1,0:T(8,128)(2,1)}, u32[]{:S(2)}) copy-start(bf16[512,1536]{1,0:T(8,128)(2,1)} %tokens_in.1) | copy-start | bytes 4718596
  303.5 15.3 %collective-permute-start = (f32[12976]{0:T(1024)}, f32[12976]{0:T(1024)}, u32[]{:S(2)}, u32[]{:S(2)}) collective-permute-start(f32[12976]{0:T(1024)} %pad_maximum_fusion.1), channel_id=1, source_target_pairs={{0,1},{1,0},{2,3},{3,2},{4,5},{5,4},{6,7},{7,6},{8,9},{9,8},{10,11... | collective-permute-start | bytes 155720 | tf_op jit(solution)/shard_map/ppermute | solution.py:997
  309.1 6.9 %copy-start.5 = (f32[8,1536]{1,0:T(8,128)S(1)}, f32[8,1536]{1,0:T(8,128)}, u32[]{:S(2)}) copy-start(f32[8,1536]{1,0:T(8,128)} %get-tuple-element.78) | copy-start | bytes 147460
  309.1 9.7 %copy-start.3 = (f32[96,256]{1,0:T(8,128)S(1)}, f32[96,256]{1,0:T(8,128)}, u32[]{:S(2)}) copy-start(f32[96,256]{1,0:T(8,128)} %slice.93) | copy-start | bytes 294916

commit v7 on v6

--- a/solution.py
+++ b/solution.py
@@ -103,14 +103,19 @@
 def mixer_forward(links, normed, wi, wsx, kin, kst, bias, log_rate, skip_in, *refs):
     refs = list(refs)
     if links:
-        sent = refs[:3] + refs[13:15]
-        refs = refs[3:13] + refs[15:]
+        sent = refs[:3] + refs[14:16]
+        gain, gate_refs = refs[3], refs[16:19]
+        refs = refs[4:14] + refs[19:]
     inner_out, ssd_out, states_out, cst_out, bc_out, step_out, cum_out, stepT_out, cumT_out, preT_out = refs[:10]
     buf, gram, colc, cols, rowp, mst, xst, state = refs[10:18]
     i = pl.program_id(0)
     tokens = normed.shape[0]
     spans = tokens // Q
-    work = BesideForward(*sent, *refs[18:]) if links else None
+    blocks = inner_out.shape[1] // BW
+    if links:
+        work = BesideForward(*sent, *refs[27:])
+        ssd_v, *gate_scratch = refs[18:27]
+        blocks = ssd_v.shape[0] - 1
     heads = bias.shape[0]
     skip = lay(head_row(skip_in), as_units(heads, i))[0:1]
 
@@ -141,53 +146,142 @@
         cumT_out[...] = jnp.transpose(cum_out[...])[:48]
         mst[...] = jnp.zeros(mst.shape, bf16)
 
-    inner = mm(normed[...], wi[...])
-    inner_out[...] = inner
-    buf[8 : 8 + tokens] = inner
-    turn = lax.rem(128 - 8 * i, 128)
-    colc[...] = pltpu.roll(cum_out[...], turn, 1)
-    cols[...] = pltpu.roll(step_out[...], turn, 1)
-    rows8 = pl.ds(pl.multiple_of(8 * i, 8), 8)
-    rowp[...] = cumT_out[rows8] - jnp.log2(stepT_out[rows8])
-    state[...] = jnp.zeros(state.shape, f32)
-    masks = head_masks()
-
-    def span(s, carry):
-        at = pl.multiple_of(s * Q, Q)
-        rows = pl.ds(at, Q)
-        conv = conv_taps(buf[pl.ds(at, Q + 8)], kin[...])
-        xs = conv * sigmoid(conv)
-        x_low = xs.astype(bf16)
-        col = colc[rows]
-        total = col[Q - 1 : Q]
-        growth = expand(jnp.exp2(col[:, :8]))
-        weight = expand(jnp.exp2(total[:, :8] - col[:, :8]) * cols[rows][:, :8])
-        xw_low = (xs * weight).astype(bf16)
-        for j in range(HB):
-            xst[j * Q : j * Q + Q] = x_low * masks[j]
-            row = rowp[j : j + 1, rows]
-            for r, half, diag in quads():
-                part = gram[s, r : r + 64, half * 128 : half * 128 + 128]
-                dec = decay_chunk(col[:, j : j + 1], row, r, half, diag)
-                mst[r : r + 64, j * Q + half * 128 : j * Q + half * 128 + 128] = (part * dec).astype(bf16)
-        intra = mm(mst[...], xst[...])
-        state_in = state[...]
-        states_out[s] = state_in
-        bc = bc_out[rows]
-        readout = mm(bc[:, 128:], state_in.astype(bf16), 1, 1)
-        ssd_out[rows] = intra + growth * readout + skip * xs
-        local = mm(xw_low, bc[:, :128], 0, 0)
-        fade = jnp.exp2(total)
-        for j in range(HB):
-            at_j = slice(j * HEAD, j * HEAD + HEAD)
-            state[at_j] = fade[:, j : j + 1] * state_in[at_j] + local[at_j]
-        if links:
-            work.step(i * spans + s)
-        return carry
-
-    lax.fori_loop(0, spans, span, 0)
-    if links:
-        pl.when(i == pl.num_programs(0) - 1)(work.finish)
+    def mix():
+        inner = mm(normed[...], wi[...])
+        inner_out[...] = inner
+        buf[8 : 8 + tokens] = inner
+        turn = lax.rem(128 - 8 * i, 128)
+        colc[...] = pltpu.roll(cum_out[...], turn, 1)
+        cols[...] = pltpu.roll(step_out[...], turn, 1)
+        rows8 = pl.ds(pl.multiple_of(8 * i, 8), 8)
+        rowp[...] = cumT_out[rows8] - jnp.log2(stepT_out[rows8])
+        state[...] = jnp.zeros(state.shape, f32)
+        masks = head_masks()
+
+        def span(s, carry):
+            at = pl.multiple_of(s * Q, Q)
+            rows = pl.ds(at, Q)
+            conv = conv_taps(buf[pl.ds(at, Q + 8)], kin[...])
+            xs = conv * sigmoid(conv)
+            x_low = xs.astype(bf16)
+            col = colc[rows]
+            total = col[Q - 1 : Q]
+            growth = expand(jnp.exp2(col[:, :8]))
+            weight = expand(jnp.exp2(total[:, :8] - col[:, :8]) * cols[rows][:, :8])
+            xw_low = (xs * weight).astype(bf16)
+            for j in range(HB):
+                xst[j * Q : j * Q + Q] = x_low * masks[j]
+                row = rowp[j : j + 1, rows]
+                for r, half, diag in quads():
+                    part = gram[s, r : r + 64, half * 128 : half * 128 + 128]
+                    dec = decay_chunk(col[:, j : j + 1], row, r, half, diag)
+                    mst[r : r + 64, j * Q + half * 128 : j * Q + half * 128 + 128] = (part * dec).astype(bf16)
+            intra = mm(mst[...], xst[...])
+            state_in = state[...]
+            states_out[s] = state_in
+            bc = bc_out[rows]
+            readout = mm(bc[:, 128:], state_in.astype(bf16), 1, 1)
+            ssd = intra + growth * readout + skip * xs
+            ssd_out[rows] = ssd
+            if links:
+                ssd_v[blocks, rows] = ssd
+            local = mm(xw_low, bc[:, :128], 0, 0)
+            fade = jnp.exp2(total)
+            for j in range(HB):
+                at_j = slice(j * HEAD, j * HEAD + HEAD)
+                state[at_j] = fade[:, j : j + 1] * state_in[at_j] + local[at_j]
+            if links:
+                work.step(i * spans + s)
+            return carry
+
+        lax.fori_loop(0, spans, span, 0)
+
+    if not links:
+        mix()
+        return
+    pl.when(i < blocks)(mix)
+
+    @pl.when(i < blocks)
+    def _():
+        ssd_v[i] = ssd_v[blocks]
+
+    gates = GateForward(i - blocks, blocks, normed, sent[3], sent[4], gain, ssd_v, *gate_refs, *gate_scratch)
+
+    @pl.when(i == blocks)
+    def _():
+        work.first()
+        gates.start(0)
+
+    pl.when((i >= blocks) & (i < 2 * blocks))(gates.gate)
+
+    @pl.when(i == 2 * blocks)
+    def _():
+        work.finish()
+        gates.start(1)
+
+    pl.when(i >= 2 * blocks)(gates.pull)
+
+
+class GateForward:
+    def __init__(
+        self, at, blocks, normed, cot, wb, gain, ssd_v, gate_out, ggo_out, stats_out, w_v, cot_v, sq, gi, mine, landed, wl, cl
+    ):
+        self.at, self.blocks, self.normed, self.cot, self.wb, self.gain, self.ssd_v = at, blocks, normed, cot, wb, gain, ssd_v
+        self.gate_out, self.ggo_out, self.stats_out = gate_out, ggo_out, stats_out
+        self.w_v, self.cot_v, self.sq, self.gi, self.mine, self.landed, self.wl, self.cl = w_v, cot_v, sq, gi, mine, landed, wl, cl
+
+    def load(self, which, n):
+        cols = slice((which * self.blocks + n) * BW, (which * self.blocks + n + 1) * BW)
+        return pltpu.make_async_copy(self.wb.at[:, cols], self.w_v.at[n], self.wl.at[n])
+
+    def tokens(self):
+        return pltpu.make_async_copy(self.cot, self.cot_v, self.cl.at[0])
+
+    def start(self, which):
+        if which:
+            self.tokens().start()
+        for n in range(self.blocks):
+            self.load(which, n).start()
+        if which:
+            self.tokens().wait()
+        total = self.gi if which else self.sq
+        total[...] = jnp.zeros(total.shape, f32)
+
+    def gate(self):
+        b = self.at
+        pltpu.make_async_copy(self.wb.at[:, :BW], self.w_v.at[b], self.wl.at[b]).wait()
+        gate = mm(self.normed[...], self.w_v[b])
+        self.gate_out[...] = gate
+        gated = self.ssd_v[b] * (gate * sigmoid(gate))
+        self.ssd_v[b] = gated
+        squares = gated * gated
+        self.sq[...] += squares[:, :128] + squares[:, 128:]
+
+    def pull(self):
+        b = self.at - self.blocks
+        pltpu.make_async_copy(self.wb.at[:, :BW], self.w_v.at[b], self.wl.at[b]).wait()
+        ggo = mm(self.cot_v[...], self.w_v[b])
+        self.ggo_out[...] = ggo
+        inner = ggo * self.gain[0:1] * self.ssd_v[b]
+        self.gi[...] += inner[:, :128] + inner[:, 128:]
+        pl.when(b == self.blocks - 1)(self.last)
+
+    def last(self):
+        self.mine[...] = token_sums(self.sq[...], self.gi[...])
+        swap = remote(self.mine, self.landed, self.cl.at[1], self.cl.at[2], tensor=1 - lax.axis_index("tensor"))
+        swap.start()
+        swap.wait()
+        self.stats_out[...] = self.mine[...] + self.landed[...]
+
+
+def token_sums(sq, gi):
+    lane = iota(sq.shape, 1)
+    both = jnp.where(
+        lane == 0,
+        jnp.sum(sq, axis=1, keepdims=True),
+        jnp.where(lane == 1, jnp.sum(gi, axis=1, keepdims=True), 0.0),
+    )
+    return jnp.transpose(both)[:8]
 
 
 class BesideForward:
@@ -220,28 +314,25 @@
 
             pl.when(at == when)(go)
 
+    def first(self):
+        for move in self.moves:
+            move.hop(3)
+            move.sides(2)
+        self.moves[0].sides(3)
+        self.moves[0].finish()
+
     def finish(self):
-        for hops in (3, 4):
-            for move in self.moves:
-                if hops < 4:
-                    move.hop(hops)
-                move.sides(hops - 1)
+        self.moves[1].sides(3)
+        self.moves[1].finish()
         self.local.wait()
         self.across.wait()
-        for move in self.moves:
-            move.finish()
-
-
-def gate_forward(links, normed, cot, wg, wo, ssd, gain, gate_out, ggo_out, stats_out, sq, gi, *refs):
+
+
+def gate_forward(normed, cot, wg, wo, ssd, gain, gate_out, ggo_out, stats_out, sq, gi):
     i = pl.program_id(0)
 
     @pl.when(i == 0)
     def _():
-        if links:
-            barrier = pltpu.get_barrier_semaphore()
-            other = {"tensor": 1 - lax.axis_index("tensor")}
-            pl.semaphore_signal(barrier, 1, device_id=other, device_id_type=MESH)
-            pl.semaphore_wait(barrier, 1)
         sq[...] = jnp.zeros(sq.shape, f32)
         gi[...] = jnp.zeros(gi.shape, f32)
 
@@ -257,21 +348,7 @@
 
     @pl.when(i == pl.num_programs(0) - 1)
     def _():
-        lane = iota(sq.shape, 1)
-        both = jnp.where(
-            lane == 0,
-            jnp.sum(sq[...], axis=1, keepdims=True),
-            jnp.where(lane == 1, jnp.sum(gi[...], axis=1, keepdims=True), 0.0),
-        )
-        if not links:
-            stats_out[...] = jnp.transpose(both)[:8]
-            return
-        mine, landed, send, recv = refs
-        mine[...] = jnp.transpose(both)[:8]
-        swap = remote(mine, landed, send, recv, tensor=1 - lax.axis_index("tensor"))
-        swap.start()
-        swap.wait()
-        stats_out[...] = mine[...] + landed[...]
+        stats_out[...] = token_sums(sq[...], gi[...])
 
 
 def gate_backward(
@@ -1066,58 +1143,65 @@
 
     hbm = pl.BlockSpec(memory_space=pl.ANY)
     sem = pltpu.SemaphoreType.DMA
+    def stage(rows, first):
+        return pl.BlockSpec((rows, BW), lambda i: (0, jnp.clip(i - first, 0, blocks - 1)))
+
     inner, ssd, states, cst, bc, step, cum, step_t, cum_t, pre_t, *sent = pl.pallas_call(
         functools.partial(mixer_forward, own_links),
         name="mixer_forward",
-        grid=(blocks,),
+        grid=(blocks * (3 if own_links else 1),),
         in_specs=[
-            once((tokens, width)), by_cols(width), once((width, 384), (0, units // 384)),
-            by_cols(5), once((5, BW)), once((heads,)), once((heads,)), once((heads,)),
-        ] + [once(v.shape) for v in (cotangent, w_gate_inner, w_output_t)] * own_links,
+            once((tokens, width)), stage(width, 0), once((width, 384), (0, units // 384)),
+            stage(5, 0), once((5, BW)), once((heads,)), once((heads,)), once((heads,)),
+        ] + ([once(v.shape) for v in (cotangent, w_gate_inner, w_output_t)] + [stage(8, 2 * blocks)]) * own_links,
         out_specs=[
-            by_cols(tokens), by_cols(tokens), pl.BlockSpec((spans, BW, 128), lambda i: (0, i, 0)),
+            stage(tokens, 0), stage(tokens, 0), pl.BlockSpec((spans, BW, 128), lambda i: (0, jnp.clip(i, 0, blocks - 1), 0)),
             once((tokens, BW)), once((tokens, BW)), once((tokens, 128)), once((tokens, 128)),
             once((48, tokens)), once((48, tokens)), once((48, tokens)),
-        ] + [hbm, hbm] * own_links,
+        ] + [hbm, hbm, stage(tokens, blocks), stage(tokens, 2 * blocks), once((8, tokens))] * own_links,
         out_shape=[
             sds((tokens, units)), sds((tokens, units)), sds((spans, units, 128)),
             sds((tokens, BW)), sds((tokens, BW), bf16), sds((tokens, 128)), sds((tokens, 128)),
             sds((48, tokens)), sds((48, tokens)), sds((48, tokens)),
-        ] + [sds((tokens, width), bf16), sds((width, 2 * units), bf16)] * own_links,
+        ] + [
+            sds((tokens, width), bf16), sds((width, 2 * units), bf16), sds((tokens, units)), sds((tokens, units)),
+            sds((8, tokens)),
+        ] * own_links,
         scratch_shapes=[
             pltpu.VMEM((tokens + 8, BW), f32), pltpu.VMEM((spans, Q, Q), f32),
             pltpu.VMEM((tokens, 128), f32), pltpu.VMEM((tokens, 128), f32), pltpu.VMEM((8, tokens), f32),
             pltpu.VMEM((Q, HB * Q), bf16), pltpu.VMEM((HB * Q, BW), bf16), pltpu.VMEM((BW, 128), f32),
-        ] + (gather_scratch() + [sem, sem, sem]) * own_links,
+        ] + ([
+            pltpu.VMEM((blocks + 1, tokens, BW), f32), pltpu.VMEM((blocks, width, BW), bf16), pltpu.VMEM((tokens, width), bf16),
+            pltpu.VMEM((tokens, 128), f32), pltpu.VMEM((tokens, 128), f32), pltpu.VMEM((8, tokens), f32),
+            pltpu.VMEM((8, tokens), f32), sem((blocks,)), sem((3,)),
+        ] + gather_scratch() + [sem, sem, sem]) * own_links,
         compiler_params=params(2 if own_links else None),
         cost_estimate=pl.CostEstimate(flops=2 * tokens * width * (units + 384) + 4 * tokens * 256 * units, bytes_accessed=30_000_000, transcendentals=heads * spans * Q * Q),
     )(
         normed, wa, wa, conv_inner, conv_state, step_bias, decay_log, skip_gain,
-        *[cotangent, w_gate_inner, w_output_t] * own_links,
+        *[cotangent, w_gate_inner, w_output_t, gain8] * own_links,
     )
 
     if own_links:
-        cot, wb = sent
+        cot, wb, gate, ggo, stats = sent
     else:
         wb = lax.all_gather(jnp.concatenate([w_gate_inner[0], w_output_t], axis=1), "dp", axis=0, tiled=True)
         cot = lax.all_gather(cotangent, "tensor", axis=0, tiled=True)
-
-    gate, ggo, stats = pl.pallas_call(
-        functools.partial(gate_forward, own_links),
-        name="gate_forward",
-        grid=(blocks,),
-        in_specs=[
-            once((tokens, width)), once((tokens, width)), by_cols(width), by_cols(width, blocks),
-            by_cols(tokens), by_cols(8),
-        ],
-        out_specs=[by_cols(tokens), by_cols(tokens), once((8, tokens))],
-        out_shape=[sds((tokens, units)), sds((tokens, units)), sds((8, tokens))],
-        scratch_shapes=[pltpu.VMEM((tokens, 128), f32), pltpu.VMEM((tokens, 128), f32)]
-        + [pltpu.VMEM((8, tokens), f32), pltpu.VMEM((8, tokens), f32), sem, sem] * own_links,
-        compiler_params=params(3 if own_links else None),
-        cost_estimate=pl.CostEstimate(flops=4 * tokens * width * units, bytes_accessed=35_000_000, transcendentals=tokens * units),
-    )(normed, cot, wb, wb, ssd, gain8)
-    if not own_links:
+        gate, ggo, stats = pl.pallas_call(
+            gate_forward,
+            name="gate_forward",
+            grid=(blocks,),
+            in_specs=[
+                once((tokens, width)), once((tokens, width)), by_cols(width), by_cols(width, blocks),
+                by_cols(tokens), by_cols(8),
+            ],
+            out_specs=[by_cols(tokens), by_cols(tokens), once((8, tokens))],
+            out_shape=[sds((tokens, units)), sds((tokens, units)), sds((8, tokens))],
+            scratch_shapes=[pltpu.VMEM((tokens, 128), f32), pltpu.VMEM((tokens, 128), f32)],
+            compiler_params=params(),
+            cost_estimate=pl.CostEstimate(flops=4 * tokens * width * units, bytes_accessed=35_000_000, transcendentals=tokens * units),
+        )(normed, cot, wb, wb, ssd, gain8)
         stats = stats + swap(stats)
 
     dy, dgate, ng, ggg, grad_b, normed_t = pl.pallas_call(

time: 325 us -> 326 us (level)
    pallas_call x1 -> x0, Pallas kernels: 22.9 us -> none  [on_device(): pl.pallas_call(functools.partial(gate_forward, own_links), name='gate_for...]
    pallas_call x1, Pallas kernels: 62.5 us -> 83.6 us  [on_device(): pl.pallas_call(functools.partial(mixer_forward, own_links), name='mixer_f...]
where the time goes in v7:
time: 326 us; the launch traced here: 323 us
  Pallas kernels  277 us (85%)
  other arithmetic  19.7 us (6%)
  local copies, waits for them, and re-layouts  14.6 us (4%)
  matrix products  9.43 us (3%)
    pallas_call x1, Pallas kernels, on_device(): pl.pallas_call(functools.partial(mixer_forward, own_links), name='mixer_f...  83.6 us
    pallas_call x1, Pallas kernels, on_device(): pl.pallas_call(functools.partial(mixer_backward, own_links), name='mixer_...  76.7 us
    pallas_call x1, Pallas kernels, reduce_tail(): pl.pallas_call(tail_kernel, name='tail', in_specs=[hbm] * 6 + [vmem] * 4,...  50.3 us
    pallas_call x1, Pallas kernels, gather_rows(): pl.pallas_call(gather_kernel, name='gather_rows', in_specs=[vmem] * 5, ou...  42.4 us
    pallas_call x1, Pallas kernels, on_device(): pl.pallas_call(functools.partial(gate_backward, float(unit_total)), name=...  24.1 us
    dot_general x1, matrix products, mm(): lax.dot_general(a, b, (((ca,), (cb,)), ((), ())), preferred_element_type=...  9.43 us
    add x1, other arithmetic, on_device(): cotangent.astype(f32)  6.92 us
  transfers between devices with their start and end apart: 1, of which 0 were waited for; matrix products, arithmetic and copies ran while one was open for 5% of the time, Pallas kernels for 0%

profile of v7, /device:TPU:0, one launch (start us, length us, event | category | flops | bytes accessed | tf_op | source)
XLA Modules:
  0.0 323.0 jit_solution(2437605710889683886)
XLA Ops:
  0.6 1.4 copy.29.w_step
  2.0 1.7 slice_bitcast_fusion.2
  3.7 1.3 broadcast_in_dim.4.gain
  5.1 42.4 %gather_rows.1 = (bf16[1024,1536]{1,0:T(8,128)(2,1)}, bf16[1536,1920]{1,0:T(8,128)(2,1)}) custom-call(bf16[512,1536]{1,0:T(8,128)(2,1)} %tokens_in.1, f32[8,1536]{1,0:T(8,128)} %broadcast_in_dim.4.gain, bf16[2,96,1536]{2,1,0:T(8,128)(2,1)} %refs_1_.1, bf16[96,256]{1,0:T(8,128)(2,1)} %w_state_io.1, bf16[96,24]{1,0:T(8,128)(2,1)} %copy.29.w_step), custom_call_target="tpu_custom_call" | custom-call | tf_op jit(solution)/shard_map/gather_rows/pallas_call | solution.py:779
  47.4 1.3 broadcast_in_dim.5.refs_3_.gain
  48.8 83.6 %mixer_forward.1 = (f32[1024,1536]{1,0:T(8,128)}, f32[1024,1536]{1,0:T(8,128)}, f32[4,1536,128]{2,1,0:T(8,128)}, f32[1024,256]{1,0:T(8,128)}, bf16[1024,256]{1,0...) custom-call(bf16[1024,1536]{1,0:T(8,128)(2,1)} %get-tuple-element.46, ...), custom_call_target="tpu_custom_call" | custom-call | flops 7650410496 | bytes 30000000 | tf_op jit(solution)/shard_map/mixer_forward/pallas_call | solution.py:1149
  132.3 24.1 %gate_backward.1 = (bf16[1024,1536]{1,0:T(8,128)(2,1)}, bf16[1024,1536]{1,0:T(8,128)(2,1)}, bf16[1024,1536]{1,0:T(8,128)(2,1)}, f32[8,1536]{1,0:T(8,128)}, bf16[...) custom-call(f32[8,1024]{1,0:T(8,128)} %get-tuple-element.48.stats, f32[1024,1536]{1,0:T(8,128)} %get-tuple-element.49.gate, ...), custom_call_target="tpu_custom_call" | custom-call | flops 9663676416 | bytes 45000000 | tf_op jit(solution)/shard_map/gate_backward/pallas_call | solution.py:1207
  156.4 9.4 %fusion.2.refs_0_ = bf16[1024,1536]{1,0:T(8,128)(2,1)} fusion(bf16[1024,1536]{1,0:T(8,128)(2,1)} %get-tuple-element.53, bf16[1536,3072]{1,0:T(8,128)(2,1)} %get-tuple-element.54.wb), kind=kOutput, calls=%fused_computation.5 | convolution fusion | flops 4833411072 | bytes 11010048 | tf_op jit(solution)/shard_map/dot_general | solution.py:24
  165.9 76.7 %mixer_backward.1 = (bf16[1024,1536]{1,0:T(8,128)(2,1)}, f32[8,1536]{1,0:T(8,128)}, bf16[1024,384]{1,0:T(8,128)(2,1)}, f32[8,256]{1,0:T(8,128)}, f32[8,128]{1,0:...) custom-call(f32[1024,1536]{1,0:T(8,128)} %get-tuple-element.55.inner, ...), custom_call_target="tpu_custom_call" | custom-call | flops 40000000000 | bytes 30000000 | tf_op jit(solution)/shard_map/mixer_backward/pallas_call | solution.py:1231
  242.6 0.0 copy-start.7
  242.6 0.0 copy-start.2
  242.6 0.0 copy-start.4
  242.6 50.3 %tail.1 = (f32[512,1536]{1,0:T(8,128)}, f32[1,96,1920]{2,1,0:T(8,128)}, f32[8,1536]{1,0:T(8,128)}) custom-call(bf16[1536,1024]{1,0:T(8,128)(2,1)} %get-tuple-element.67.normed_t, bf16[1024,1536]{1,0:T(8,128)(2,1)} %get-tuple-element.68.dinner, bf16[1024,384]{1,0:T(8,128)(2,1)} %get-tuple-element.69.dsd, bf16[1024,1536]{1,0:T(8,128)(2,1)} %get-tuple-element.70.dgate, ...), custom_call_target="tpu_custom_call" | custom-call | tf_op jit(solution)/shard_map/tail/pallas_call | solution.py:1057
  292.9 0.0 copy-start.1
  292.9 0.0 copy-start.6
  293.0 0.0 copy-start
  293.0 1.7 slice.93
  294.7 0.8 slice_reduce_fusion.2
  295.5 0.7 copy.30
  296.2 0.0 copy-done.2
  296.2 2.8 slice_bitcast_fusion.1
  299.0 0.0 copy-done.1
  299.0 1.2 multiply_reduce_fusion
  300.1 0.0 copy-done.6
  300.2 0.7 dynamic-slice_divide_fusion
  300.9 0.1 dynamic_slice.22
  301.0 0.8 fusion.19
  301.8 0.6 pad_maximum_fusion.1
  302.4 1.4 collective-permute-start
  303.8 0.4 fusion.13
  304.2 1.5 slice_reduce_fusion
  305.7 2.5 fusion.7
  308.3 1.1 pad_maximum_fusion
  309.4 6.9 %fusion.10 = (f32[512,1536]{1,0:T(8,128)}, bf16[512,1536]{1,0:T(8,128)(2,1)}) fusion(bf16[512,1536]{1,0:T(8,128)(2,1)S(1)} %copy-done, bf16[512,1536]{1,0:T(8,128)(2,1)} %refs_0_.1, f32[512,1536]{1,0:T(8,128)} %get-tuple-element.75, f32[512]{0:T(512)S(1)} %broadcast_multiply_fusion, f32[1536]{0:T(1024)S(1)} %copy-done.6, f32[512]{0:T(512)S(1)} %add_rsqrt_fusion, ...), kind=kLoop, calls=%fused_computation.11 | loop fusion | flops 10223616 | bytes 14166020 | tf_op jit(solution)/shard_map/add | solution.py:1281
  316.3 0.1 copy.31
  316.4 0.6 slice.99
  317.0 0.1 reshape_squeeze.7
  317.1 0.1 reshape.82
  317.2 0.6 reshape.83
  317.8 0.1 reshape.84
  317.8 0.6 reshape.85
  318.4 0.6 reduce_sum.49
  319.1 0.0 collective-permute-done
  319.1 0.8 fusion.17
  319.9 0.6 slice.97
  320.5 0.6 slice.100
  321.1 1.2 slice_add_fusion
  322.3 0.6 copy.33
  (14 shorter events, 0.1 us)
Async XLA Ops:
  242.6 52.9 %copy-start.7 = (bf16[96,24]{0,1:T(8,128)(2,1)S(1)}, bf16[96,24]{0,1:T(8,128)(2,1)}, u32[]{:S(2)}) copy-start(bf16[96,24]{0,1:T(8,128)(2,1)} %param.17) | copy-start | bytes 13828
  242.6 53.6 %copy-start.2 = (bf16[2,96,1536]{2,1,0:T(8,128)(2,1)S(1)}, bf16[2,96,1536]{2,1,0:T(8,128)(2,1)}, u32[]{:S(2)}) copy-start(bf16[2,96,1536]{2,1,0:T(8,128)(2,1)} %refs_1_.1) | copy-start | bytes 1769476
  242.6 56.4 %copy-start.4 = (bf16[96,256]{1,0:T(8,128)(2,1)S(1)}, bf16[96,256]{1,0:T(8,128)(2,1)}, u32[]{:S(2)}) copy-start(bf16[96,256]{1,0:T(8,128)(2,1)} %w_state_io.1) | copy-start | bytes 147460
  292.9 6.1 %copy-start.1 = (f32[1,96,1920]{2,1,0:T(8,128)S(1)}, f32[1,96,1920]{2,1,0:T(8,128)}, u32[]{:S(2)}) copy-start(f32[1,96,1920]{2,1,0:T(8,128)} %get-tuple-element.77) | copy-start | bytes 2211844
  292.9 7.2 %copy-start.6 = (f32[1536]{0:T(1024)S(1)}, f32[1536]{0:T(1024)}, u32[]{:S(2)}) copy-start(f32[1536]{0:T(1024)} %param.14) | copy-start | bytes 18436
  293.0 10.9 %copy-start = (bf16[512,1536]{1,0:T(8,128)(2,1)S(1)}, bf16[512,1536]{1,0:T(8,128)(2,1)}, u32[]{:S(2)}) copy-start(bf16[512,1536]{1,0:T(8,128)(2,1)} %tokens_in.1) | copy-start | bytes 4718596
  302.4 16.6 %collective-permute-start = (f32[12976]{0:T(1024)}, f32[12976]{0:T(1024)}, u32[]{:S(2)}, u32[]{:S(2)}) collective-permute-start(f32[12976]{0:T(1024)} %pad_maximum_fusion.1), channel_id=1, source_target_pairs={{0,1},{1,0},{2,3},{3,2},{4,5},{5,4},{6,7},{7,6},{8,9},{9,8},{10,11... | collective-permute-start | bytes 155720 | tf_op jit(solution)/shard_map/ppermute | solution.py:1074
  309.4 6.9 %copy-start.5 = (f32[8,1536]{1,0:T(8,128)S(1)}, f32[8,1536]{1,0:T(8,128)}, u32[]{:S(2)}) copy-start(f32[8,1536]{1,0:T(8,128)} %get-tuple-element.78) | copy-start | bytes 147460
  309.4 9.7 %copy-start.3 = (f32[96,256]{1,0:T(8,128)S(1)}, f32[96,256]{1,0:T(8,128)}, u32[]{:S(2)}) copy-start(f32[96,256]{1,0:T(8,128)} %slice.93) | copy-start | bytes 294916

commit v8 on v7

--- a/solution.py
+++ b/solution.py
@@ -300,30 +300,33 @@
 
     def start(self):
         greet(self.here, True)
-        for move in self.moves:
-            move.start()
+        self.moves[0].start()
         self.across.start()
         self.local.start()
 
     def step(self, at):
-        for when, chunk, hops in ((7, 0, 1), (11, 1, 1), (15, 0, 2), (19, 1, 2)):
-
-            def go(move=self.moves[chunk], hops=hops):
+        for when, chunk, hops in ((4, 0, 1), (9, 0, 2), (15, 0, 3), (19, 1, 1)):
+
+            def go(move=self.moves[chunk], chunk=chunk, hops=hops):
                 move.hop(hops)
                 move.sides(hops - 1)
+                if chunk == 0 and hops == 2:
+                    self.moves[1].start()
 
             pl.when(at == when)(go)
 
     def first(self):
-        for move in self.moves:
-            move.hop(3)
-            move.sides(2)
         self.moves[0].sides(3)
+        self.moves[1].hop(2)
         self.moves[0].finish()
 
     def finish(self):
-        self.moves[1].sides(3)
-        self.moves[1].finish()
+        move = self.moves[1]
+        move.sides(1)
+        move.hop(3)
+        move.sides(2)
+        move.sides(3)
+        move.finish()
         self.local.wait()
         self.across.wait()
 
@@ -407,10 +410,10 @@
         ends = (z == 0) | (z == 3)
         for n, block in enumerate(total.order):
             pl.when(at == n)(lambda z=block: total.cores(z))
-            pl.when(at == (4, 6, 7, 8)[n])(lambda z=block: total.stay(z))
-            pl.when(at == (5, 10, 15, 19)[n])(lambda z=block: total.sides(z))
+            pl.when(at == (4, 5, 7, 8)[n])(lambda z=block: total.stay(z))
+            pl.when(at == (6, 11, 17, 22)[n])(lambda z=block: total.sides(z))
         for n, block in enumerate(total.order[:3]):
-            when = jnp.where(ends, (5, 10, 15)[n], (11, 16, 17)[n])
+            when = jnp.where(ends, (6, 11, 17)[n], (12, 18, 19)[n])
             pl.when(at == when)(lambda z=block: total.pass_on(z))
 
     def finish(self):

time: 326 us -> 326 us (level)
    pallas_call x1, Pallas kernels: 76.7 us -> 71.2 us  [on_device(): pl.pallas_call(functools.partial(mixer_backward, own_links), name='mixer_...]
where the time goes in v8:
time: 326 us; the launch traced here: 324 us
  Pallas kernels  277 us (85%)
  other arithmetic  19.7 us (6%)
  local copies, waits for them, and re-layouts  14.6 us (4%)
  matrix products  9.43 us (3%)
    pallas_call x1, Pallas kernels, on_device(): pl.pallas_call(functools.partial(mixer_forward, own_links), name='mixer_f...  86.8 us
    pallas_call x1, Pallas kernels, on_device(): pl.pallas_call(functools.partial(mixer_backward, own_links), name='mixer_...  71.2 us
    pallas_call x1, Pallas kernels, reduce_tail(): pl.pallas_call(tail_kernel, name='tail', in_specs=[hbm] * 6 + [vmem] * 4,...  52.6 us
    pallas_call x1, Pallas kernels, gather_rows(): pl.pallas_call(gather_kernel, name='gather_rows', in_specs=[vmem] * 5, ou...  42.4 us
    pallas_call x1, Pallas kernels, on_device(): pl.pallas_call(functools.partial(gate_backward, float(unit_total)), name=...  24.1 us
    dot_general x1, matrix products, mm(): lax.dot_general(a, b, (((ca,), (cb,)), ((), ())), preferred_element_type=...  9.43 us
    add x1, other arithmetic, on_device(): cotangent.astype(f32)  6.92 us
  transfers between devices with their start and end apart: 1, of which 0 were waited for; matrix products, arithmetic and copies ran while one was open for 5% of the time, Pallas kernels for 0%

profile of v8, /device:TPU:0, one launch (start us, length us, event | category | flops | bytes accessed | tf_op | source)
XLA Modules:
  0.0 323.9 jit_solution(2428474508181799938)
XLA Ops:
  0.6 1.4 copy.29.w_step
  2.0 1.7 slice_bitcast_fusion.2
  3.7 1.3 broadcast_in_dim.4.gain
  5.1 42.4 %gather_rows.1 = (bf16[1024,1536]{1,0:T(8,128)(2,1)}, bf16[1536,1920]{1,0:T(8,128)(2,1)}) custom-call(bf16[512,1536]{1,0:T(8,128)(2,1)} %tokens_in.1, f32[8,1536]{1,0:T(8,128)} %broadcast_in_dim.4.gain, bf16[2,96,1536]{2,1,0:T(8,128)(2,1)} %refs_1_.1, bf16[96,256]{1,0:T(8,128)(2,1)} %w_state_io.1, bf16[96,24]{1,0:T(8,128)(2,1)} %copy.29.w_step), custom_call_target="tpu_custom_call" | custom-call | tf_op jit(solution)/shard_map/gather_rows/pallas_call | solution.py:782
  47.4 1.3 broadcast_in_dim.5.refs_3_.gain
  48.8 86.8 %mixer_forward.1 = (f32[1024,1536]{1,0:T(8,128)}, f32[1024,1536]{1,0:T(8,128)}, f32[4,1536,128]{2,1,0:T(8,128)}, f32[1024,256]{1,0:T(8,128)}, bf16[1024,256]{1,0...) custom-call(bf16[1024,1536]{1,0:T(8,128)(2,1)} %get-tuple-element.46, ...), custom_call_target="tpu_custom_call" | custom-call | flops 7650410496 | bytes 30000000 | tf_op jit(solution)/shard_map/mixer_forward/pallas_call | solution.py:1152
  135.6 24.1 %gate_backward.1 = (bf16[1024,1536]{1,0:T(8,128)(2,1)}, bf16[1024,1536]{1,0:T(8,128)(2,1)}, bf16[1024,1536]{1,0:T(8,128)(2,1)}, f32[8,1536]{1,0:T(8,128)}, bf16[...) custom-call(f32[8,1024]{1,0:T(8,128)} %get-tuple-element.48.stats, f32[1024,1536]{1,0:T(8,128)} %get-tuple-element.49.gate, ...), custom_call_target="tpu_custom_call" | custom-call | flops 9663676416 | bytes 45000000 | tf_op jit(solution)/shard_map/gate_backward/pallas_call | solution.py:1210
  159.7 9.4 %fusion.2.refs_0_ = bf16[1024,1536]{1,0:T(8,128)(2,1)} fusion(bf16[1024,1536]{1,0:T(8,128)(2,1)} %get-tuple-element.53, bf16[1536,3072]{1,0:T(8,128)(2,1)} %get-tuple-element.54.wb), kind=kOutput, calls=%fused_computation.5 | convolution fusion | flops 4833411072 | bytes 11010048 | tf_op jit(solution)/shard_map/dot_general | solution.py:24
  169.1 71.2 %mixer_backward.1 = (bf16[1024,1536]{1,0:T(8,128)(2,1)}, f32[8,1536]{1,0:T(8,128)}, bf16[1024,384]{1,0:T(8,128)(2,1)}, f32[8,256]{1,0:T(8,128)}, f32[8,128]{1,0:...) custom-call(f32[1024,1536]{1,0:T(8,128)} %get-tuple-element.55.inner, ...), custom_call_target="tpu_custom_call" | custom-call | flops 40000000000 | bytes 30000000 | tf_op jit(solution)/shard_map/mixer_backward/pallas_call | solution.py:1234
  240.3 0.0 copy-start.7
  240.3 0.0 copy-start.2
  240.3 0.0 copy-start.4
  240.3 52.6 %tail.1 = (f32[512,1536]{1,0:T(8,128)}, f32[1,96,1920]{2,1,0:T(8,128)}, f32[8,1536]{1,0:T(8,128)}) custom-call(bf16[1536,1024]{1,0:T(8,128)(2,1)} %get-tuple-element.67.normed_t, bf16[1024,1536]{1,0:T(8,128)(2,1)} %get-tuple-element.68.dinner, bf16[1024,384]{1,0:T(8,128)(2,1)} %get-tuple-element.69.dsd, bf16[1024,1536]{1,0:T(8,128)(2,1)} %get-tuple-element.70.dgate, ...), custom_call_target="tpu_custom_call" | custom-call | tf_op jit(solution)/shard_map/tail/pallas_call | solution.py:1060
  292.9 0.0 copy-start.1
  292.9 0.0 copy-start.6
  292.9 0.0 copy-start
  293.0 1.7 slice.93
  294.7 0.8 slice_reduce_fusion.2
  295.5 0.7 copy.30
  296.2 2.8 slice_bitcast_fusion.1
  299.0 0.0 copy-done.1
  299.0 1.2 multiply_reduce_fusion
  300.1 0.0 copy-done.6
  300.2 0.7 dynamic-slice_divide_fusion
  300.9 0.1 dynamic_slice.22
  301.0 0.8 fusion.19
  301.8 0.6 pad_maximum_fusion.1
  302.4 2.3 collective-permute-start
  304.8 0.4 fusion.13
  305.1 1.5 slice_reduce_fusion
  306.7 2.5 fusion.7
  309.2 1.1 pad_maximum_fusion
  310.3 6.9 %fusion.10 = (f32[512,1536]{1,0:T(8,128)}, bf16[512,1536]{1,0:T(8,128)(2,1)}) fusion(bf16[512,1536]{1,0:T(8,128)(2,1)S(1)} %copy-done, bf16[512,1536]{1,0:T(8,128)(2,1)} %refs_0_.1, f32[512,1536]{1,0:T(8,128)} %get-tuple-element.75, f32[512]{0:T(512)S(1)} %broadcast_multiply_fusion, f32[1536]{0:T(1024)S(1)} %copy-done.6, f32[512]{0:T(512)S(1)} %add_rsqrt_fusion, ...), kind=kLoop, calls=%fused_computation.11 | loop fusion | flops 10223616 | bytes 14166020 | tf_op jit(solution)/shard_map/add | solution.py:1284
  317.2 0.1 copy.31
  317.3 0.6 slice.99
  317.9 0.1 reshape_squeeze.7
  318.0 0.1 reshape.82
  318.1 0.6 reshape.83
  318.7 0.1 reshape.84
  318.8 0.6 reshape.85
  319.3 0.6 reduce_sum.49
  320.0 0.0 collective-permute-done
  320.0 0.0 copy-done.3
  320.0 0.8 fusion.17
  320.8 0.6 slice.97
  321.4 0.6 slice.100
  322.0 1.2 slice_add_fusion
  323.3 0.6 copy.33
  (14 shorter events, 0.1 us)
Async XLA Ops:
  240.3 55.2 %copy-start.7 = (bf16[96,24]{0,1:T(8,128)(2,1)S(1)}, bf16[96,24]{0,1:T(8,128)(2,1)}, u32[]{:S(2)}) copy-start(bf16[96,24]{0,1:T(8,128)(2,1)} %param.17) | copy-start | bytes 13828
  240.3 55.9 %copy-start.2 = (bf16[2,96,1536]{2,1,0:T(8,128)(2,1)S(1)}, bf16[2,96,1536]{2,1,0:T(8,128)(2,1)}, u32[]{:S(2)}) copy-start(bf16[2,96,1536]{2,1,0:T(8,128)(2,1)} %refs_1_.1) | copy-start | bytes 1769476
  240.3 58.7 %copy-start.4 = (bf16[96,256]{1,0:T(8,128)(2,1)S(1)}, bf16[96,256]{1,0:T(8,128)(2,1)}, u32[]{:S(2)}) copy-start(bf16[96,256]{1,0:T(8,128)(2,1)} %w_state_io.1) | copy-start | bytes 147460
  292.9 6.1 %copy-start.1 = (f32[1,96,1920]{2,1,0:T(8,128)S(1)}, f32[1,96,1920]{2,1,0:T(8,128)}, u32[]{:S(2)}) copy-start(f32[1,96,1920]{2,1,0:T(8,128)} %get-tuple-element.77) | copy-start | bytes 2211844
  292.9 7.2 %copy-start.6 = (f32[1536]{0:T(1024)S(1)}, f32[1536]{0:T(1024)}, u32[]{:S(2)}) copy-start(f32[1536]{0:T(1024)} %param.14) | copy-start | bytes 18436
  292.9 11.8 %copy-start = (bf16[512,1536]{1,0:T(8,128)(2,1)S(1)}, bf16[512,1536]{1,0:T(8,128)(2,1)}, u32[]{:S(2)}) copy-start(bf16[512,1536]{1,0:T(8,128)(2,1)} %tokens_in.1) | copy-start | bytes 4718596
  302.4 17.6 %collective-permute-start = (f32[12976]{0:T(1024)}, f32[12976]{0:T(1024)}, u32[]{:S(2)}, u32[]{:S(2)}) collective-permute-start(f32[12976]{0:T(1024)} %pad_maximum_fusion.1), channel_id=1, source_target_pairs={{0,1},{1,0},{2,3},{3,2},{4,5},{5,4},{6,7},{7,6},{8,9},{9,8},{10,11... | collective-permute-start | bytes 155720 | tf_op jit(solution)/shard_map/ppermute | solution.py:1077
  310.3 6.9 %copy-start.5 = (f32[8,1536]{1,0:T(8,128)S(1)}, f32[8,1536]{1,0:T(8,128)}, u32[]{:S(2)}) copy-start(f32[8,1536]{1,0:T(8,128)} %get-tuple-element.78) | copy-start | bytes 147460
  310.3 9.7 %copy-start.3 = (f32[96,256]{1,0:T(8,128)S(1)}, f32[96,256]{1,0:T(8,128)}, u32[]{:S(2)}) copy-start(f32[96,256]{1,0:T(8,128)} %slice.93) | copy-start | bytes 294916

commit v9 on v8

--- a/solution.py
+++ b/solution.py
@@ -212,7 +212,12 @@
         work.first()
         gates.start(0)
 
-    pl.when((i >= blocks) & (i < 2 * blocks))(gates.gate)
+
+    @pl.when((i >= blocks) & (i < 2 * blocks))
+    def _():
+        gates.gate()
+        work.between(i - blocks)
+
 
     @pl.when(i == 2 * blocks)
     def _():
@@ -317,13 +322,16 @@
 
     def first(self):
         self.moves[0].sides(3)
-        self.moves[1].hop(2)
         self.moves[0].finish()
+
+    def between(self, at):
+        move = self.moves[1]
+        pl.when(at == 1)(lambda: move.hop(2))
+        pl.when(at == 3)(lambda: move.sides(1))
+        pl.when(at == 5)(lambda: move.hop(3))
 
     def finish(self):
         move = self.moves[1]
-        move.sides(1)
-        move.hop(3)
         move.sides(2)
         move.sides(3)
         move.finish()
@@ -932,8 +940,8 @@
 
 
 def tail_kernel(
-    normed_t, dinner, dsd, dgate, wb, wa, gk, ggg, gks, hs, gn_out, shard_out, small_out,
-    nt_v, dinner_v, dsd_v, dgate_v, wg_v, wa_v, away, came, total, landed, loads, send_x, recv_x, send, recv, *scratch,
+    normed_t, dinner, dsd, dgate, wb, wa, gk, ggg, gks, hs, norm_gain, w_gate_inner, w_state_io, w_step, gate_grads,
+    gn_out, inner_out, step_out, both_out, small_out, shard_out, give, got, send_g, recv_g, nt_v, dinner_v, dsd_v, dgate_v, wg_v, wa_v, away, came, total, landed, loads, send_x, recv_x, send, recv, *scratch,
 ):
     here = Place()
     half = lax.axis_index("tensor")
@@ -1046,10 +1054,45 @@
         gn_out[:, at] = gn_out[:, at] + came[n].astype(f32)
         return carry
 
+    inner_out[0] = gate_grads[0]
+    inner_out[1] = shard_out[0, :, :units]
+    step_out[...] = shard_out[0, :, units + BW :]
+    count = work.rows
+    part = shard_out[0, :, units + BW :] * mm(w_step[...], as_places(w_step.shape[1]))
+    for c in range(2):
+        at = slice(units + c * 128, units + c * 128 + 128)
+        part = part + shard_out[0, :, at] * w_state_io[:, c * 128 : c * 128 + 128].astype(f32)
+    for c in range(units // 128):
+        at = slice(c * 128, c * 128 + 128)
+        part = part + gate_grads[0, :, at] * w_gate_inner[0, :, at].astype(f32)
+        part = part + shard_out[0, :, at] * w_gate_inner[1, :, at].astype(f32)
+    part = jnp.concatenate([part, jnp.zeros((128 - count, 128), f32)], axis=0)
+    row = jnp.sum(jnp.transpose(part), axis=0, keepdims=True)
+    shape = (norm_gain.shape[1], 128)
+    pick = (iota(shape, 0) == iota(shape, 1) + here.me * count) & (iota(shape, 1) < count)
+    gain = lay(norm_gain[...], pick.astype(f32).astype(bf16))[0:1]
+    row = row / jnp.where(iota((1, 128), 1) < count, gain, 1.0)
+    low = pltpu.roll(row, 128 - count // 2, 1)
+    first = half == 0
+
+    def share(at, a, b):
+        both_out[at] = jnp.where(first, a, b)
+        give[at] = jnp.where(first, b, a)
+
+    share(slice(0, count), shard_out[0, :, units : units + 128], shard_out[0, :, units + 128 : units + 256])
+    for k in range(5):
+        pair = [small_out[7:8, k * BW + c * 128 : k * BW + c * 128 + 128] for c in range(2)]
+        share(slice(count + k, count + k + 1), *pair)
+    share(slice(count + 5, count + 6), row, low)
+    share(slice(count + 6, count + 8), jnp.zeros((2, 128), f32), jnp.zeros((2, 128), f32))
+    last = remote(give, got, send_g, recv_g, tensor=1 - half)
+    last.start()
     lax.fori_loop(0, chunks, arrive, 0)
-
-
-def reduce_tail(normed_t, dinner, dsd, dgate, wb, wa, sums, ways, collective_id):
+    last.wait()
+    both_out[...] = both_out[...] + got[...]
+
+
+def reduce_tail(normed_t, dinner, dsd, dgate, wb, wa, sums, weights, ways, collective_id):
     width, tokens = normed_t.shape
     small = sums[0]
     units, cols, rows = dgate.shape[1], wa.shape[1], width // ways
@@ -1058,9 +1101,12 @@
     hbm = pl.BlockSpec(memory_space=pl.ANY)
     sem = pltpu.SemaphoreType.DMA
     return pl.pallas_call(
-        tail_kernel, name="tail", in_specs=[hbm] * 6 + [vmem] * 4, out_specs=[vmem] * 3,
-        out_shape=[sds((tokens // 2, width)), sds((1, rows, cols)), sds(small.shape)],
+        tail_kernel, name="tail", in_specs=[hbm] * 6 + [vmem] * 9, out_specs=[vmem] * 5,
+        out_shape=[
+            sds((tokens // 2, width)), sds((2, rows, units)), sds((rows, 128)), sds((rows + 8, 128)), sds(small.shape),
+        ],
         scratch_shapes=[
+            pltpu.VMEM((1, rows, cols), f32), pltpu.VMEM((rows + 8, 128), f32), pltpu.VMEM((rows + 8, 128), f32), sem, sem,
             pltpu.VMEM(normed_t.shape, bf16), pltpu.VMEM(dinner.shape, bf16), pltpu.VMEM(dsd.shape, bf16),
             pltpu.VMEM(dgate.shape, bf16), pltpu.VMEM((width, units), bf16), pltpu.VMEM(wa.shape, bf16),
             pltpu.VMEM((chunks, tokens // 2, BW), bf16), pltpu.VMEM((chunks, tokens // 2, BW), bf16),
@@ -1070,7 +1116,7 @@
         compiler_params=pltpu.CompilerParams(
             collective_id=collective_id, has_side_effects=True, vmem_limit_bytes=62 * 1024 * 1024
         ),
-    )(normed_t, dinner, dsd, dgate, wb, wa, *sums)
+    )(normed_t, dinner, dsd, dgate, wb, wa, *sums, *weights)
 
 
 def swap(v):
@@ -1133,10 +1179,9 @@
     scaled = rows_in * rstd_in
     pack_a = jnp.concatenate([w_gate_inner[1], w_state_io, spread(w_step)], axis=1)
     w_output_t = w_output.T
+    gain_in = jnp.broadcast_to(norm_gain[None], (8, width))
     if own_links:
-        normed, wa = gather_rows(
-            residual, jnp.broadcast_to(norm_gain[None], (8, width)), w_gate_inner, w_state_io, w_step, ways, 1
-        )
+        normed, wa = gather_rows(residual, gain_in, w_gate_inner, w_state_io, w_step, ways, 1)
     else:
         wa = lax.all_gather(pack_a, "dp", axis=0, tiled=True)
         normed = lax.all_gather((scaled * norm_gain).astype(bf16), "tensor", axis=0, tiled=True)
@@ -1269,8 +1314,11 @@
     output = (rows_in + mixed_near.astype(f32) + mixed_got.astype(f32)).astype(bf16)
 
     if own_links:
-        grad_normed, wa_shard, small = reduce_tail(normed_t, dinner, dsd, dgate, wb, wa, (gk, ggg, gks, hs), ways, 5)
-        wa_shard = wa_shard[0]
+        weights = (gain_in, w_gate_inner, w_state_io, w_step, wb_shard)
+        sums = (gk, ggg, gks, hs)
+        grad_normed, inner_grads, step_grads, both, small = reduce_tail(
+            normed_t, dinner, dsd, dgate, wb, wa, sums, weights, ways, 5
+        )
     else:
         last = jnp.concatenate([gks[:5].reshape(-1), hs[0], hs[1]])
         small = jnp.concatenate([gk[:6], ggg[:1], last[None]], axis=0)
@@ -1285,31 +1333,36 @@
         grad_v - scaled * jnp.mean(grad_v * scaled, axis=1, keepdims=True)
     )
 
-    conv_state_sum = small[7, : 5 * BW].reshape(5, BW)
     bias_sum = gathered_heads(small[7, 5 * BW : 5 * BW + 128], heads)
     decay_sum = gathered_heads(small[7, 5 * BW + 128 : 5 * BW + 256], heads)
     skip_sum = jnp.sum(small[5].reshape(heads, HEAD), axis=1)
 
-    gain_rows = jnp.sum(wb_shard[0] * w_gate_inner[0].astype(f32), axis=1) + jnp.sum(
-        wa_shard * pack_a.astype(f32), axis=1
-    )
-    count = gain_rows.shape[0]
-    gain_own = gain_rows / lax.dynamic_slice_in_dim(norm_gain, lax.axis_index("dp") * count, count)
-    near_s, far_s = halves(jnp.concatenate([wa_shard[:, units : units + BW], conv_state_sum], axis=0), 1)
-    near_g, far_g = halves(gain_own, 0)
-    far_all = jnp.concatenate([far_s.reshape(-1), far_g])
-    got = swap(far_all)
-    both = near_s + got[: far_s.size].reshape(far_s.shape)
-    gain_part = near_g + got[far_s.size :]
+    count = width // ways
+    if own_links:
+        gain_part = both[count + 5, : count // 2]
+    else:
+        conv_state_sum = small[7, : 5 * BW].reshape(5, BW)
+        gain_rows = jnp.sum(wb_shard[0] * w_gate_inner[0].astype(f32), axis=1) + jnp.sum(
+            wa_shard * pack_a.astype(f32), axis=1
+        )
+        gain_own = gain_rows / lax.dynamic_slice_in_dim(norm_gain, lax.axis_index("dp") * count, count)
+        near_s, far_s = halves(jnp.concatenate([wa_shard[:, units : units + BW], conv_state_sum], axis=0), 1)
+        near_g, far_g = halves(gain_own, 0)
+        far_all = jnp.concatenate([far_s.reshape(-1), far_g])
+        got = swap(far_all)
+        both = near_s + got[: far_s.size].reshape(far_s.shape)
+        gain_part = near_g + got[far_s.size :]
+        inner_grads = jnp.stack([wb_shard[0], wa_shard[:, :units]])
+        step_grads = wa_shard[:, units + BW :]
     return (
         output,
         grad_residual,
         gain_part,
-        jnp.stack([wb_shard[0], wa_shard[:, :units]]),
+        inner_grads,
         both[:count],
-        gathered_heads(wa_shard[:, units + BW :], heads),
+        gathered_heads(step_grads, heads),
         small[0:5],
-        both[count:],
+        both[count : count + 5],
         bias_sum,
         decay_sum,
         skip_sum,

time: 326 us -> 318 us (0.975)
  other arithmetic: 19.7 us -> 10.5 us
  Pallas kernels: 277 us -> 283 us
    pallas_call x1, Pallas kernels: 52.6 us -> 57.8 us  [reduce_tail(): pl.pallas_call(tail_kernel, name='tail', in_specs=[hbm] * 6 + [vmem] * 9,...]
  transfers between devices with their start and end apart: 1 -> 0, of which waited for: 0 -> 0; matrix products, arithmetic and copies ran while one was open for 5% -> 0% of each run, Pallas kernels for 0% -> 0%
where the time goes in v9:
time: 318 us; the launch traced here: 316 us
  Pallas kernels  283 us (89%)
  local copies, waits for them, and re-layouts  12.4 us (4%)
  other arithmetic  10.5 us (3%)
  matrix products  9.43 us (3%)
    pallas_call x1, Pallas kernels, on_device(): pl.pallas_call(functools.partial(mixer_forward, own_links), name='mixer_f...  87.2 us
    pallas_call x1, Pallas kernels, on_device(): pl.pallas_call(functools.partial(mixer_backward, own_links), name='mixer_...  71.1 us
    pallas_call x1, Pallas kernels, reduce_tail(): pl.pallas_call(tail_kernel, name='tail', in_specs=[hbm] * 6 + [vmem] * 9,...  57.8 us
    pallas_call x1, Pallas kernels, gather_rows(): pl.pallas_call(gather_kernel, name='gather_rows', in_specs=[vmem] * 5, ou...  42.4 us
    pallas_call x1, Pallas kernels, on_device(): pl.pallas_call(functools.partial(gate_backward, float(unit_total)), name=...  24.1 us
    dot_general x1, matrix products, mm(): lax.dot_general(a, b, (((ca,), (cb,)), ((), ())), preferred_element_type=...  9.43 us
    add x1, other arithmetic, on_device(): cotangent.astype(f32)  6.99 us

profile of v9, /device:TPU:0, one launch (start us, length us, event | category | flops | bytes accessed | tf_op | source)
XLA Modules:
  0.0 315.6 jit_solution(6553637619830865447)
XLA Ops:
  0.6 1.3 broadcast_in_dim.4.gain.norm_gain
  2.0 1.4 copy.29.w_step
  3.4 42.4 %gather_rows.1 = (bf16[1024,1536]{1,0:T(8,128)(2,1)}, bf16[1536,1920]{1,0:T(8,128)(2,1)}) custom-call(bf16[512,1536]{1,0:T(8,128)(2,1)} %tokens_in.1, f32[8,1536]{1,0:T(8,128)} %broadcast_in_dim.4.gain.norm_gain, bf16[2,96,1536]{2,1,0:T(8,128)(2,1)} %w_gate_inner.3, bf16[96,256]{1,0:T(8,128)(2,1)} %w_state_io.3, bf16[96,24]{1,0:T(8,128)(2,1)} %copy.29.w_step), custom_call_target="tpu_custom_call" | custom-call | tf_op jit(solution)/shard_map/gather_rows/pallas_call | solution.py:790
  45.7 1.3 broadcast_in_dim.5.refs_3_.gain
  47.1 87.2 %mixer_forward.1 = (f32[1024,1536]{1,0:T(8,128)}, f32[1024,1536]{1,0:T(8,128)}, f32[4,1536,128]{2,1,0:T(8,128)}, f32[1024,256]{1,0:T(8,128)}, bf16[1024,256]{1,0...) custom-call(bf16[1024,1536]{1,0:T(8,128)(2,1)} %get-tuple-element.48, ...), custom_call_target="tpu_custom_call" | custom-call | flops 7650410496 | bytes 30000000 | tf_op jit(solution)/shard_map/mixer_forward/pallas_call | solution.py:1197
  134.3 24.1 %gate_backward.1 = (bf16[1024,1536]{1,0:T(8,128)(2,1)}, bf16[1024,1536]{1,0:T(8,128)(2,1)}, bf16[1024,1536]{1,0:T(8,128)(2,1)}, f32[8,1536]{1,0:T(8,128)}, bf16[...) custom-call(f32[8,1024]{1,0:T(8,128)} %get-tuple-element.50.stats, f32[1024,1536]{1,0:T(8,128)} %get-tuple-element.51.gate, ...), custom_call_target="tpu_custom_call" | custom-call | flops 9663676416 | bytes 45000000 | tf_op jit(solution)/shard_map/gate_backward/pallas_call | solution.py:1255
  158.3 9.4 %fusion.2.refs_0_ = bf16[1024,1536]{1,0:T(8,128)(2,1)} fusion(bf16[1024,1536]{1,0:T(8,128)(2,1)} %get-tuple-element.55, bf16[1536,3072]{1,0:T(8,128)(2,1)} %get-tuple-element.56.wb), kind=kOutput, calls=%fused_computation.5 | convolution fusion | flops 4833411072 | bytes 11010048 | tf_op jit(solution)/shard_map/dot_general | solution.py:24
  167.8 71.1 %mixer_backward.1 = (bf16[1024,1536]{1,0:T(8,128)(2,1)}, f32[8,1536]{1,0:T(8,128)}, bf16[1024,384]{1,0:T(8,128)(2,1)}, f32[8,256]{1,0:T(8,128)}, f32[8,128]{1,0:...) custom-call(f32[1024,1536]{1,0:T(8,128)} %get-tuple-element.57.inner, ...), custom_call_target="tpu_custom_call" | custom-call | flops 40000000000 | bytes 30000000 | tf_op jit(solution)/shard_map/mixer_backward/pallas_call | solution.py:1279
  238.9 0.0 copy-start
  238.9 0.0 copy-start.3
  238.9 57.8 %tail.1 = (f32[512,1536]{1,0:T(8,128)}, f32[2,96,1536]{2,1,0:T(8,128)}, f32[96,128]{1,0:T(8,128)}, f32[104,128]{1,0:T(8,128)}, f32[8,1536]{1,0:T(8,128)}) custom-call(bf16[1536,1024]{1,0:T(8,128)(2,1)} %get-tuple-element.69.normed_t, bf16[1024,1536]{1,0:T(8,128)(2,1)} %get-tuple-element.70.dinner, bf16[1024,384]{1,0:T(8,128)(2,1)} %get-tuple-element.71.dsd, ...), custom_call_target="tpu_custom_call" | custom-call | tf_op jit(solution)/shard_map/tail/pallas_call | solution.py:1103
  296.7 0.0 copy-done
  296.7 0.4 fusion.13
  297.1 0.0 copy-done.3
  297.1 2.5 fusion.7
  299.7 0.0 copy-start.4
  299.7 0.0 copy-start.5
  299.7 0.0 copy-start.2
  299.7 0.0 copy-start.1
  299.7 7.0 %fusion.10 = (f32[512,1536]{1,0:T(8,128)}, bf16[512,1536]{1,0:T(8,128)(2,1)}) fusion(bf16[512,1536]{1,0:T(8,128)(2,1)S(1)} %copy-done, bf16[512,1536]{1,0:T(8,128)(2,1)} %refs_0_.1, f32[512,1536]{1,0:T(8,128)} %get-tuple-element.78, f32[512]{0:T(512)S(1)} %broadcast_multiply_fusion, f32[1536]{0:T(1024)S(1)} %copy-done.3, f32[512]{0:T(512)S(1)} %add_rsqrt_fusion, ...), kind=kLoop, calls=%fused_computation.11 | loop fusion | flops 10223616 | bytes 14166020 | tf_op jit(solution)/shard_map/add | solution.py:1332
  306.7 0.0 copy-done.4
  306.7 0.6 slice.50
  307.3 0.0 copy-done.5
  307.3 0.1 copy.31
  307.4 0.6 slice.62
  308.0 0.0 copy-done.2
  308.0 0.6 slice_reduce_fusion
  308.6 0.1 reshape_squeeze.3
  308.7 0.6 reduce_sum.29
  309.3 0.1 reshape.64
  309.4 0.6 reshape.65
  310.0 0.1 reshape.66
  310.1 0.6 reshape.67
  310.7 0.6 slice.54
  311.3 0.5 slice_bitcast_fusion.1
  311.8 0.0 copy-done.1
  311.8 0.9 slice_bitcast_fusion
  312.7 2.4 copy.34
  315.0 0.6 copy.35
  (3 shorter events, 0.0 us)
Async XLA Ops:
  238.9 57.8 %copy-start = (bf16[512,1536]{1,0:T(8,128)(2,1)S(1)}, bf16[512,1536]{1,0:T(8,128)(2,1)}, u32[]{:S(2)}) copy-start(bf16[512,1536]{1,0:T(8,128)(2,1)} %tokens_in.1) | copy-start | bytes 4718596
  238.9 58.2 %copy-start.3 = (f32[1536]{0:T(1024)S(1)}, f32[1536]{0:T(1024)}, u32[]{:S(2)}) copy-start(f32[1536]{0:T(1024)} %param.14) | copy-start | bytes 18436
  299.7 7.0 %copy-start.4 = (f32[104,128]{1,0:T(8,128)S(1)}, f32[104,128]{1,0:T(8,128)}, u32[]{:S(2)}) copy-start(f32[104,128]{1,0:T(8,128)} %get-tuple-element.79) | copy-start | bytes 159748
  299.7 7.6 %copy-start.5 = (f32[96,128]{1,0:T(8,128)S(1)}, f32[96,128]{1,0:T(8,128)}, u32[]{:S(2)}) copy-start(f32[96,128]{1,0:T(8,128)} %get-tuple-element.81) | copy-start | bytes 147460
  299.7 8.3 %copy-start.2 = (f32[8,1536]{1,0:T(8,128)S(1)}, f32[8,1536]{1,0:T(8,128)}, u32[]{:S(2)}) copy-start(f32[8,1536]{1,0:T(8,128)} %get-tuple-element.82) | copy-start | bytes 147460
  299.7 12.1 %copy-start.1 = (f32[2,96,1536]{2,1,0:T(8,128)S(1)}, f32[2,96,1536]{2,1,0:T(8,128)}, u32[]{:S(2)}) copy-start(f32[2,96,1536]{2,1,0:T(8,128)} %get-tuple-element.77.gate_grads) | copy-start | bytes 3538948

commit v10 on v9

--- a/solution.py
+++ b/solution.py
@@ -243,7 +243,7 @@
         return pltpu.make_async_copy(self.cot, self.cot_v, self.cl.at[0])
 
     def start(self, which):
-        if which:
+        if not which:
             self.tokens().start()
         for n in range(self.blocks):
             self.load(which, n).start()
@@ -305,38 +305,34 @@
 
     def start(self):
         greet(self.here, True)
-        self.moves[0].start()
+        for move in self.moves:
+            move.start()
         self.across.start()
         self.local.start()
 
     def step(self, at):
-        for when, chunk, hops in ((4, 0, 1), (9, 0, 2), (15, 0, 3), (19, 1, 1)):
-
-            def go(move=self.moves[chunk], chunk=chunk, hops=hops):
+        for when, chunk, hops in ((6, 0, 1), (10, 1, 1), (14, 0, 2), (18, 1, 2), (22, 0, 3)):
+
+            def go(move=self.moves[chunk], hops=hops):
                 move.hop(hops)
                 move.sides(hops - 1)
-                if chunk == 0 and hops == 2:
-                    self.moves[1].start()
 
             pl.when(at == when)(go)
 
     def first(self):
         self.moves[0].sides(3)
+        self.moves[1].hop(3)
         self.moves[0].finish()
+        self.local.wait()
+        self.across.wait()
 
     def between(self, at):
-        move = self.moves[1]
-        pl.when(at == 1)(lambda: move.hop(2))
-        pl.when(at == 3)(lambda: move.sides(1))
-        pl.when(at == 5)(lambda: move.hop(3))
+        pl.when(at == 1)(lambda: self.moves[1].sides(2))
 
     def finish(self):
         move = self.moves[1]
-        move.sides(2)
         move.sides(3)
         move.finish()
-        self.local.wait()
-        self.across.wait()
 
 
 def gate_forward(normed, cot, wg, wo, ssd, gain, gate_out, ggo_out, stats_out, sq, gi):
@@ -654,6 +650,7 @@
         self.here, self.full, self.ss, self.rs, self.chunk, self.cols = here, full, ss, rs, chunk, cols
         self.rows = own.shape[0]
         self.own = own
+        self.lift = chunk == 0
         self.local = pltpu.make_async_copy(own, self.slot(here.me), ls.at[chunk])
 
     def slot(self, origin):
@@ -669,61 +666,61 @@
     def arrived(self, origin):
         self.copy(origin, 3).wait_recv()
 
-    def each_send(self, act):
+    def ways(self, hops):
+        z = self.here.z
+        return ((0, z),) if hops == 0 else ((0, z - hops), (1, z + hops))
+
+    def onward(self, way):
+        return (self.here.z < 3) if way == 0 else (self.here.z > 0)
+
+    def own_sends(self, hops, way, origin_z, act):
         here = self.here
-        for hops in range(4):
-            for way, origin_z in ((0, here.z - hops), (1, here.z + hops)):
-                if hops == 0:
-                    if way == 1:
-                        continue
-                    origin = here.me
-                    pl.when(here.z < 3)(lambda o=origin: act(o, 0))
-                    pl.when(here.z > 0)(lambda o=origin: act(o, 1))
-                    act(origin, 2)
-                    act(origin, 3)
-                    continue
-                origin = here.at(origin_z, here.y, here.c)
-
-                def go(o=origin, way=way):
-                    pl.when((here.z < 3) if way == 0 else (here.z > 0))(lambda: act(o, way))
-                    act(o, 2)
-                    act(o, 3)
-
-                pl.when((origin_z >= 0) & (origin_z <= 3))(go)
+        origin = here.at(origin_z, here.y, here.c)
+        for along in (0, 1) if hops == 0 else (way,):
+            pl.when(self.onward(along))(lambda along=along: act(origin, along))
+        if hops and self.lift:
+            pl.when((origin_z != 0) & (origin_z != 3))(lambda: act(origin, 2))
+        else:
+            act(origin, 2)
+        act(origin, 3)
+
+    def side_sends(self, hops, way, origin_z, act):
+        here = self.here
+        origin = here.at(origin_z, 1 - here.y, here.c)
+        act(origin, 3)
+        if self.lift and hops == 0:
+            pl.when(here.z == 0)(lambda: act(origin, 0))
+            pl.when(here.z == 3)(lambda: act(origin, 1))
+        elif self.lift:
+            pl.when((origin_z == 3 * way) & self.onward(way))(lambda: act(origin, way))
+
+    def each(self, hops, act):
+        for way, origin_z in self.ways(hops):
+            if hops == 0:
+                act(way, origin_z)
+            else:
+                pl.when((origin_z >= 0) & (origin_z <= 3))(lambda way=way, origin_z=origin_z: act(way, origin_z))
+
+    def send(self, origin, way):
+        self.copy(origin, way).start()
 
     def start(self):
-        here = self.here
-        pl.when(here.z < 3)(lambda: self.copy(here.me, 0, self.own).start())
-        pl.when(here.z > 0)(lambda: self.copy(here.me, 1, self.own).start())
-        self.copy(here.me, 2, self.own).start()
-        self.copy(here.me, 3, self.own).start()
+        self.own_sends(0, 0, self.here.z, lambda origin, way: self.copy(origin, way, self.own).start())
         self.local.start()
 
     def hop(self, hops):
-        here = self.here
-        for way, origin_z in ((0, here.z - hops), (1, here.z + hops)):
-
-            def go(way=way, origin_z=origin_z):
-                origin = here.at(origin_z, here.y, here.c)
-                self.arrived(origin)
-                pl.when((here.z < 3) if way == 0 else (here.z > 0))(lambda: self.copy(origin, way).start())
-                self.copy(origin, 2).start()
-                self.copy(origin, 3).start()
-
-            pl.when((origin_z >= 0) & (origin_z <= 3))(go)
+        def go(way, origin_z):
+            self.arrived(self.here.at(origin_z, self.here.y, self.here.c))
+            self.own_sends(hops, way, origin_z, self.send)
+
+        self.each(hops, go)
 
     def sides(self, hops):
-        here = self.here
-        for way, origin_z in ((0, here.z - hops), (1, here.z + hops)):
-            if hops == 0 and way == 1:
-                continue
-
-            def go(origin_z=origin_z):
-                origin = here.at(origin_z, 1 - here.y, here.c)
-                self.arrived(origin)
-                self.copy(origin, 3).start()
-
-            pl.when((origin_z >= 0) & (origin_z <= 3))(go)
+        def go(way, origin_z):
+            self.arrived(self.here.at(origin_z, 1 - self.here.y, self.here.c))
+            self.side_sends(hops, way, origin_z, self.send)
+
+        self.each(hops, go)
 
     def finish(self):
         here = self.here
@@ -731,9 +728,17 @@
         for z in range(4):
             for y in range(2):
                 self.arrived(here.at(z, y, 1 - here.c))
-        self.each_send(lambda origin, way: self.copy(origin, way).wait_send())
-        for z in range(4):
-            self.copy(here.at(z, 1 - here.y, here.c), 3).wait_send()
+
+        def sent(origin, way):
+            self.copy(origin, way).wait_send()
+
+        for hops in range(4):
+
+            def go(way, origin_z, hops=hops):
+                self.own_sends(hops, way, origin_z, sent)
+                self.side_sends(hops, way, origin_z, sent)
+
+            self.each(hops, go)
 
 
 def gather_scratch():

time: 318 us -> 312 us (0.981)
  Pallas kernels: 283 us -> 276 us
    pallas_call x1, Pallas kernels: 87.2 us -> 80.2 us  [on_device(): pl.pallas_call(functools.partial(mixer_forward, own_links), name='mixer_f...]
where the time goes in v10:
time: 312 us; the launch traced here: 309 us
  Pallas kernels  276 us (88%)
  local copies, waits for them, and re-layouts  12.4 us (4%)
  other arithmetic  10.5 us (3%)
  matrix products  9.43 us (3%)
    pallas_call x1, Pallas kernels, on_device(): pl.pallas_call(functools.partial(mixer_forward, own_links), name='mixer_f...  80.2 us
    pallas_call x1, Pallas kernels, on_device(): pl.pallas_call(functools.partial(mixer_backward, own_links), name='mixer_...  72.2 us
    pallas_call x1, Pallas kernels, reduce_tail(): pl.pallas_call(tail_kernel, name='tail', in_specs=[hbm] * 6 + [vmem] * 9,...  57.3 us
    pallas_call x1, Pallas kernels, gather_rows(): pl.pallas_call(gather_kernel, name='gather_rows', in_specs=[vmem] * 5, ou...  42.4 us
    pallas_call x1, Pallas kernels, on_device(): pl.pallas_call(functools.partial(gate_backward, float(unit_total)), name=...  24.1 us
    dot_general x1, matrix products, mm(): lax.dot_general(a, b, (((ca,), (cb,)), ((), ())), preferred_element_type=...  9.43 us
    add x1, other arithmetic, on_device(): cotangent.astype(f32)  6.99 us

profile of v10, /device:TPU:0, one launch (start us, length us, event | category | flops | bytes accessed | tf_op | source)
XLA Modules:
  0.0 309.4 jit_solution(1311164496720615274)
XLA Ops:
  0.6 1.3 broadcast_in_dim.4.gain.norm_gain
  2.0 1.4 copy.29.w_step
  3.4 42.4 %gather_rows.1 = (bf16[1024,1536]{1,0:T(8,128)(2,1)}, bf16[1536,1920]{1,0:T(8,128)(2,1)}) custom-call(bf16[512,1536]{1,0:T(8,128)(2,1)} %tokens_in.1, f32[8,1536]{1,0:T(8,128)} %broadcast_in_dim.4.gain.norm_gain, bf16[2,96,1536]{2,1,0:T(8,128)(2,1)} %w_gate_inner.3, bf16[96,256]{1,0:T(8,128)(2,1)} %w_state_io.3, bf16[96,24]{1,0:T(8,128)(2,1)} %copy.29.w_step), custom_call_target="tpu_custom_call" | custom-call | tf_op jit(solution)/shard_map/gather_rows/pallas_call | solution.py:795
  45.8 1.3 broadcast_in_dim.5.refs_3_.gain
  47.1 80.2 %mixer_forward.1 = (f32[1024,1536]{1,0:T(8,128)}, f32[1024,1536]{1,0:T(8,128)}, f32[4,1536,128]{2,1,0:T(8,128)}, f32[1024,256]{1,0:T(8,128)}, bf16[1024,256]{1,0...) custom-call(bf16[1024,1536]{1,0:T(8,128)(2,1)} %get-tuple-element.48, ...), custom_call_target="tpu_custom_call" | custom-call | flops 7650410496 | bytes 30000000 | tf_op jit(solution)/shard_map/mixer_forward/pallas_call | solution.py:1202
  127.3 24.1 %gate_backward.1 = (bf16[1024,1536]{1,0:T(8,128)(2,1)}, bf16[1024,1536]{1,0:T(8,128)(2,1)}, bf16[1024,1536]{1,0:T(8,128)(2,1)}, f32[8,1536]{1,0:T(8,128)}, bf16[...) custom-call(f32[8,1024]{1,0:T(8,128)} %get-tuple-element.50.stats, f32[1024,1536]{1,0:T(8,128)} %get-tuple-element.51.gate, ...), custom_call_target="tpu_custom_call" | custom-call | flops 9663676416 | bytes 45000000 | tf_op jit(solution)/shard_map/gate_backward/pallas_call | solution.py:1260
  151.4 9.4 %fusion.2.refs_0_ = bf16[1024,1536]{1,0:T(8,128)(2,1)} fusion(bf16[1024,1536]{1,0:T(8,128)(2,1)} %get-tuple-element.55, bf16[1536,3072]{1,0:T(8,128)(2,1)} %get-tuple-element.56.wb), kind=kOutput, calls=%fused_computation.5 | convolution fusion | flops 4833411072 | bytes 11010048 | tf_op jit(solution)/shard_map/dot_general | solution.py:24
  160.8 72.2 %mixer_backward.1 = (bf16[1024,1536]{1,0:T(8,128)(2,1)}, f32[8,1536]{1,0:T(8,128)}, bf16[1024,384]{1,0:T(8,128)(2,1)}, f32[8,256]{1,0:T(8,128)}, f32[8,128]{1,0:...) custom-call(f32[1024,1536]{1,0:T(8,128)} %get-tuple-element.57.inner, ...), custom_call_target="tpu_custom_call" | custom-call | flops 40000000000 | bytes 30000000 | tf_op jit(solution)/shard_map/mixer_backward/pallas_call | solution.py:1284
  233.1 0.0 copy-start
  233.1 0.0 copy-start.3
  233.1 57.3 %tail.1 = (f32[512,1536]{1,0:T(8,128)}, f32[2,96,1536]{2,1,0:T(8,128)}, f32[96,128]{1,0:T(8,128)}, f32[104,128]{1,0:T(8,128)}, f32[8,1536]{1,0:T(8,128)}) custom-call(bf16[1536,1024]{1,0:T(8,128)(2,1)} %get-tuple-element.69.normed_t, bf16[1024,1536]{1,0:T(8,128)(2,1)} %get-tuple-element.70.dinner, bf16[1024,384]{1,0:T(8,128)(2,1)} %get-tuple-element.71.dsd, ...), custom_call_target="tpu_custom_call" | custom-call | tf_op jit(solution)/shard_map/tail/pallas_call | solution.py:1108
  290.4 0.0 copy-done
  290.4 0.4 fusion.13
  290.8 0.0 copy-done.3
  290.8 2.5 fusion.7
  293.4 0.0 copy-start.4
  293.4 0.0 copy-start.5
  293.4 0.0 copy-start.2
  293.4 0.0 copy-start.1
  293.4 7.0 %fusion.10 = (f32[512,1536]{1,0:T(8,128)}, bf16[512,1536]{1,0:T(8,128)(2,1)}) fusion(bf16[512,1536]{1,0:T(8,128)(2,1)S(1)} %copy-done, bf16[512,1536]{1,0:T(8,128)(2,1)} %refs_0_.1, f32[512,1536]{1,0:T(8,128)} %get-tuple-element.78, f32[512]{0:T(512)S(1)} %broadcast_multiply_fusion, f32[1536]{0:T(1024)S(1)} %copy-done.3, f32[512]{0:T(512)S(1)} %add_rsqrt_fusion, ...), kind=kLoop, calls=%fused_computation.11 | loop fusion | flops 10223616 | bytes 14166020 | tf_op jit(solution)/shard_map/add | solution.py:1337
  300.4 0.0 copy-done.4
  300.4 0.6 slice.50
  301.0 0.0 copy-done.5
  301.0 0.1 copy.31
  301.1 0.6 slice.62
  301.7 0.0 copy-done.2
  301.7 0.6 slice_reduce_fusion
  302.3 0.1 reshape_squeeze.3
  302.4 0.6 reduce_sum.29
  303.1 0.1 reshape.64
  303.1 0.6 reshape.65
  303.7 0.1 reshape.66
  303.8 0.6 reshape.67
  304.4 0.6 slice.54
  305.0 0.5 slice_bitcast_fusion.1
  305.5 0.0 copy-done.1
  305.5 0.9 slice_bitcast_fusion
  306.4 2.4 copy.34
  308.7 0.6 copy.35
  (3 shorter events, 0.0 us)
Async XLA Ops:
  233.1 57.4 %copy-start = (bf16[512,1536]{1,0:T(8,128)(2,1)S(1)}, bf16[512,1536]{1,0:T(8,128)(2,1)}, u32[]{:S(2)}) copy-start(bf16[512,1536]{1,0:T(8,128)(2,1)} %tokens_in.1) | copy-start | bytes 4718596
  233.1 57.8 %copy-start.3 = (f32[1536]{0:T(1024)S(1)}, f32[1536]{0:T(1024)}, u32[]{:S(2)}) copy-start(f32[1536]{0:T(1024)} %param.14) | copy-start | bytes 18436
  293.4 7.0 %copy-start.4 = (f32[104,128]{1,0:T(8,128)S(1)}, f32[104,128]{1,0:T(8,128)}, u32[]{:S(2)}) copy-start(f32[104,128]{1,0:T(8,128)} %get-tuple-element.79) | copy-start | bytes 159748
  293.4 7.6 %copy-start.5 = (f32[96,128]{1,0:T(8,128)S(1)}, f32[96,128]{1,0:T(8,128)}, u32[]{:S(2)}) copy-start(f32[96,128]{1,0:T(8,128)} %get-tuple-element.81) | copy-start | bytes 147460
  293.4 8.3 %copy-start.2 = (f32[8,1536]{1,0:T(8,128)S(1)}, f32[8,1536]{1,0:T(8,128)}, u32[]{:S(2)}) copy-start(f32[8,1536]{1,0:T(8,128)} %get-tuple-element.82) | copy-start | bytes 147460
  293.4 12.1 %copy-start.1 = (f32[2,96,1536]{2,1,0:T(8,128)S(1)}, f32[2,96,1536]{2,1,0:T(8,128)}, u32[]{:S(2)}) copy-start(f32[2,96,1536]{2,1,0:T(8,128)} %get-tuple-element.77.gate_grads) | copy-start | bytes 3538948

commit v11 on v10

--- a/solution.py
+++ b/solution.py
@@ -956,7 +956,7 @@
         pltpu.make_async_copy(src, dst, loads.at[n])
         for n, (src, dst) in enumerate(zip(sources, (nt_v, dinner_v, dsd_v, dgate_v, wg_v, wa_v)))
     ]
-    for copy in pending:
+    for copy in pending[:3]:
         copy.start()
     far = pltpu.get_barrier_semaphore()
     partners = [here.me + bit - 2 * bit * ((here.me // bit) % 2) for bit in (2, 4, 8, 1)]
@@ -1011,12 +1011,15 @@
         work.copy_a(z, 1 - here.y).start()
         work.copy_a(z, here.y).start()
 
-        @pl.when(n == 0)
+        @pl.when(n == 1)
         def _():
             for copy in pending[3:]:
                 copy.wait()
 
-        far_chunk(n, carry)
+        @pl.when(n > 0)
+        def _():
+            far_chunk(n - 1, carry)
+
         work.cores(z)
         return carry
 
@@ -1029,13 +1032,15 @@
     swap(0).start()
     for copy in pending[:3]:
         copy.wait()
+    for copy in pending[3:]:
+        copy.start()
     swapped(0)
     lax.fori_loop(0, 4, grads, 0)
     swapped(1)
     work.stay(order[0])
     work.sides(order[0])
     pl.when(~middle)(lambda: work.pass_on(order[0]))
-    lax.fori_loop(4, chunks, far_chunk, 0)
+    lax.fori_loop(3, chunks, far_chunk, 0)
     swapped(2)
     for n in range(1, 4):
         work.stay(order[n])

time: 312 us -> 311 us (level)
  no operation moved by 1% of the time
where the time goes in v11:
time: 311 us
  Pallas kernels  278 us (89%)
  local copies, waits for them, and re-layouts  12.4 us (4%)
  other arithmetic  10.5 us (3%)
  matrix products  9.43 us (3%)
    pallas_call x1, Pallas kernels, on_device(): pl.pallas_call(functools.partial(mixer_forward, own_links), name='mixer_f...  80.2 us
    pallas_call x1, Pallas kernels, on_device(): pl.pallas_call(functools.partial(mixer_backward, own_links), name='mixer_...  72.2 us
    pallas_call x1, Pallas kernels, reduce_tail(): pl.pallas_call(tail_kernel, name='tail', in_specs=[hbm] * 6 + [vmem] * 9,...  58.7 us
    pallas_call x1, Pallas kernels, gather_rows(): pl.pallas_call(gather_kernel, name='gather_rows', in_specs=[vmem] * 5, ou...  42.4 us
    pallas_call x1, Pallas kernels, on_device(): pl.pallas_call(functools.partial(gate_backward, float(unit_total)), name=...  24.1 us
    dot_general x1, matrix products, mm(): lax.dot_general(a, b, (((ca,), (cb,)), ((), ())), preferred_element_type=...  9.43 us
    add x1, other arithmetic, on_device(): cotangent.astype(f32)  6.99 us

profile of v11, /device:TPU:0, one launch (start us, length us, event | category | flops | bytes accessed | tf_op | source)
XLA Modules:
  0.0 310.7 jit_solution(6961864521472382935)
XLA Ops:
  0.6 1.3 broadcast_in_dim.4.gain.norm_gain
  2.0 1.4 copy.29.w_step
  3.4 42.4 %gather_rows.1 = (bf16[1024,1536]{1,0:T(8,128)(2,1)}, bf16[1536,1920]{1,0:T(8,128)(2,1)}) custom-call(bf16[512,1536]{1,0:T(8,128)(2,1)} %tokens_in.1, f32[8,1536]{1,0:T(8,128)} %broadcast_in_dim.4.gain.norm_gain, bf16[2,96,1536]{2,1,0:T(8,128)(2,1)} %w_gate_inner.3, bf16[96,256]{1,0:T(8,128)(2,1)} %w_state_io.3, bf16[96,24]{1,0:T(8,128)(2,1)} %copy.29.w_step), custom_call_target="tpu_custom_call" | custom-call | tf_op jit(solution)/shard_map/gather_rows/pallas_call | solution.py:795
  45.8 1.3 broadcast_in_dim.5.refs_3_.gain
  47.1 80.2 %mixer_forward.1 = (f32[1024,1536]{1,0:T(8,128)}, f32[1024,1536]{1,0:T(8,128)}, f32[4,1536,128]{2,1,0:T(8,128)}, f32[1024,256]{1,0:T(8,128)}, bf16[1024,256]{1,0...) custom-call(bf16[1024,1536]{1,0:T(8,128)(2,1)} %get-tuple-element.48, ...), custom_call_target="tpu_custom_call" | custom-call | flops 7650410496 | bytes 30000000 | tf_op jit(solution)/shard_map/mixer_forward/pallas_call | solution.py:1207
  127.3 24.1 %gate_backward.1 = (bf16[1024,1536]{1,0:T(8,128)(2,1)}, bf16[1024,1536]{1,0:T(8,128)(2,1)}, bf16[1024,1536]{1,0:T(8,128)(2,1)}, f32[8,1536]{1,0:T(8,128)}, bf16[...) custom-call(f32[8,1024]{1,0:T(8,128)} %get-tuple-element.50.stats, f32[1024,1536]{1,0:T(8,128)} %get-tuple-element.51.gate, ...), custom_call_target="tpu_custom_call" | custom-call | flops 9663676416 | bytes 45000000 | tf_op jit(solution)/shard_map/gate_backward/pallas_call | solution.py:1265
  151.4 9.4 %fusion.2.refs_0_ = bf16[1024,1536]{1,0:T(8,128)(2,1)} fusion(bf16[1024,1536]{1,0:T(8,128)(2,1)} %get-tuple-element.55, bf16[1536,3072]{1,0:T(8,128)(2,1)} %get-tuple-element.56.wb), kind=kOutput, calls=%fused_computation.5 | convolution fusion | flops 4833411072 | bytes 11010048 | tf_op jit(solution)/shard_map/dot_general | solution.py:24
  160.8 72.2 %mixer_backward.1 = (bf16[1024,1536]{1,0:T(8,128)(2,1)}, f32[8,1536]{1,0:T(8,128)}, bf16[1024,384]{1,0:T(8,128)(2,1)}, f32[8,256]{1,0:T(8,128)}, f32[8,128]{1,0:...) custom-call(f32[1024,1536]{1,0:T(8,128)} %get-tuple-element.57.inner, ...), custom_call_target="tpu_custom_call" | custom-call | flops 40000000000 | bytes 30000000 | tf_op jit(solution)/shard_map/mixer_backward/pallas_call | solution.py:1289
  233.1 0.0 copy-start
  233.1 0.0 copy-start.3
  233.1 58.7 %tail.1 = (f32[512,1536]{1,0:T(8,128)}, f32[2,96,1536]{2,1,0:T(8,128)}, f32[96,128]{1,0:T(8,128)}, f32[104,128]{1,0:T(8,128)}, f32[8,1536]{1,0:T(8,128)}) custom-call(bf16[1536,1024]{1,0:T(8,128)(2,1)} %get-tuple-element.69.normed_t, bf16[1024,1536]{1,0:T(8,128)(2,1)} %get-tuple-element.70.dinner, bf16[1024,384]{1,0:T(8,128)(2,1)} %get-tuple-element.71.dsd, ...), custom_call_target="tpu_custom_call" | custom-call | tf_op jit(solution)/shard_map/tail/pallas_call | solution.py:1113
  291.8 0.0 copy-done
  291.8 0.4 fusion.13
  292.2 0.0 copy-done.3
  292.2 2.5 fusion.7
  294.7 0.0 copy-start.4
  294.7 0.0 copy-start.5
  294.7 0.0 copy-start.2
  294.8 0.0 copy-start.1
  294.8 7.0 %fusion.10 = (f32[512,1536]{1,0:T(8,128)}, bf16[512,1536]{1,0:T(8,128)(2,1)}) fusion(bf16[512,1536]{1,0:T(8,128)(2,1)S(1)} %copy-done, bf16[512,1536]{1,0:T(8,128)(2,1)} %refs_0_.1, f32[512,1536]{1,0:T(8,128)} %get-tuple-element.78, f32[512]{0:T(512)S(1)} %broadcast_multiply_fusion, f32[1536]{0:T(1024)S(1)} %copy-done.3, f32[512]{0:T(512)S(1)} %add_rsqrt_fusion, ...), kind=kLoop, calls=%fused_computation.11 | loop fusion | flops 10223616 | bytes 14166020 | tf_op jit(solution)/shard_map/add | solution.py:1342
  301.8 0.0 copy-done.4
  301.8 0.6 slice.50
  302.4 0.0 copy-done.5
  302.4 0.1 copy.31
  302.4 0.6 slice.62
  303.1 0.0 copy-done.2
  303.1 0.6 slice_reduce_fusion
  303.7 0.1 reshape_squeeze.3
  303.8 0.6 reduce_sum.29
  304.4 0.1 reshape.64
  304.5 0.6 reshape.65
  305.1 0.1 reshape.66
  305.2 0.6 reshape.67
  305.8 0.6 slice.54
  306.4 0.5 slice_bitcast_fusion.1
  306.9 0.0 copy-done.1
  306.9 0.9 slice_bitcast_fusion
  307.7 2.4 copy.34
  310.1 0.6 copy.35
  (3 shorter events, 0.0 us)
Async XLA Ops:
  233.1 58.7 %copy-start = (bf16[512,1536]{1,0:T(8,128)(2,1)S(1)}, bf16[512,1536]{1,0:T(8,128)(2,1)}, u32[]{:S(2)}) copy-start(bf16[512,1536]{1,0:T(8,128)(2,1)} %tokens_in.1) | copy-start | bytes 4718596
  233.1 59.1 %copy-start.3 = (f32[1536]{0:T(1024)S(1)}, f32[1536]{0:T(1024)}, u32[]{:S(2)}) copy-start(f32[1536]{0:T(1024)} %param.14) | copy-start | bytes 18436
  294.7 7.0 %copy-start.4 = (f32[104,128]{1,0:T(8,128)S(1)}, f32[104,128]{1,0:T(8,128)}, u32[]{:S(2)}) copy-start(f32[104,128]{1,0:T(8,128)} %get-tuple-element.79) | copy-start | bytes 159748
  294.7 7.6 %copy-start.5 = (f32[96,128]{1,0:T(8,128)S(1)}, f32[96,128]{1,0:T(8,128)}, u32[]{:S(2)}) copy-start(f32[96,128]{1,0:T(8,128)} %get-tuple-element.81) | copy-start | bytes 147460
  294.7 8.3 %copy-start.2 = (f32[8,1536]{1,0:T(8,128)S(1)}, f32[8,1536]{1,0:T(8,128)}, u32[]{:S(2)}) copy-start(f32[8,1536]{1,0:T(8,128)} %get-tuple-element.82) | copy-start | bytes 147460
  294.8 12.1 %copy-start.1 = (f32[2,96,1536]{2,1,0:T(8,128)S(1)}, f32[2,96,1536]{2,1,0:T(8,128)}, u32[]{:S(2)}) copy-start(f32[2,96,1536]{2,1,0:T(8,128)} %get-tuple-element.77.gate_grads) | copy-start | bytes 3538948

commit v12 on v10

--- a/solution.py
+++ b/solution.py
@@ -213,11 +213,7 @@
         gates.start(0)
 
 
-    @pl.when((i >= blocks) & (i < 2 * blocks))
-    def _():
-        gates.gate()
-        work.between(i - blocks)
-
+    pl.when((i >= blocks) & (i < 2 * blocks))(gates.gate)
 
     @pl.when(i == 2 * blocks)
     def _():
@@ -311,7 +307,7 @@
         self.local.start()
 
     def step(self, at):
-        for when, chunk, hops in ((6, 0, 1), (10, 1, 1), (14, 0, 2), (18, 1, 2), (22, 0, 3)):
+        for when, chunk, hops in ((5, 0, 1), (9, 1, 1), (13, 0, 2), (16, 1, 2), (20, 0, 3), (23, 1, 3)):
 
             def go(move=self.moves[chunk], hops=hops):
                 move.hop(hops)
@@ -321,13 +317,9 @@
 
     def first(self):
         self.moves[0].sides(3)
-        self.moves[1].hop(3)
         self.moves[0].finish()
         self.local.wait()
         self.across.wait()
-
-    def between(self, at):
-        pl.when(at == 1)(lambda: self.moves[1].sides(2))
 
     def finish(self):
         move = self.moves[1]

time: 312 us -> 311 us (level)
  no operation moved by 1% of the time
where the time goes in v12:
time: 311 us; the launch traced here: 308 us
  Pallas kernels  275 us (88%)
  local copies, waits for them, and re-layouts  12.4 us (4%)
  other arithmetic  10.5 us (3%)
  matrix products  9.43 us (3%)
    pallas_call x1, Pallas kernels, on_device(): pl.pallas_call(functools.partial(mixer_forward, own_links), name='mixer_f...  80.2 us
    pallas_call x1, Pallas kernels, on_device(): pl.pallas_call(functools.partial(mixer_backward, own_links), name='mixer_...  72.2 us
    pallas_call x1, Pallas kernels, reduce_tail(): pl.pallas_call(tail_kernel, name='tail', in_specs=[hbm] * 6 + [vmem] * 9,...  55.9 us
    pallas_call x1, Pallas kernels, gather_rows(): pl.pallas_call(gather_kernel, name='gather_rows', in_specs=[vmem] * 5, ou...  42.4 us
    pallas_call x1, Pallas kernels, on_device(): pl.pallas_call(functools.partial(gate_backward, float(unit_total)), name=...  24.1 us
    dot_general x1, matrix products, mm(): lax.dot_general(a, b, (((ca,), (cb,)), ((), ())), preferred_element_type=...  9.43 us
    add x1, other arithmetic, on_device(): cotangent.astype(f32)  6.99 us

profile of v12, /device:TPU:0, one launch (start us, length us, event | category | flops | bytes accessed | tf_op | source)
XLA Modules:
  0.0 307.9 jit_solution(3082801683914236475)
XLA Ops:
  0.6 1.3 broadcast_in_dim.4.gain.norm_gain
  2.0 1.4 copy.29.w_step
  3.4 42.4 %gather_rows.1 = (bf16[1024,1536]{1,0:T(8,128)(2,1)}, bf16[1536,1920]{1,0:T(8,128)(2,1)}) custom-call(bf16[512,1536]{1,0:T(8,128)(2,1)} %tokens_in.1, f32[8,1536]{1,0:T(8,128)} %broadcast_in_dim.4.gain.norm_gain, bf16[2,96,1536]{2,1,0:T(8,128)(2,1)} %w_gate_inner.3, bf16[96,256]{1,0:T(8,128)(2,1)} %w_state_io.3, bf16[96,24]{1,0:T(8,128)(2,1)} %copy.29.w_step), custom_call_target="tpu_custom_call" | custom-call | tf_op jit(solution)/shard_map/gather_rows/pallas_call | solution.py:787
  45.8 1.3 broadcast_in_dim.5.refs_3_.gain
  47.1 80.2 %mixer_forward.1 = (f32[1024,1536]{1,0:T(8,128)}, f32[1024,1536]{1,0:T(8,128)}, f32[4,1536,128]{2,1,0:T(8,128)}, f32[1024,256]{1,0:T(8,128)}, bf16[1024,256]{1,0...) custom-call(bf16[1024,1536]{1,0:T(8,128)(2,1)} %get-tuple-element.48, ...), custom_call_target="tpu_custom_call" | custom-call | flops 7650410496 | bytes 30000000 | tf_op jit(solution)/shard_map/mixer_forward/pallas_call | solution.py:1194
  127.3 24.1 %gate_backward.1 = (bf16[1024,1536]{1,0:T(8,128)(2,1)}, bf16[1024,1536]{1,0:T(8,128)(2,1)}, bf16[1024,1536]{1,0:T(8,128)(2,1)}, f32[8,1536]{1,0:T(8,128)}, bf16[...) custom-call(f32[8,1024]{1,0:T(8,128)} %get-tuple-element.50.stats, f32[1024,1536]{1,0:T(8,128)} %get-tuple-element.51.gate, ...), custom_call_target="tpu_custom_call" | custom-call | flops 9663676416 | bytes 45000000 | tf_op jit(solution)/shard_map/gate_backward/pallas_call | solution.py:1252
  151.4 9.4 %fusion.2.refs_0_ = bf16[1024,1536]{1,0:T(8,128)(2,1)} fusion(bf16[1024,1536]{1,0:T(8,128)(2,1)} %get-tuple-element.55, bf16[1536,3072]{1,0:T(8,128)(2,1)} %get-tuple-element.56.wb), kind=kOutput, calls=%fused_computation.5 | convolution fusion | flops 4833411072 | bytes 11010048 | tf_op jit(solution)/shard_map/dot_general | solution.py:24
  160.8 72.2 %mixer_backward.1 = (bf16[1024,1536]{1,0:T(8,128)(2,1)}, f32[8,1536]{1,0:T(8,128)}, bf16[1024,384]{1,0:T(8,128)(2,1)}, f32[8,256]{1,0:T(8,128)}, f32[8,128]{1,0:...) custom-call(f32[1024,1536]{1,0:T(8,128)} %get-tuple-element.57.inner, ...), custom_call_target="tpu_custom_call" | custom-call | flops 40000000000 | bytes 30000000 | tf_op jit(solution)/shard_map/mixer_backward/pallas_call | solution.py:1276
  233.1 0.0 copy-start
  233.1 0.0 copy-start.3
  233.1 55.9 %tail.1 = (f32[512,1536]{1,0:T(8,128)}, f32[2,96,1536]{2,1,0:T(8,128)}, f32[96,128]{1,0:T(8,128)}, f32[104,128]{1,0:T(8,128)}, f32[8,1536]{1,0:T(8,128)}) custom-call(bf16[1536,1024]{1,0:T(8,128)(2,1)} %get-tuple-element.69.normed_t, bf16[1024,1536]{1,0:T(8,128)(2,1)} %get-tuple-element.70.dinner, bf16[1024,384]{1,0:T(8,128)(2,1)} %get-tuple-element.71.dsd, ...), custom_call_target="tpu_custom_call" | custom-call | tf_op jit(solution)/shard_map/tail/pallas_call | solution.py:1100
  289.0 0.0 copy-done
  289.0 0.4 fusion.13
  289.4 0.0 copy-done.3
  289.4 2.5 fusion.7
  292.0 0.0 copy-start.4
  292.0 0.0 copy-start.5
  292.0 0.0 copy-start.2
  292.0 0.0 copy-start.1
  292.0 7.0 %fusion.10 = (f32[512,1536]{1,0:T(8,128)}, bf16[512,1536]{1,0:T(8,128)(2,1)}) fusion(bf16[512,1536]{1,0:T(8,128)(2,1)S(1)} %copy-done, bf16[512,1536]{1,0:T(8,128)(2,1)} %refs_0_.1, f32[512,1536]{1,0:T(8,128)} %get-tuple-element.78, f32[512]{0:T(512)S(1)} %broadcast_multiply_fusion, f32[1536]{0:T(1024)S(1)} %copy-done.3, f32[512]{0:T(512)S(1)} %add_rsqrt_fusion, ...), kind=kLoop, calls=%fused_computation.11 | loop fusion | flops 10223616 | bytes 14166020 | tf_op jit(solution)/shard_map/add | solution.py:1329
  299.0 0.0 copy-done.4
  299.0 0.6 slice.50
  299.6 0.0 copy-done.5
  299.6 0.1 copy.31
  299.7 0.6 slice.62
  300.3 0.0 copy-done.2
  300.3 0.6 slice_reduce_fusion
  300.9 0.1 reshape_squeeze.3
  301.0 0.6 reduce_sum.29
  301.7 0.1 reshape.64
  301.7 0.6 reshape.65
  302.3 0.1 reshape.66
  302.4 0.6 reshape.67
  303.0 0.6 slice.54
  303.6 0.5 slice_bitcast_fusion.1
  304.1 0.0 copy-done.1
  304.1 0.9 slice_bitcast_fusion
  305.0 2.4 copy.34
  307.3 0.6 copy.35
  (3 shorter events, 0.0 us)
Async XLA Ops:
  233.1 56.0 %copy-start = (bf16[512,1536]{1,0:T(8,128)(2,1)S(1)}, bf16[512,1536]{1,0:T(8,128)(2,1)}, u32[]{:S(2)}) copy-start(bf16[512,1536]{1,0:T(8,128)(2,1)} %tokens_in.1) | copy-start | bytes 4718596
  233.1 56.3 %copy-start.3 = (f32[1536]{0:T(1024)S(1)}, f32[1536]{0:T(1024)}, u32[]{:S(2)}) copy-start(f32[1536]{0:T(1024)} %param.14) | copy-start | bytes 18436
  292.0 7.0 %copy-start.4 = (f32[104,128]{1,0:T(8,128)S(1)}, f32[104,128]{1,0:T(8,128)}, u32[]{:S(2)}) copy-start(f32[104,128]{1,0:T(8,128)} %get-tuple-element.79) | copy-start | bytes 159748
  292.0 7.6 %copy-start.5 = (f32[96,128]{1,0:T(8,128)S(1)}, f32[96,128]{1,0:T(8,128)}, u32[]{:S(2)}) copy-start(f32[96,128]{1,0:T(8,128)} %get-tuple-element.81) | copy-start | bytes 147460
  292.0 8.3 %copy-start.2 = (f32[8,1536]{1,0:T(8,128)S(1)}, f32[8,1536]{1,0:T(8,128)}, u32[]{:S(2)}) copy-start(f32[8,1536]{1,0:T(8,128)} %get-tuple-element.82) | copy-start | bytes 147460
  292.0 12.1 %copy-start.1 = (f32[2,96,1536]{2,1,0:T(8,128)S(1)}, f32[2,96,1536]{2,1,0:T(8,128)}, u32[]{:S(2)}) copy-start(f32[2,96,1536]{2,1,0:T(8,128)} %get-tuple-element.77.gate_grads) | copy-start | bytes 3538948
